TPU v7x, 128 devices: a whole 4x4x4 slice. The times are simulated.
128 devices in a mesh: pair: 16 (over y_hi, z, core), rows: 8 (over y_lo, x).
Axes of the slice: x: 4, y: 4 (y_hi: 2, y_lo: 2; y = y_hi * 2 + y_lo), z: 4, core: 2. Of those that a mesh axis runs over, the one named last changes fastest.
Arguments:
- matrix: float32 [4096, 16384], P(('rows', 'pair')), may hold values from -6 to 6
- plan: int32 [32], replicated, may hold values from 0 to 31, each once
Outputs:
- rotated: float32 [4096, 16384], P('rows', 'pair')
Inputs may be any that keep to these rules, and one draw needn't show every extreme that they name: `plan`: each block number appears once.
All inputs are finite; a program needn't handle non-finite values.
Results may differ from a plain program's by a relative error of at most 0.0003.
Values sent between devices are 32-bit elements; how exact they have to be, the bound alone decides.
A program may use at most 64 MiB of HBM per device.

v0:
```python
import functools

import jax
import jax.numpy as jnp
from jax import lax
from jax.experimental import pallas as pl
from jax.experimental.pallas import tpu as pltpu
from jax.sharding import PartitionSpec as P

MESH = pl.DeviceIdType.MESH

BLK = 512
STEPS = 2


epsilon = 1e-06
high = lax.Precision.HIGHEST
fast = lax.Precision.HIGH


def shifted(v, axis, count, by):
    return lax.ppermute(v, axis, [(i, (i + by) % count) for i in range(count)])


def scatter_sum(v, axis, count):
    me = lax.axis_index(axis)
    chunks = v.reshape(count, v.shape[0] // count, *v.shape[1:])
    total = lax.dynamic_index_in_dim(chunks, me, keepdims=False)
    for by in range(1, count):
        piece = lax.dynamic_index_in_dim(chunks, (me + by) % count, keepdims=False)
        total = total + shifted(piece, axis, count, by)
    return total


def gather_all(v, axis, count):
    me = lax.axis_index(axis)
    out = jnp.zeros((count,) + v.shape, v.dtype)
    out = lax.dynamic_update_index_in_dim(out, v, me, 0)
    for by in range(1, count):
        out = lax.dynamic_update_index_in_dim(out, shifted(v, axis, count, by), (me - by) % count, 0)
    return out.reshape(count * v.shape[0], *v.shape[1:])


def remote(src, dst, sends, recvs, slot, device):
    copy = pltpu.make_async_remote_copy(
        src_ref=src,
        dst_ref=dst,
        send_sem=sends.at[slot],
        recv_sem=recvs.at[slot],
        device_id=device,
        device_id_type=MESH,
    )
    copy.start()
    return copy


def rows_sum_kernel(
    outer, inner, payload, out, a_in, a_acc, a_halves, a_own, a_all, b_in, b_acc, b_parts, b_own, b_row, b_all, sends, recvs
):
    pair = lax.axis_index("pair")
    me_y = lax.axis_index("ylo")
    me_x = lax.axis_index("x")
    rows, width = payload.shape
    half_w = width // 2
    a_chunk = rows // inner
    a_half = a_chunk // outer
    b_half = rows // outer
    b_chunk = b_half // inner
    partner = (me_y + 1) % outer
    cols_a = pl.ds(0, half_w)
    cols_b = pl.ds(half_w, half_w)

    def x_peer(by):
        return (pair, me_y, (me_x + by) % inner)

    y_peer = (pair, partner, me_x)

    barrier = pltpu.get_barrier_semaphore()
    for by in range(1, inner):
        pl.semaphore_signal(barrier, inc=1, device_id=x_peer(by), device_id_type=MESH)
    pl.semaphore_signal(barrier, inc=1, device_id=y_peer, device_id_type=MESH)
    pl.semaphore_wait(barrier, inner)

    copies = []
    for by in range(1, inner):
        target = (me_x + by) % inner
        rows_k = pl.ds(pl.multiple_of(target * a_chunk, 8), a_chunk)
        copies.append(remote(payload.at[rows_k, cols_a], a_in.at[by - 1], sends, recvs, by - 1, x_peer(by)))
    rows_k = pl.ds(pl.multiple_of(partner * b_half, 8), b_half)
    copies.append(remote(payload.at[rows_k, cols_b], b_in, sends, recvs, 8, y_peer))
    for copy in copies:
        copy.wait()
    total = payload[pl.ds(pl.multiple_of(me_x * a_chunk, 8), a_chunk), cols_a]
    for by in range(1, inner):
        total = total + a_in[by - 1]
    a_acc[...] = total
    b_acc[...] = payload[pl.ds(pl.multiple_of(me_y * b_half, 8), b_half), cols_b] + b_in[...]

    copies = [
        remote(a_acc.at[pl.ds(pl.multiple_of(partner * a_half, 8), a_half)], a_halves.at[0], sends, recvs, 3, y_peer)
    ]
    for by in range(1, inner):
        target = (me_x + by) % inner
        rows_k = pl.ds(pl.multiple_of(target * b_chunk, 8), b_chunk)
        copies.append(remote(b_acc.at[rows_k], b_parts.at[by - 1], sends, recvs, 8 + by, x_peer(by)))
    for copy in copies:
        copy.wait()
    a_own[...] = a_acc[pl.ds(pl.multiple_of(me_y * a_half, 8), a_half), :] + a_halves[0]
    total = b_acc[pl.ds(pl.multiple_of(me_x * b_chunk, 8), b_chunk), :]
    for by in range(1, inner):
        total = total + b_parts[by - 1]
    b_own[...] = total

    copies = [remote(a_own, a_halves.at[1], sends, recvs, 4, y_peer)]
    for by in range(1, inner):
        copies.append(remote(b_own, b_row.at[me_x], sends, recvs, 11 + by, x_peer(by)))
    for copy in copies:
        copy.wait()
    a_all[me_x, pl.ds(pl.multiple_of(me_y * a_half, 8), a_half), :] = a_own[...]
    a_all[me_x, pl.ds(pl.multiple_of(partner * a_half, 8), a_half), :] = a_halves[1]
    b_row[me_x] = b_own[...]
    b_all[me_y] = b_row[...]

    copies = []
    for by in range(1, inner):
        copies.append(remote(a_all.at[me_x], a_all.at[me_x], sends, recvs, 4 + by, x_peer(by)))
    copies.append(remote(b_row, b_all.at[me_y], sends, recvs, 15, y_peer))
    for copy in copies:
        copy.wait()
    for k in range(inner):
        out[pl.ds(k * a_chunk, a_chunk), cols_a] = a_all[k]
    for j in range(outer):
        for k in range(inner):
            out[pl.ds(j * b_half + k * b_chunk, b_chunk), cols_b] = b_all[j, k]


def rows_sum(v, outer, inner):
    rows, width = v.shape
    half_w = width // 2
    a_chunk = rows // inner
    a_half = a_chunk // outer
    b_half = rows // outer
    b_chunk = b_half // inner
    return pl.pallas_call(
        functools.partial(rows_sum_kernel, outer, inner),
        out_shape=jax.ShapeDtypeStruct(v.shape, v.dtype),
        in_specs=[pl.BlockSpec(memory_space=pltpu.VMEM)],
        out_specs=pl.BlockSpec(memory_space=pltpu.VMEM),
        scratch_shapes=[
            pltpu.VMEM((inner - 1, a_chunk, half_w), jnp.float32),
            pltpu.VMEM((a_chunk, half_w), jnp.float32),
            pltpu.VMEM((2, a_half, half_w), jnp.float32),
            pltpu.VMEM((a_half, half_w), jnp.float32),
            pltpu.VMEM((inner, a_chunk, half_w), jnp.float32),
            pltpu.VMEM((b_half, half_w), jnp.float32),
            pltpu.VMEM((b_half, half_w), jnp.float32),
            pltpu.VMEM((inner - 1, b_chunk, half_w), jnp.float32),
            pltpu.VMEM((b_chunk, half_w), jnp.float32),
            pltpu.VMEM((inner, b_chunk, half_w), jnp.float32),
            pltpu.VMEM((outer, inner, b_chunk, half_w), jnp.float32),
            pltpu.SemaphoreType.DMA((16,)),
            pltpu.SemaphoreType.DMA((16,)),
        ],
        compiler_params=pltpu.CompilerParams(collective_id=0, has_side_effects=True),
    )(v)


def summed_gram(upper, lower, outer, inner):
    width = upper.shape[1]
    row = lax.broadcasted_iota(jnp.int32, (width, width), 0)
    col = lax.broadcasted_iota(jnp.int32, (width, width), 1)
    upper_gram = inner_gram(upper, upper)
    lower_gram = inner_gram(lower, lower)
    cross_gram = inner_gram(upper, lower)
    packed = jnp.where(col >= row, upper_gram, lower_gram)
    tail = jnp.zeros((64, width), jnp.float32).at[0].set(masked_diagonal(lower_gram))
    total = rows_sum(jnp.concatenate([packed, cross_gram, tail]), outer, inner)
    packed, cross_gram, lower_diagonal = total[:width], total[width : 2 * width], total[2 * width]
    strict_upper = jnp.where(col > row, packed, 0.0)
    upper_gram = jnp.where(col >= row, packed, 0.0) + strict_upper.T
    strict_lower = jnp.where(col < row, packed, 0.0)
    lower_gram = strict_lower + strict_lower.T + jnp.where(col == row, lower_diagonal[None, :], 0.0)
    return upper_gram, lower_gram, cross_gram, masked_diagonal(packed), lower_diagonal


def from_behind(x, axis, by):
    count = lax.axis_size(axis)
    pairs = [(i, i + by) for i in range(count) if 0 <= i + by < count]
    return lax.ppermute(x, axis, pairs)


def inner_gram(left, right):
    return lax.dot_general(
        left, right, (((0,), (0,)), ((), ())), precision=fast, preferred_element_type=jnp.float32
    )


def masked_diagonal(block):
    width = block.shape[0]
    eye = lax.broadcasted_iota(jnp.int32, (width, width), 0) == lax.broadcasted_iota(jnp.int32, (width, width), 1)
    return jnp.sum(jnp.where(eye, block, 0.0), axis=0)


def normalize(gram, diagonal):
    width = gram.shape[0]
    diagonal = diagonal + epsilon
    inverse = 1.0 / jnp.sqrt(diagonal)
    normed = gram * inverse[:, None] * inverse[None, :]
    spread = 1.5 * jnp.sqrt(jnp.sum(normed * normed)) / jnp.sqrt(jnp.float32(width))
    scaled_gram = normed / spread
    identity = jnp.eye(width, dtype=jnp.float32)
    first_iter = 0.5 * (3.0 * identity - scaled_gram)
    factor = 0.5 * jnp.sqrt(diagonal) / jnp.sqrt(spread)
    return (scaled_gram, first_iter, inverse, factor, identity)


def per_device(matrix, plan, outer, inner):
    local_rows = matrix.shape[0]
    blocks = matrix.reshape(local_rows, -1, BLK)
    slots = jnp.take(blocks, plan, axis=1).reshape(local_rows, -1)
    current = lax.all_to_all(slots, "pair", split_axis=1, concat_axis=0, tiled=True)
    pair_index = lax.axis_index("pair")
    pair_count = lax.axis_size("pair")
    for turn_index in range(STEPS):
        upper = current[:, :BLK]
        lower = current[:, BLK:]
        upper_gram, lower_gram, cross_gram, upper_diagonal, lower_diagonal = summed_gram(
            upper, lower, outer, inner
        )
        gram = jnp.concatenate(
            [
                jnp.concatenate([upper_gram, cross_gram], axis=1),
                jnp.concatenate([cross_gram.T, lower_gram], axis=1),
            ],
            axis=0,
        )
        diagonal = jnp.concatenate([upper_diagonal, lower_diagonal])
        scaled_gram, first_iter, inverse, factor, identity = normalize(gram, diagonal)
        weighted = current * inverse[None, :]
        applied = jnp.dot(weighted, first_iter, precision=fast, preferred_element_type=jnp.float32)
        chain = jnp.dot(applied, scaled_gram, precision=fast, preferred_element_type=jnp.float32)
        chain = jnp.dot(chain, first_iter, precision=fast, preferred_element_type=jnp.float32)
        chain = jnp.dot(chain, first_iter, precision=fast, preferred_element_type=jnp.float32)
        current = (3.0 * applied - chain) * factor[None, :]
        upper = current[:, :BLK]
        lower = current[:, BLK:]
        outgoing = jnp.where(pair_index == 0, lower, upper)
        arrived_up = from_behind(outgoing, "pair", 1)
        arrived_down = from_behind(lower, "pair", -1)
        new_upper = jnp.where(pair_index == 0, upper, arrived_up)
        new_lower = jnp.where(pair_index == pair_count - 1, upper, arrived_down)
        current = jnp.concatenate([new_upper, new_lower], axis=1)
    return current


def solution(mesh):
    pairs, rows = mesh.shape["pair"], mesh.shape["rows"]
    inner = 4
    outer = rows // inner
    split = jax.sharding.Mesh(mesh.devices.reshape(pairs, outer, inner), ("pair", "ylo", "x"))
    placed = (P(("ylo", "x", "pair"), None), P())
    return jax.shard_map(
        functools.partial(per_device, outer=outer, inner=inner),
        mesh=split,
        in_specs=placed,
        out_specs=P(("ylo", "x"), "pair"),
        check_vma=False,
    )
```

profile of v0, /device:TPU:97, one launch (start us, length us, event | category | flops | bytes accessed | tf_op | source)
XLA Modules:
  0.0 278.3 jit_solution(17905611117658843386)
XLA Ops:
  1.3 1.8 copy.74
  3.2 2.0 gather_fusion
  5.2 4.2 %copy.46 = f32[32,32,512]{2,1,0:T(8,128)} copy(f32[32,32,512]{2,0,1:T(8,128)} %bitcast.50) | data formatting | bytes 4194304 | tf_op jit(solution)/shard_map/jit(_take)/gather | solution.py:220
  9.3 1.9 gather.7
  11.7 2.5 copy.47
  14.3 7.6 %all-to-all-start = ((f32[32,16,1024]{2,0,1:T(8,128)}), f32[32,16,1024]{2,0,1:T(8,128)S(1)}, u32[]{:S(2)}, u32[]{:S(2)}) async-start(f32[32,16,1024]{2,0,1:T(8,128)} %copy.47), calls=%async_computation | async-start | bytes 4194304 | tf_op jit(solution)/shard_map/all_to_all | solution.py:221
  21.9 29.3 %all-to-all-done = f32[32,16,1024]{2,0,1:T(8,128)S(1)} async-done(((f32[32,16,1024]{2,0,1:T(8,128)}), f32[32,16,1024]{2,0,1:T(8,128)S(1)}, u32[]{:S(2)}, u32[]{:S(2)}) %all-to-all-start) | async-done | bytes 2097184 | tf_op jit(solution)/shard_map/all_to_all | solution.py:221
  51.2 1.0 select_reduce_fusion.3
  54.4 1.5 select_maximum_fusion.1.payload
  55.9 50.6 %shard_map.28 = f32[1088,512]{1,0:T(8,128)} custom-call(f32[1088,512]{1,0:T(8,128)} %select_maximum_fusion.1.payload), custom_call_target="tpu_custom_call" | custom-call | tf_op jit(solution)/shard_map/pallas_call | solution.py:144
  106.5 1.3 slice.66
  108.5 1.3 copy.48
  109.9 3.9 %bitcast_add_fusion.3 = (f32[512,512]{1,0:T(8,128)}, f32[512]{0:T(512)S(1)}, f32[512,512]{1,0:T(8,128)S(1)}, f32[512,512]{0,1:T(8,128)}, f32[512,512]{1,0:T(8,128)}) fusion(f32[512,512]{0,1:T(8,128)} %copy.48, f32[1088,512]{1,0:T(8,128)} %shard_map.28), kind=kLoop, calls=%fused_computation.56 | loop fusion | flops 2620928 | bytes 7342080 | tf_op jit(solution)/shard_map/add | solution.py:180
  113.7 1.3 copy.50
  115.0 2.7 fusion.42
  117.7 1.6 copy.51
  119.3 3.7 %multiply_reduce_fusion.1 = f32[]{:T(128)} fusion(f32[1024]{0:T(1024)S(1)} %fusion.52, f32[512,512]{1,0:T(8,128)} %fusion.42, f32[512,512]{1,0:T(8,128)S(1)} %copy.51, f32[512,512]{1,0:T(8,128)} %get-tuple-element.36, f32[512,512]{1,0:T(8,128)} %get-tuple-element.32), kind=kLoop, calls=%fused_computation.10 | loop fusion | flops 7340031 | bytes 4198404 | tf_op jit(solution)/shard_map/reduce_sum | solution.py:209
  123.6 2.4 broadcast_divide_fusion.1
  126.1 3.5 %fusion.14 = f32[512,1024]{1,0:T(8,128)S(1)} fusion(f32[1024,1024]{1,0:T(8,128)S(1)} %broadcast_divide_fusion.1, f32[512,1024]{1,0:T(8,128)S(1)} %bitcast.46, f32[1024]{0:T(1024)S(1)} %fusion.52), kind=kOutput, calls=%fused_computation.20 | convolution fusion | flops 3225944064 | bytes 8392704 | tf_op jit(solution)/shard_map/dot_general | solution.py:240
  129.6 4.0 %fusion.72 = f32[512,1024]{1,0:T(8,128)S(1)} fusion(f32[512,1024]{1,0:T(8,128)S(1)} %fusion.14, f32[1024,1024]{1,0:T(8,128)S(1)} %broadcast_divide_fusion.1), kind=kOutput, calls=%fused_computation.112 | convolution fusion | flops 3221225472 | bytes 8388608 | tf_op jit(solution)/shard_map/dot_general | solution.py:241
  133.6 3.5 %fusion.12 = f32[512,1024]{1,0:T(8,128)S(1)} fusion(f32[512,1024]{1,0:T(8,128)S(1)} %fusion.72, f32[1024,1024]{1,0:T(8,128)S(1)} %broadcast_divide_fusion.1), kind=kOutput, calls=%fused_computation.19 | convolution fusion | flops 3225419776 | bytes 8388608 | tf_op jit(solution)/shard_map/dot_general | solution.py:242
  137.1 3.5 %subtract_multiply_fusion.1 = f32[512,1024]{1,0:T(8,128)S(1)} fusion(f32[512,1024]{1,0:T(8,128)S(1)} %fusion.14, f32[512,1024]{1,0:T(8,128)S(1)} %fusion.12, f32[1024,1024]{1,0:T(8,128)S(1)} %broadcast_divide_fusion.1, f32[1024]{0:T(1024)S(1)} %multiply_divide_fusion.1), kind=kOutput, calls=%fused_computation.28 | convolution fusion | flops 3226992640 | bytes 10489856 | tf_op jit(solution)/shard_map/dot_general | solution.py:243
  140.7 1.3 copy-done
  142.3 2.4 collective-permute-start
  144.7 3.5 %collective-permute-start.1 = (f32[512,512]{1,0:T(8,128)S(1)}, f32[512,512]{1,0:T(8,128)}, u32[]{:S(2)}, u32[]{:S(2)}) collective-permute-start(f32[512,512]{1,0:T(8,128)S(1)} %get-tuple-element.44), channel_id=1, source_target_pairs={{8,0},{16,8},{24,16},{32,24},{40,32},{48,40},{56,48},{64,56},{72,6... | collective-permute-start | bytes 3145736 | tf_op jit(solution)/shard_map/ppermute | solution.py:189
  148.7 7.8 %collective-permute-done = f32[512,512]{1,0:T(8,128)} collective-permute-done((f32[512,512]{1,0:T(8,128)S(1)}, f32[512,512]{1,0:T(8,128)}, u32[]{:S(2)}, u32[]{:S(2)}) %collective-permute-start) | collective-permute-done | bytes 1048608 | tf_op jit(solution)/shard_map/ppermute | solution.py:189
  156.4 8.1 %collective-permute-done.1 = f32[512,512]{1,0:T(8,128)} collective-permute-done((f32[512,512]{1,0:T(8,128)S(1)}, f32[512,512]{1,0:T(8,128)}, u32[]{:S(2)}, u32[]{:S(2)}) %collective-permute-start.1) | collective-permute-done | bytes 1048608 | tf_op jit(solution)/shard_map/ppermute | solution.py:189
  164.6 2.2 slice_select_fusion.4
  166.8 1.0 select_reduce_fusion.1
  169.9 1.5 select_maximum_fusion.payload
  171.4 45.7 %shard_map.29 = f32[1088,512]{1,0:T(8,128)} custom-call(f32[1088,512]{1,0:T(8,128)} %select_maximum_fusion.payload), custom_call_target="tpu_custom_call" | custom-call | tf_op jit(solution)/shard_map/pallas_call | solution.py:144
  217.2 2.3 slice.71
  220.1 1.6 copy.61
  221.7 1.3 broadcast_select_fusion.1
  223.0 2.5 copy.60
  225.5 4.4 %bitcast_add_fusion.1 = (f32[512,512]{1,0:T(8,128)}, f32[512]{0:T(512)S(1)}, f32[512,512]{1,0:T(8,128)S(1)}, f32[512,512]{1,0:T(8,128)}) fusion(f32[512,512]{0,1:T(8,128)} %copy-done.1, f32[1088,512]{1,0:T(8,128)} %shard_map.29, f32[512]{0:T(512)S(1)} %bitcast.57, f32[512,512]{1,0:T(8,128)} %copy.60, f32[512,512]{0,1:T(8,128)} %broadcast_select_fusion.1), kind=kLoop, calls=%fused_computation.53 | loop fusion | flops 3145216 | bytes 8392704 | tf_op jit(solution)/shard_map/add | solution.py:180
  229.9 1.3 copy.62
  231.2 3.8 %multiply_reduce_fusion = f32[]{:T(128)} fusion(f32[1024]{0:T(1024)S(1)} %fusion.51, f32[512,512]{1,0:T(8,128)} %get-tuple-element.49, f32[512,512]{1,0:T(8,128)} %bitcast.47, f32[512,512]{1,0:T(8,128)S(1)} %get-tuple-element.31, f32[512,512]{1,0:T(8,128)} %get-tuple-element.29), kind=kLoop, calls=%fused_computation.9 | loop fusion | flops 7340031 | bytes 4198404 | tf_op jit(solution)/shard_map/reduce_sum | solution.py:209
  235.8 2.4 broadcast_divide_fusion
  238.2 3.5 %fusion.8 = f32[512,1024]{1,0:T(8,128)S(1)} fusion(f32[1024,1024]{1,0:T(8,128)S(1)} %broadcast_divide_fusion, f32[512,512]{1,0:T(8,128)S(1)} %get-tuple-element.42, f32[512,512]{1,0:T(8,128)S(1)} %get-tuple-element.41, f32[1024]{0:T(1024)S(1)} %fusion.51), kind=kOutput, calls=%fused_computation.17 | convolution fusion | flops 3226468352 | bytes 8392704 | tf_op jit(solution)/shard_map/dot_general | solution.py:240
  241.7 4.0 %fusion.74 = f32[512,1024]{1,0:T(8,128)S(1)} fusion(f32[512,1024]{1,0:T(8,128)S(1)} %fusion.8, f32[1024,1024]{1,0:T(8,128)S(1)} %broadcast_divide_fusion), kind=kOutput, calls=%fused_computation.114 | convolution fusion | flops 3221225472 | bytes 8388608 | tf_op jit(solution)/shard_map/dot_general | solution.py:241
  245.7 3.5 %fusion.6 = f32[512,1024]{1,0:T(8,128)S(1)} fusion(f32[512,1024]{1,0:T(8,128)S(1)} %fusion.74, f32[1024,1024]{1,0:T(8,128)S(1)} %broadcast_divide_fusion), kind=kOutput, calls=%fused_computation.16 | convolution fusion | flops 3225419776 | bytes 8388608 | tf_op jit(solution)/shard_map/dot_general | solution.py:242
  249.2 3.6 %subtract_multiply_fusion = f32[512,1024]{1,0:T(8,128)S(1)} fusion(f32[512,1024]{1,0:T(8,128)S(1)} %fusion.8, f32[512,1024]{1,0:T(8,128)S(1)} %fusion.6, f32[1024,1024]{1,0:T(8,128)S(1)} %broadcast_divide_fusion, f32[1024]{0:T(1024)S(1)} %multiply_divide_fusion), kind=kOutput, calls=%fused_computation.26 | convolution fusion | flops 3226992640 | bytes 10489856 | tf_op jit(solution)/shard_map/dot_general | solution.py:243
  253.0 3.5 %collective-permute-start.2 = (f32[512,512]{1,0:T(8,128)S(1)}, f32[512,512]{1,0:T(8,128)S(1)}, u32[]{:S(2)}, u32[]{:S(2)}) collective-permute-start(f32[512,512]{1,0:T(8,128)S(1)} %get-tuple-element.39), channel_id=1, source_target_pairs={{0,8},{8,16},{16,24},{24,32},{32,40},{40,48},{48,56},{56,64},{64,7... | collective-permute-start | bytes 3145736 | tf_op jit(solution)/shard_map/ppermute | solution.py:189
  256.6 2.2 collective-permute-start.3
  258.7 9.5 %collective-permute-done.2 = f32[512,512]{1,0:T(8,128)S(1)} collective-permute-done((f32[512,512]{1,0:T(8,128)S(1)}, f32[512,512]{1,0:T(8,128)S(1)}, u32[]{:S(2)}, u32[]{:S(2)}) %collective-permute-start.2) | collective-permute-done | bytes 1048608 | tf_op jit(solution)/shard_map/ppermute | solution.py:189
  268.3 8.0 %collective-permute-done.3 = f32[512,512]{1,0:T(8,128)S(1)} collective-permute-done((f32[512,512]{1,0:T(8,128)S(1)}, f32[512,512]{1,0:T(8,128)S(1)}, u32[]{:S(2)}, u32[]{:S(2)}) %collective-permute-start.3) | collective-permute-done | bytes 1048608 | tf_op jit(solution)/shard_map/ppermute | solution.py:189
  276.7 1.5 pad_maximum_fusion
  (25 shorter events, 8.7 us)
Async XLA Ops:
  14.3 37.0 %all-to-all-start = ((f32[32,16,1024]{2,0,1:T(8,128)}), f32[32,16,1024]{2,0,1:T(8,128)S(1)}, u32[]{:S(2)}, u32[]{:S(2)}) async-start(f32[32,16,1024]{2,0,1:T(8,128)} %copy.47), calls=%async_computation | async-start | bytes 4194304 | tf_op jit(solution)/shard_map/all_to_all | solution.py:221
  140.7 1.3 copy-start
  142.3 14.2 %collective-permute-start = (f32[512,512]{1,0:T(8,128)S(1)}, f32[512,512]{1,0:T(8,128)}, u32[]{:S(2)}, u32[]{:S(2)}) collective-permute-start(f32[512,512]{1,0:T(8,128)S(1)} %get-tuple-element.43), channel_id=1, source_target_pairs={{0,8},{8,16},{16,24},{24,32},{32,40},{40,48},{48,56},{56,64},{64,7... | collective-permute-start | bytes 3145736 | tf_op jit(solution)/shard_map/ppermute | solution.py:189
  144.7 19.8 %collective-permute-start.1 = (f32[512,512]{1,0:T(8,128)S(1)}, f32[512,512]{1,0:T(8,128)}, u32[]{:S(2)}, u32[]{:S(2)}) collective-permute-start(f32[512,512]{1,0:T(8,128)S(1)} %get-tuple-element.44), channel_id=1, source_target_pairs={{8,0},{16,8},{24,16},{32,24},{40,32},{48,40},{56,48},{64,56},{72,6... | collective-permute-start | bytes 3145736 | tf_op jit(solution)/shard_map/ppermute | solution.py:189
  221.7 3.8 %copy-start.1 = (f32[512,512]{0,1:T(8,128)}, f32[512,512]{0,1:T(8,128)S(1)}, u32[]{:S(2)}) copy-start(f32[512,512]{0,1:T(8,128)S(1)} %copy.61) | copy-start | bytes 3145732
  253.0 15.3 %collective-permute-start.2 = (f32[512,512]{1,0:T(8,128)S(1)}, f32[512,512]{1,0:T(8,128)S(1)}, u32[]{:S(2)}, u32[]{:S(2)}) collective-permute-start(f32[512,512]{1,0:T(8,128)S(1)} %get-tuple-element.39), channel_id=1, source_target_pairs={{0,8},{8,16},{16,24},{24,32},{32,40},{40,48},{48,56},{56,64},{64,7... | collective-permute-start | bytes 3145736 | tf_op jit(solution)/shard_map/ppermute | solution.py:189
  256.6 19.7 %collective-permute-start.3 = (f32[512,512]{1,0:T(8,128)S(1)}, f32[512,512]{1,0:T(8,128)S(1)}, u32[]{:S(2)}, u32[]{:S(2)}) collective-permute-start(f32[512,512]{1,0:T(8,128)S(1)} %get-tuple-element.40), channel_id=1, source_target_pairs={{8,0},{16,8},{24,16},{32,24},{40,32},{48,40},{56,48},{64,56},{72,6... | collective-permute-start | bytes 3145736 | tf_op jit(solution)/shard_map/ppermute | solution.py:189
where the time goes:
time: 284 us; the launch traced here: 278 us
  Pallas kernels  96.4 us (34%)
  waiting for transfers between devices  62.8 us (22%)
  matrix products  35.4 us (12%)
  other arithmetic  33.7 us (12%)
  local copies, waits for them, and re-layouts  29 us (10%)
  starting transfers between devices  19.2 us (7%)
    pallas_call x2, Pallas kernels, rows_sum(): pl.pallas_call(functools.partial(rows_sum_kernel, outer, inner), out_shap...  96.4 us
    ppermute x4, waiting for transfers between devices, from_behind(): return lax.ppermute(x, axis, pairs)  33.4 us
    all_to_all x1, waiting for transfers between devices, per_device(): lax.all_to_all(slots, 'pair', split_axis=1, concat_axis=0, tiled=True)  29.3 us
    dot_general x4, matrix products, per_device(): jnp.dot(chain, first_iter, precision=fast, preferred_element_type=jnp.flo...  14.1 us
    ppermute x4, starting transfers between devices, from_behind(): return lax.ppermute(x, axis, pairs)  11.6 us
    add x2, other arithmetic, summed_gram(): upper_gram = jnp.where(col >= row, packed, 0.0) + strict_upper.T  8.24 us
    gather x3, local copies, waits for them, and re-layouts, per_device(): slots = jnp.take(blocks, plan, axis=1).reshape(local_rows, -1)  8.09 us
    dot_general x2, matrix products, per_device(): jnp.dot(applied, scaled_gram, precision=fast, preferred_element_type=jnp....  7.97 us
  transfers between devices with their start and end apart: 5, of which 5 were waited for; matrix products, arithmetic and copies ran while one was open for 0% of the time, Pallas kernels for 0%

commit v1 on v0

--- a/solution.py
+++ b/solution.py
@@ -55,7 +55,27 @@
 
 
 def rows_sum_kernel(
-    outer, inner, payload, out, a_in, a_acc, a_halves, a_own, a_all, b_in, b_acc, b_parts, b_own, b_row, b_all, sends, recvs
+    outer,
+    inner,
+    payload,
+    scaled_out,
+    first_out,
+    inverse_out,
+    factor_out,
+    a_in,
+    a_acc,
+    a_halves,
+    a_own,
+    a_all,
+    b_in,
+    b_acc,
+    b_parts,
+    b_own,
+    b_row,
+    b_all,
+    out,
+    sends,
+    recvs,
 ):
     pair = lax.axis_index("pair")
     me_y = lax.axis_index("ylo")
@@ -132,6 +152,53 @@
     for j in range(outer):
         for k in range(inner):
             out[pl.ds(j * b_half + k * b_chunk, b_chunk), cols_b] = b_all[j, k]
+    normalize_packed(out, scaled_out, first_out, inverse_out, factor_out)
+
+
+def normalize_packed(packed, scaled_out, first_out, inverse_out, factor_out):
+    width = packed.shape[1]
+    row = lax.broadcasted_iota(jnp.int32, (width, width), 0)
+    col = lax.broadcasted_iota(jnp.int32, (width, width), 1)
+    eye = row == col
+    top = packed[pl.ds(0, width), :]
+    cross = packed[pl.ds(width, width), :]
+    lower_diagonal = packed[pl.ds(2 * width, 1), :]
+    strict_upper = jnp.where(col > row, top, 0.0)
+    upper = jnp.where(col >= row, top, 0.0) + strict_upper.T
+    strict_lower = jnp.where(col < row, top, 0.0)
+    lower = strict_lower + strict_lower.T + jnp.where(eye, lower_diagonal, 0.0)
+    upper_row = jnp.sum(jnp.where(eye, top, 0.0), axis=0, keepdims=True) + epsilon
+    upper_col = jnp.sum(jnp.where(eye, top, 0.0), axis=1, keepdims=True) + epsilon
+    lower_row = lower_diagonal + epsilon
+    lower_col = jnp.sum(jnp.where(eye, lower, 0.0), axis=1, keepdims=True) + epsilon
+    inv_upper_row, inv_upper_col = 1.0 / jnp.sqrt(upper_row), 1.0 / jnp.sqrt(upper_col)
+    inv_lower_row, inv_lower_col = 1.0 / jnp.sqrt(lower_row), 1.0 / jnp.sqrt(lower_col)
+    upper = upper * inv_upper_col * inv_upper_row
+    lower = lower * inv_lower_col * inv_lower_row
+    cross = cross * inv_upper_col * inv_lower_row
+
+    def total(v):
+        return jnp.sum(jnp.sum(v * v, axis=0, keepdims=True), axis=1, keepdims=True)
+
+    squares = total(upper) + total(lower) + 2.0 * total(cross)
+    spread = 1.5 * jnp.sqrt(squares) / jnp.sqrt(jnp.float32(2 * width))
+    upper = upper / spread
+    lower = lower / spread
+    cross = cross / spread
+    three = jnp.where(eye, 3.0, 0.0)
+    near, far = pl.ds(0, width), pl.ds(width, width)
+    scaled_out[near, near] = upper
+    scaled_out[near, far] = cross
+    scaled_out[far, near] = cross.T
+    scaled_out[far, far] = lower
+    first_out[near, near] = 0.5 * (three - upper)
+    first_out[near, far] = 0.5 * (0.0 - cross)
+    first_out[far, near] = 0.5 * (0.0 - cross.T)
+    first_out[far, far] = 0.5 * (three - lower)
+    inverse_out[:, near] = inv_upper_row
+    inverse_out[:, far] = inv_lower_row
+    factor_out[:, near] = 0.5 * jnp.sqrt(upper_row) / jnp.sqrt(spread)
+    factor_out[:, far] = 0.5 * jnp.sqrt(lower_row) / jnp.sqrt(spread)
 
 
 def rows_sum(v, outer, inner):
@@ -143,9 +210,14 @@
     b_chunk = b_half // inner
     return pl.pallas_call(
         functools.partial(rows_sum_kernel, outer, inner),
-        out_shape=jax.ShapeDtypeStruct(v.shape, v.dtype),
+        out_shape=(
+            jax.ShapeDtypeStruct((2 * width, 2 * width), jnp.float32),
+            jax.ShapeDtypeStruct((2 * width, 2 * width), jnp.float32),
+            jax.ShapeDtypeStruct((1, 2 * width), jnp.float32),
+            jax.ShapeDtypeStruct((1, 2 * width), jnp.float32),
+        ),
         in_specs=[pl.BlockSpec(memory_space=pltpu.VMEM)],
-        out_specs=pl.BlockSpec(memory_space=pltpu.VMEM),
+        out_specs=[pl.BlockSpec(memory_space=pltpu.VMEM)] * 4,
         scratch_shapes=[
             pltpu.VMEM((inner - 1, a_chunk, half_w), jnp.float32),
             pltpu.VMEM((a_chunk, half_w), jnp.float32),
@@ -158,6 +230,7 @@
             pltpu.VMEM((b_chunk, half_w), jnp.float32),
             pltpu.VMEM((inner, b_chunk, half_w), jnp.float32),
             pltpu.VMEM((outer, inner, b_chunk, half_w), jnp.float32),
+            pltpu.VMEM((rows, width), jnp.float32),
             pltpu.SemaphoreType.DMA((16,)),
             pltpu.SemaphoreType.DMA((16,)),
         ],
@@ -174,13 +247,7 @@
     cross_gram = inner_gram(upper, lower)
     packed = jnp.where(col >= row, upper_gram, lower_gram)
     tail = jnp.zeros((64, width), jnp.float32).at[0].set(masked_diagonal(lower_gram))
-    total = rows_sum(jnp.concatenate([packed, cross_gram, tail]), outer, inner)
-    packed, cross_gram, lower_diagonal = total[:width], total[width : 2 * width], total[2 * width]
-    strict_upper = jnp.where(col > row, packed, 0.0)
-    upper_gram = jnp.where(col >= row, packed, 0.0) + strict_upper.T
-    strict_lower = jnp.where(col < row, packed, 0.0)
-    lower_gram = strict_lower + strict_lower.T + jnp.where(col == row, lower_diagonal[None, :], 0.0)
-    return upper_gram, lower_gram, cross_gram, masked_diagonal(packed), lower_diagonal
+    return rows_sum(jnp.concatenate([packed, cross_gram, tail]), outer, inner)
 
 
 def from_behind(x, axis, by):
@@ -224,24 +291,13 @@
     for turn_index in range(STEPS):
         upper = current[:, :BLK]
         lower = current[:, BLK:]
-        upper_gram, lower_gram, cross_gram, upper_diagonal, lower_diagonal = summed_gram(
-            upper, lower, outer, inner
-        )
-        gram = jnp.concatenate(
-            [
-                jnp.concatenate([upper_gram, cross_gram], axis=1),
-                jnp.concatenate([cross_gram.T, lower_gram], axis=1),
-            ],
-            axis=0,
-        )
-        diagonal = jnp.concatenate([upper_diagonal, lower_diagonal])
-        scaled_gram, first_iter, inverse, factor, identity = normalize(gram, diagonal)
-        weighted = current * inverse[None, :]
+        scaled_gram, first_iter, inverse, factor = summed_gram(upper, lower, outer, inner)
+        weighted = current * inverse
         applied = jnp.dot(weighted, first_iter, precision=fast, preferred_element_type=jnp.float32)
         chain = jnp.dot(applied, scaled_gram, precision=fast, preferred_element_type=jnp.float32)
         chain = jnp.dot(chain, first_iter, precision=fast, preferred_element_type=jnp.float32)
         chain = jnp.dot(chain, first_iter, precision=fast, preferred_element_type=jnp.float32)
-        current = (3.0 * applied - chain) * factor[None, :]
+        current = (3.0 * applied - chain) * factor
         upper = current[:, :BLK]
         lower = current[:, BLK:]
         outgoing = jnp.where(pair_index == 0, lower, upper)

time: 284 us -> 255 us (0.90)
  other arithmetic: 33.7 us -> 8.97 us
  local copies, waits for them, and re-layouts: 29 us -> 13.7 us
  Pallas kernels: 96.4 us -> 104 us
  matrix products: 35.4 us -> 40 us
    add x3 -> x0, other arithmetic: 10.9 us -> none  [the longest x2 8.24 us: summed_gram(): upper_gram = jnp.where(col >= row, packed, 0.0) + strict_upper.T]
    pallas_call x2, Pallas kernels: 96.4 us -> 104 us  [rows_sum(): pl.pallas_call(functools.partial(rows_sum_kernel, outer, inner), out_shap...]
    reduce_sum x2 -> x0, other arithmetic: 7.45 us -> none  [normalize(): jnp.sum(normed * normed)]
    slice x5 -> x0, local copies, waits for them, and re-layouts: 6.3 us -> none  [the longest x3 4.86 us: summed_gram(): total[:width]]
    dot_general x2, matrix products: 7.09 us -> 12.5 us  [per_device(): jnp.dot(weighted, first_iter, precision=fast, preferred_element_type=jnp....]
    div x4 -> x0, other arithmetic: 4.83 us -> none  [the longest x2 4.8 us: normalize(): scaled_gram = normed / spread]
    select_n x2 -> x0, local copies, waits for them, and re-layouts: 3.85 us -> none  [summed_gram(): strict_lower = jnp.where(col < row, packed, 0.0)]
    unnamed x7 -> x15, local copies, waits for them, and re-layouts: 4.21 us -> 1.1 us
where the time goes in v1:
time: 255 us; the launch traced here: 250 us
  Pallas kernels  104 us (41%)
  waiting for transfers between devices  63.1 us (25%)
  matrix products  40 us (16%)
  starting transfers between devices  19.5 us (8%)
  local copies, waits for them, and re-layouts  13.7 us (5%)
  other arithmetic  8.97 us (4%)
    pallas_call x2, Pallas kernels, rows_sum(): pl.pallas_call(functools.partial(rows_sum_kernel, outer, inner), out_shap...  104 us
    ppermute x4, waiting for transfers between devices, from_behind(): return lax.ppermute(x, axis, pairs)  33.7 us
    all_to_all x1, waiting for transfers between devices, per_device(): lax.all_to_all(slots, 'pair', split_axis=1, concat_axis=0, tiled=True)  29.4 us
    dot_general x4, matrix products, per_device(): jnp.dot(chain, first_iter, precision=fast, preferred_element_type=jnp.flo...  14.3 us
    dot_general x2, matrix products, per_device(): jnp.dot(weighted, first_iter, precision=fast, preferred_element_type=jnp....  12.5 us
    ppermute x4, starting transfers between devices, from_behind(): return lax.ppermute(x, axis, pairs)  11.6 us
    all_to_all x1, starting transfers between devices, per_device(): lax.all_to_all(slots, 'pair', split_axis=1, concat_axis=0, tiled=True)  7.85 us
    dot_general x2, matrix products, per_device(): jnp.dot(applied, scaled_gram, precision=fast, preferred_element_type=jnp....  7.14 us
  transfers between devices with their start and end apart: 5, of which 5 were waited for; matrix products, arithmetic and copies ran while one was open for 0% of the time, Pallas kernels for 0%

profile of v1, /device:TPU:97, one launch (start us, length us, event | category | flops | bytes accessed | tf_op | source)
XLA Modules:
  0.0 250.3 jit_solution(14191070344083735632)
XLA Ops:
  0.0 0.7 compare_and_fusion
  0.7 0.7 compare_select_fusion
  1.3 0.1 broadcast_in_dim.23
  1.4 0.1 broadcast_in_dim.24
  1.5 3.2 %copy.12 = f32[4,32,8,512]{3,2,0,1:T(8,128)} copy(f32[4,32,8,512]{3,2,1,0:T(8,128)} %bitcast.42) | data formatting | bytes 4194304 | tf_op jit(solution)/shard_map/reshape | solution.py:286
  4.7 2.3 gather_fusion
  7.0 2.5 %copy.7 = f32[32,32,512]{2,1,0:T(8,128)} copy(f32[32,32,512]{2,0,1:T(8,128)S(1)} %bitcast.40) | data formatting | bytes 4194304 | tf_op jit(solution)/shard_map/jit(_take)/gather | solution.py:287
  9.5 1.9 gather.7
  11.4 0.2 broadcast_select_fusion
  11.7 2.5 %copy.8 = f32[32,16,1024]{2,0,1:T(8,128)} copy(f32[32,16,1024]{2,1,0:T(8,128)S(1)} %broadcast_select_fusion) | data formatting | bytes 4194304 | tf_op jit(solution)/shard_map/jit(_take)/select_n | solution.py:287
  14.2 7.8 %all-to-all-start = ((f32[32,16,1024]{2,0,1:T(8,128)}), f32[32,16,1024]{2,0,1:T(8,128)S(1)}, u32[]{:S(2)}, u32[]{:S(2)}) async-start(f32[32,16,1024]{2,0,1:T(8,128)} %copy.8), calls=%async_computation | async-start | bytes 4194304 | tf_op jit(solution)/shard_map/all_to_all | solution.py:288
  22.1 29.4 %all-to-all-done = f32[32,16,1024]{2,0,1:T(8,128)S(1)} async-done(((f32[32,16,1024]{2,0,1:T(8,128)}), f32[32,16,1024]{2,0,1:T(8,128)S(1)}, u32[]{:S(2)}, u32[]{:S(2)}) %all-to-all-start) | async-done | bytes 2097184 | tf_op jit(solution)/shard_map/all_to_all | solution.py:288
  51.5 1.0 fusion.7
  52.5 1.0 select_reduce_fusion.1
  53.6 1.0 convolution_select_fusion.1
  54.6 1.6 select_maximum_fusion.1.payload
  56.2 54.7 %shard_map.28 = (f32[1024,1024]{1,0:T(8,128)}, f32[1024,1024]{1,0:T(8,128)}, f32[1,1024]{1,0:T(1,128)}, f32[1,1024]{1,0:T(1,128)}) custom-call(f32[1088,512]{1,0:T(8,128)} %select_maximum_fusion.1.payload), custom_call_target="tpu_custom_call" | custom-call | tf_op jit(solution)/shard_map/pallas_call | solution.py:211
  110.9 6.4 %fusion.3 = f32[512,1024]{1,0:T(8,128)S(1)} fusion(f32[1024,1024]{1,0:T(8,128)} %get-tuple-element.38, f32[512,1024]{1,0:T(8,128)S(1)} %bitcast.39, f32[1024]{0:T(1024)} %bitcast.50), kind=kOutput, calls=%fused_computation.12 | convolution fusion | flops 3221749760 | bytes 8392704 | tf_op jit(solution)/shard_map/dot_general | solution.py:296
  117.4 3.6 %fusion.14 = f32[512,1024]{1,0:T(8,128)S(1)} fusion(f32[512,1024]{1,0:T(8,128)S(1)} %fusion.3, f32[1024,1024]{1,0:T(8,128)S(1)} %copy-done.4), kind=kOutput, calls=%fused_computation.39 | convolution fusion | flops 3221225472 | bytes 8388608 | tf_op jit(solution)/shard_map/dot_general | solution.py:297
  120.9 0.0 copy-done.1
  120.9 0.0 copy-start.6
  120.9 3.6 %fusion.15 = f32[512,1024]{1,0:T(8,128)S(1)} fusion(f32[512,1024]{1,0:T(8,128)S(1)} %fusion.14, f32[1024,1024]{1,0:T(8,128)S(1)} %copy-done.1), kind=kOutput, calls=%fused_computation.40 | convolution fusion | flops 3221225472 | bytes 8388608 | tf_op jit(solution)/shard_map/dot_general | solution.py:298
  124.5 0.0 copy-done.6
  124.5 3.6 %subtract_multiply_fusion.1 = f32[512,1024]{1,0:T(8,128)S(1)} fusion(f32[512,1024]{1,0:T(8,128)S(1)} %fusion.3, f32[512,1024]{1,0:T(8,128)S(1)} %fusion.15, f32[1024,1024]{1,0:T(8,128)S(1)} %copy-done.1, f32[1024]{0:T(1024)S(1)} %bitcast.48), kind=kOutput, calls=%fused_computation.11 | convolution fusion | flops 3222798336 | bytes 10489856 | tf_op jit(solution)/shard_map/dot_general | solution.py:299
  128.1 0.0 copy-start.2
  128.1 0.2 slice_select_fusion.5
  128.4 1.1 copy-done.2
  129.4 2.4 collective-permute-start
  131.8 3.3 %collective-permute-start.1 = (f32[512,512]{1,0:T(8,128)S(1)}, f32[512,512]{1,0:T(8,128)}, u32[]{:S(2)}, u32[]{:S(2)}) collective-permute-start(f32[512,512]{1,0:T(8,128)S(1)} %get-tuple-element.52), channel_id=1, source_target_pairs={{8,0},{16,8},{24,16},{32,24},{40,32},{48,40},{56,48},{64,56},{72,6... | collective-permute-start | bytes 3145736 | tf_op jit(solution)/shard_map/ppermute | solution.py:256
  135.1 8.4 %collective-permute-done = f32[512,512]{1,0:T(8,128)S(1)} collective-permute-done((f32[512,512]{1,0:T(8,128)S(1)}, f32[512,512]{1,0:T(8,128)S(1)}, u32[]{:S(2)}, u32[]{:S(2)}) %collective-permute-start) | collective-permute-done | bytes 1048608 | tf_op jit(solution)/shard_map/ppermute | solution.py:256
  143.5 8.1 %collective-permute-done.1 = f32[512,512]{1,0:T(8,128)} collective-permute-done((f32[512,512]{1,0:T(8,128)S(1)}, f32[512,512]{1,0:T(8,128)}, u32[]{:S(2)}, u32[]{:S(2)}) %collective-permute-start.1) | collective-permute-done | bytes 1048608 | tf_op jit(solution)/shard_map/ppermute | solution.py:256
  151.6 1.9 slice_select_fusion.4
  153.5 1.0 select_reduce_fusion
  154.5 1.0 fusion.16
  155.6 1.0 convolution_select_fusion
  156.6 1.6 select_maximum_fusion.payload
  158.2 49.8 %shard_map.29 = (f32[1024,1024]{1,0:T(8,128)}, f32[1024,1024]{1,0:T(8,128)}, f32[1,1024]{1,0:T(1,128)}, f32[1,1024]{1,0:T(1,128)}) custom-call(f32[1088,512]{1,0:T(8,128)} %select_maximum_fusion.payload), custom_call_target="tpu_custom_call" | custom-call | tf_op jit(solution)/shard_map/pallas_call | solution.py:211
  208.0 6.1 %fusion = f32[512,1024]{1,0:T(8,128)S(1)} fusion(f32[1024,1024]{1,0:T(8,128)} %get-tuple-element.42, f32[512,512]{1,0:T(8,128)S(1)} %get-tuple-element.50, f32[512,512]{1,0:T(8,128)S(1)} %get-tuple-element.49, f32[1024]{0:T(1024)} %bitcast.49), kind=kOutput, calls=%fused_computation.6 | convolution fusion | flops 3222274048 | bytes 8392704 | tf_op jit(solution)/shard_map/dot_general | solution.py:296
  214.1 3.6 %fusion.17 = f32[512,1024]{1,0:T(8,128)S(1)} fusion(f32[512,1024]{1,0:T(8,128)S(1)} %fusion, f32[1024,1024]{1,0:T(8,128)S(1)} %copy-done.3), kind=kOutput, calls=%fused_computation.42 | convolution fusion | flops 3221225472 | bytes 8388608 | tf_op jit(solution)/shard_map/dot_general | solution.py:297
  217.7 3.6 %fusion.18 = f32[512,1024]{1,0:T(8,128)S(1)} fusion(f32[512,1024]{1,0:T(8,128)S(1)} %fusion.17, f32[1024,1024]{1,0:T(8,128)S(1)} %copy-done), kind=kOutput, calls=%fused_computation.43 | convolution fusion | flops 3221225472 | bytes 8388608 | tf_op jit(solution)/shard_map/dot_general | solution.py:298
  221.3 3.6 %subtract_multiply_fusion = f32[512,1024]{1,0:T(8,128)S(1)} fusion(f32[512,1024]{1,0:T(8,128)S(1)} %fusion, f32[512,1024]{1,0:T(8,128)S(1)} %fusion.18, f32[1024,1024]{1,0:T(8,128)S(1)} %copy-done, f32[1024]{0:T(1024)S(1)} %bitcast.47), kind=kOutput, calls=%fused_computation.10 | convolution fusion | flops 3222798336 | bytes 10489856 | tf_op jit(solution)/shard_map/dot_general | solution.py:299
  224.9 0.2 slice_select_fusion.2
  225.1 3.4 %collective-permute-start.2 = (f32[512,512]{1,0:T(8,128)S(1)}, f32[512,512]{1,0:T(8,128)S(1)}, u32[]{:S(2)}, u32[]{:S(2)}) collective-permute-start(f32[512,512]{1,0:T(8,128)S(1)} %get-tuple-element.47), channel_id=1, source_target_pairs={{0,8},{8,16},{16,24},{24,32},{32,40},{40,48},{48,56},{56,64},{64,7... | collective-permute-start | bytes 3145736 | tf_op jit(solution)/shard_map/ppermute | solution.py:256
  228.6 2.5 %collective-permute-start.3 = (f32[512,512]{1,0:T(8,128)S(1)}, f32[512,512]{1,0:T(8,128)S(1)}, u32[]{:S(2)}, u32[]{:S(2)}) collective-permute-start(f32[512,512]{1,0:T(8,128)S(1)} %get-tuple-element.48), channel_id=1, source_target_pairs={{8,0},{16,8},{24,16},{32,24},{40,32},{48,40},{56,48},{64,56},{72,6... | collective-permute-start | bytes 3145736 | tf_op jit(solution)/shard_map/ppermute | solution.py:256
  231.1 9.2 %collective-permute-done.2 = f32[512,512]{1,0:T(8,128)S(1)} collective-permute-done((f32[512,512]{1,0:T(8,128)S(1)}, f32[512,512]{1,0:T(8,128)S(1)}, u32[]{:S(2)}, u32[]{:S(2)}) %collective-permute-start.2) | collective-permute-done | bytes 1048608 | tf_op jit(solution)/shard_map/ppermute | solution.py:256
  240.3 8.0 %collective-permute-done.3 = f32[512,512]{1,0:T(8,128)S(1)} collective-permute-done((f32[512,512]{1,0:T(8,128)S(1)}, f32[512,512]{1,0:T(8,128)S(1)}, u32[]{:S(2)}, u32[]{:S(2)}) %collective-permute-start.3) | collective-permute-done | bytes 1048608 | tf_op jit(solution)/shard_map/ppermute | solution.py:256
  248.3 0.3 slice_select_fusion.1
  248.7 1.5 pad_maximum_fusion
  (11 shorter events, 0.0 us)
Async XLA Ops:
  14.2 37.3 %all-to-all-start = ((f32[32,16,1024]{2,0,1:T(8,128)}), f32[32,16,1024]{2,0,1:T(8,128)S(1)}, u32[]{:S(2)}, u32[]{:S(2)}) async-start(f32[32,16,1024]{2,0,1:T(8,128)} %copy.8), calls=%async_computation | async-start | bytes 4194304 | tf_op jit(solution)/shard_map/all_to_all | solution.py:288
  110.9 6.4 %copy-start.4 = (f32[1024,1024]{1,0:T(8,128)S(1)}, f32[1024,1024]{1,0:T(8,128)}, u32[]{:S(2)}) copy-start(f32[1024,1024]{1,0:T(8,128)} %get-tuple-element.39) | copy-start | bytes 12582916
  117.3 3.6 %copy-start.1 = (f32[1024,1024]{1,0:T(8,128)S(1)}, f32[1024,1024]{1,0:T(8,128)}, u32[]{:S(2)}) copy-start(f32[1024,1024]{1,0:T(8,128)} %get-tuple-element.38) | copy-start | bytes 12582916
  120.9 3.6 %copy-start.6 = (f32[1,1024]{1,0:T(1,128)S(1)}, f32[1,1024]{1,0:T(1,128)}, u32[]{:S(2)}) copy-start(f32[1,1024]{1,0:T(1,128)} %get-tuple-element.40) | copy-start | bytes 12292
  128.1 1.3 copy-start.2
  129.4 14.1 %collective-permute-start = (f32[512,512]{1,0:T(8,128)S(1)}, f32[512,512]{1,0:T(8,128)S(1)}, u32[]{:S(2)}, u32[]{:S(2)}) collective-permute-start(f32[512,512]{1,0:T(8,128)S(1)} %get-tuple-element.51), channel_id=1, source_target_pairs={{0,8},{8,16},{16,24},{24,32},{32,40},{40,48},{48,56},{56,64},{64,7... | collective-permute-start | bytes 3145736 | tf_op jit(solution)/shard_map/ppermute | solution.py:256
  131.8 19.8 %collective-permute-start.1 = (f32[512,512]{1,0:T(8,128)S(1)}, f32[512,512]{1,0:T(8,128)}, u32[]{:S(2)}, u32[]{:S(2)}) collective-permute-start(f32[512,512]{1,0:T(8,128)S(1)} %get-tuple-element.52), channel_id=1, source_target_pairs={{8,0},{16,8},{24,16},{32,24},{40,32},{48,40},{56,48},{64,56},{72,6... | collective-permute-start | bytes 3145736 | tf_op jit(solution)/shard_map/ppermute | solution.py:256
  208.0 6.1 %copy-start.3 = (f32[1024,1024]{1,0:T(8,128)S(1)}, f32[1024,1024]{1,0:T(8,128)}, u32[]{:S(2)}) copy-start(f32[1024,1024]{1,0:T(8,128)} %get-tuple-element.43) | copy-start | bytes 12582916
  214.1 3.6 %copy-start = (f32[1024,1024]{1,0:T(8,128)S(1)}, f32[1024,1024]{1,0:T(8,128)}, u32[]{:S(2)}) copy-start(f32[1024,1024]{1,0:T(8,128)} %get-tuple-element.42) | copy-start | bytes 12582916
  217.7 3.6 %copy-start.5 = (f32[1,1024]{1,0:T(1,128)S(1)}, f32[1,1024]{1,0:T(1,128)}, u32[]{:S(2)}) copy-start(f32[1,1024]{1,0:T(1,128)} %get-tuple-element.44) | copy-start | bytes 12292
  225.1 15.2 %collective-permute-start.2 = (f32[512,512]{1,0:T(8,128)S(1)}, f32[512,512]{1,0:T(8,128)S(1)}, u32[]{:S(2)}, u32[]{:S(2)}) collective-permute-start(f32[512,512]{1,0:T(8,128)S(1)} %get-tuple-element.47), channel_id=1, source_target_pairs={{0,8},{8,16},{16,24},{24,32},{32,40},{40,48},{48,56},{56,64},{64,7... | collective-permute-start | bytes 3145736 | tf_op jit(solution)/shard_map/ppermute | solution.py:256
  228.6 19.7 %collective-permute-start.3 = (f32[512,512]{1,0:T(8,128)S(1)}, f32[512,512]{1,0:T(8,128)S(1)}, u32[]{:S(2)}, u32[]{:S(2)}) collective-permute-start(f32[512,512]{1,0:T(8,128)S(1)} %get-tuple-element.48), channel_id=1, source_target_pairs={{8,0},{16,8},{24,16},{32,24},{40,32},{48,40},{56,48},{64,56},{72,6... | collective-permute-start | bytes 3145736 | tf_op jit(solution)/shard_map/ppermute | solution.py:256

commit v2 on v1

--- a/solution.py
+++ b/solution.py
@@ -284,11 +284,11 @@
 def per_device(matrix, plan, outer, inner):
     local_rows = matrix.shape[0]
     blocks = matrix.reshape(local_rows, -1, BLK)
-    slots = jnp.take(blocks, plan, axis=1).reshape(local_rows, -1)
+    slots = jnp.take(blocks, plan, axis=1, mode="clip").reshape(local_rows, -1)
     current = lax.all_to_all(slots, "pair", split_axis=1, concat_axis=0, tiled=True)
     pair_index = lax.axis_index("pair")
     pair_count = lax.axis_size("pair")
-    for turn_index in range(STEPS):
+    def turn(turn_index, current):
         upper = current[:, :BLK]
         lower = current[:, BLK:]
         scaled_gram, first_iter, inverse, factor = summed_gram(upper, lower, outer, inner)
@@ -306,6 +306,9 @@
         new_upper = jnp.where(pair_index == 0, upper, arrived_up)
         new_lower = jnp.where(pair_index == pair_count - 1, upper, arrived_down)
         current = jnp.concatenate([new_upper, new_lower], axis=1)
+        return current
+
+    current = lax.fori_loop(0, STEPS, turn, current)
     return current
 
 

time: 255 us -> 252 us (0.988); the launches traced: 250 us -> 251 us
    all_to_all x0 -> x2, local copies, waits for them, and re-layouts: none -> 4.47 us  [per_device(): lax.all_to_all(slots, 'pair', split_axis=1, concat_axis=0, tiled=True)]
    select_n x6 -> x4, other arithmetic: 3.6 us -> 6.24 us  [the longest x2 3.79 us: turn(): new_upper = jnp.where(pair_index == 0, upper, arrived_up)]
    gather x3 -> x2, local copies, waits for them, and re-layouts: 6.74 us -> 4.81 us  [per_device(): slots = jnp.take(blocks, plan, axis=1, mode='clip').reshape(local_rows, -1)]
where the time goes in v2:
time: 252 us; the launch traced here: 251 us
  Pallas kernels  104 us (41%)
  waiting for transfers between devices  63.8 us (25%)
  matrix products  39.3 us (16%)
  starting transfers between devices  18.7 us (7%)
  local copies, waits for them, and re-layouts  13.8 us (5%)
  other arithmetic  10.4 us (4%)
    pallas_call x2, Pallas kernels, rows_sum(): pl.pallas_call(functools.partial(rows_sum_kernel, outer, inner), out_shap...  104 us
    ppermute x4, waiting for transfers between devices, from_behind(): return lax.ppermute(x, axis, pairs)  34.3 us
    all_to_all x1, waiting for transfers between devices, per_device(): lax.all_to_all(slots, 'pair', split_axis=1, concat_axis=0, tiled=True)  29.5 us
    dot_general x4, matrix products, turn(): jnp.dot(chain, first_iter, precision=fast, preferred_element_type=jnp.flo...  14.3 us
    dot_general x2, matrix products, turn(): jnp.dot(weighted, first_iter, precision=fast, preferred_element_type=jnp....  11.7 us
    ppermute x4, starting transfers between devices, from_behind(): return lax.ppermute(x, axis, pairs)  11.2 us
    all_to_all x1, starting transfers between devices, per_device(): lax.all_to_all(slots, 'pair', split_axis=1, concat_axis=0, tiled=True)  7.47 us
    dot_general x2, matrix products, turn(): jnp.dot(applied, scaled_gram, precision=fast, preferred_element_type=jnp....  7.11 us
  transfers between devices with their start and end apart: 5, of which 5 were waited for; matrix products, arithmetic and copies ran while one was open for 0% of the time, Pallas kernels for 0%

profile of v2, /device:TPU:97, one launch (start us, length us, event | category | flops | bytes accessed | tf_op | source)
XLA Modules:
  0.0 250.6 jit_solution(17990060495270725234)
XLA Ops:
  0.0 0.7 pad_clamp_fusion
  0.7 3.2 %copy.12 = f32[4,32,8,512]{3,2,0,1:T(8,128)} copy(f32[4,32,8,512]{3,2,1,0:T(8,128)} %bitcast.41) | data formatting | bytes 4194304 | tf_op jit(solution)/shard_map/reshape | solution.py:286
  3.8 2.3 gather_fusion
  6.1 2.5 %copy.8 = f32[32,32,512]{2,1,0:T(8,128)} copy(f32[32,32,512]{2,0,1:T(8,128)S(1)} %bitcast.39) | data formatting | bytes 4194304 | tf_op jit(solution)/shard_map/jit(_take)/gather | solution.py:287
  8.6 1.9 all_to_all.14
  10.6 2.5 %copy.9 = f32[32,16,1024]{2,0,1:T(8,128)} copy(f32[32,16,1024]{2,1,0:T(8,128)S(1)} %all_to_all.14) | data formatting | bytes 4194304 | tf_op jit(solution)/shard_map/all_to_all | solution.py:288
  13.1 7.5 %all-to-all-start = ((f32[32,16,1024]{2,0,1:T(8,128)}), f32[32,16,1024]{2,0,1:T(8,128)S(1)}, u32[]{:S(2)}, u32[]{:S(2)}) async-start(f32[32,16,1024]{2,0,1:T(8,128)} %copy.9), calls=%async_computation | async-start | bytes 4194304 | tf_op jit(solution)/shard_map/all_to_all | solution.py:288
  20.6 29.5 %all-to-all-done = f32[32,16,1024]{2,0,1:T(8,128)S(1)} async-done(((f32[32,16,1024]{2,0,1:T(8,128)}), f32[32,16,1024]{2,0,1:T(8,128)S(1)}, u32[]{:S(2)}, u32[]{:S(2)}) %all-to-all-start) | async-done | bytes 2097184 | tf_op jit(solution)/shard_map/all_to_all | solution.py:288
  50.1 199.2 %while.13 = (s32[]{:T(128)}, f32[512,1024]{1,0:T(8,128)S(1)}, pred[]{:T(512)}, pred[]{:T(512)}, s32[]{:T(128)}) while((s32[]{:T(128)}, f32[512,1024]{1,0:T(8,128)S(1)}, pred[]{:T(512)}, pred[]{:T(512)}, s32[]{:T(128)}) %tuple.42), condition=%wide.region_2.3_spmd, body=%wide.region_0.2_spmd.sunk | while | flops 15307767808 | bytes 103968984 | solution.py:311
  50.1 1.0 fusion.44
  51.1 1.0 select_reduce_fusion.2
  52.2 1.0 convolution_select_fusion.2
  53.2 1.6 select_maximum_fusion.2.payload
  54.8 54.7 %eval_jaxpr.4 = (f32[1024,1024]{1,0:T(8,128)}, f32[1024,1024]{1,0:T(8,128)}, f32[1,1024]{1,0:T(1,128)}, f32[1,1024]{1,0:T(1,128)}) custom-call(f32[1088,512]{1,0:T(8,128)} %select_maximum_fusion.2.payload), custom_call_target="tpu_custom_call" | custom-call | tf_op jit(solution)/shard_map/while/body/eval_jaxpr/pallas_call | solution.py:211
  109.5 5.9 %fusion.45 = f32[512,1024]{1,0:T(8,128)S(1)} fusion(f32[1024,1024]{1,0:T(8,128)} %get-tuple-element.122, f32[512,1024]{1,0:T(8,128)S(1)} %get-tuple-element.136, f32[1024]{0:T(1024)} %bitcast.44), kind=kOutput, calls=%fused_computation.5.clone.1 | convolution fusion | flops 3221749760 | bytes 8392704 | tf_op jit(solution)/shard_map/while/body/eval_jaxpr/dot_general | solution.py:296
  115.4 3.6 %fusion.46 = f32[512,1024]{1,0:T(8,128)S(1)} fusion(f32[512,1024]{1,0:T(8,128)S(1)} %fusion.45, f32[1024,1024]{1,0:T(8,128)S(1)} %copy-done.1), kind=kOutput, calls=%fused_computation.23.clone.1 | convolution fusion | flops 3221225472 | bytes 8388608 | tf_op jit(solution)/shard_map/while/body/eval_jaxpr/dot_general | solution.py:297
  118.9 0.0 copy-done
  118.9 0.0 copy-start.2
  118.9 3.6 %fusion.47 = f32[512,1024]{1,0:T(8,128)S(1)} fusion(f32[512,1024]{1,0:T(8,128)S(1)} %fusion.46, f32[1024,1024]{1,0:T(8,128)S(1)} %copy-done), kind=kOutput, calls=%fused_computation.24.clone.1 | convolution fusion | flops 3221225472 | bytes 8388608 | tf_op jit(solution)/shard_map/while/body/eval_jaxpr/dot_general | solution.py:298
  122.5 0.0 copy-done.2
  122.5 3.6 %subtract_multiply_fusion.2 = f32[512,1024]{1,0:T(8,128)S(1)} fusion(f32[512,1024]{1,0:T(8,128)S(1)} %fusion.45, f32[512,1024]{1,0:T(8,128)S(1)} %fusion.47, f32[1024,1024]{1,0:T(8,128)S(1)} %copy-done, f32[1024]{0:T(1024)S(1)} %bitcast.43), kind=kOutput, calls=%fused_computation.4.clone.1 | convolution fusion | flops 3222798336 | bytes 10489856 | tf_op jit(solution)/shard_map/while/body/eval_jaxpr/dot_general | solution.py:299
  126.1 1.2 slice_select_fusion.5
  127.3 2.4 collective-permute-start
  129.7 3.1 %collective-permute-start.1 = (f32[512,512]{1,0:T(8,128)S(1)}, f32[512,512]{1,0:T(8,128)}, u32[]{:S(2)}, u32[]{:S(2)}) collective-permute-start(f32[512,512]{1,0:T(8,128)S(1)} %get-tuple-element.127), channel_id=1, source_target_pairs={{8,0},{16,8},{24,16},{32,24},{40,32},{48,40},{56,48},{64,56},{72,6... | collective-permute-start | bytes 3145736 | tf_op jit(solution)/shard_map/while/body/eval_jaxpr/ppermute | solution.py:256
  132.8 8.9 %collective-permute-done = f32[512,512]{1,0:T(8,128)} collective-permute-done((f32[512,512]{1,0:T(8,128)}, f32[512,512]{1,0:T(8,128)}, u32[]{:S(2)}, u32[]{:S(2)}) %collective-permute-start) | collective-permute-done | bytes 1048608 | tf_op jit(solution)/shard_map/while/body/eval_jaxpr/ppermute | solution.py:256
  141.8 7.8 %collective-permute-done.1 = f32[512,512]{1,0:T(8,128)} collective-permute-done((f32[512,512]{1,0:T(8,128)S(1)}, f32[512,512]{1,0:T(8,128)}, u32[]{:S(2)}, u32[]{:S(2)}) %collective-permute-start.1) | collective-permute-done | bytes 1048608 | tf_op jit(solution)/shard_map/while/body/eval_jaxpr/ppermute | solution.py:256
  149.6 1.9 slice_select_fusion.6
  151.5 0.1 pad_maximum_fusion.2
  151.6 1.0 fusion.44
  152.7 1.0 select_reduce_fusion.2
  153.7 1.0 convolution_select_fusion.2
  154.7 1.6 select_maximum_fusion.2.payload
  156.3 49.8 %eval_jaxpr.4 = (f32[1024,1024]{1,0:T(8,128)}, f32[1024,1024]{1,0:T(8,128)}, f32[1,1024]{1,0:T(1,128)}, f32[1,1024]{1,0:T(1,128)}) custom-call(f32[1088,512]{1,0:T(8,128)} %select_maximum_fusion.2.payload), custom_call_target="tpu_custom_call" | custom-call | tf_op jit(solution)/shard_map/while/body/eval_jaxpr/pallas_call | solution.py:211
  206.1 5.9 %fusion.45 = f32[512,1024]{1,0:T(8,128)S(1)} fusion(f32[1024,1024]{1,0:T(8,128)} %get-tuple-element.122, f32[512,1024]{1,0:T(8,128)S(1)} %get-tuple-element.136, f32[1024]{0:T(1024)} %bitcast.44), kind=kOutput, calls=%fused_computation.5.clone.1 | convolution fusion | flops 3221749760 | bytes 8392704 | tf_op jit(solution)/shard_map/while/body/eval_jaxpr/dot_general | solution.py:296
  212.0 3.6 %fusion.46 = f32[512,1024]{1,0:T(8,128)S(1)} fusion(f32[512,1024]{1,0:T(8,128)S(1)} %fusion.45, f32[1024,1024]{1,0:T(8,128)S(1)} %copy-done.1), kind=kOutput, calls=%fused_computation.23.clone.1 | convolution fusion | flops 3221225472 | bytes 8388608 | tf_op jit(solution)/shard_map/while/body/eval_jaxpr/dot_general | solution.py:297
  215.5 0.0 copy-done
  215.6 0.0 copy-start.2
  215.6 3.6 %fusion.47 = f32[512,1024]{1,0:T(8,128)S(1)} fusion(f32[512,1024]{1,0:T(8,128)S(1)} %fusion.46, f32[1024,1024]{1,0:T(8,128)S(1)} %copy-done), kind=kOutput, calls=%fused_computation.24.clone.1 | convolution fusion | flops 3221225472 | bytes 8388608 | tf_op jit(solution)/shard_map/while/body/eval_jaxpr/dot_general | solution.py:298
  219.1 0.0 copy-done.2
  219.1 3.6 %subtract_multiply_fusion.2 = f32[512,1024]{1,0:T(8,128)S(1)} fusion(f32[512,1024]{1,0:T(8,128)S(1)} %fusion.45, f32[512,1024]{1,0:T(8,128)S(1)} %fusion.47, f32[1024,1024]{1,0:T(8,128)S(1)} %copy-done, f32[1024]{0:T(1024)S(1)} %bitcast.43), kind=kOutput, calls=%fused_computation.4.clone.1 | convolution fusion | flops 3222798336 | bytes 10489856 | tf_op jit(solution)/shard_map/while/body/eval_jaxpr/dot_general | solution.py:299
  222.7 1.2 slice_select_fusion.5
  223.9 3.5 %collective-permute-start = (f32[512,512]{1,0:T(8,128)}, f32[512,512]{1,0:T(8,128)}, u32[]{:S(2)}, u32[]{:S(2)}) collective-permute-start(f32[512,512]{1,0:T(8,128)} %get-tuple-element.126), channel_id=1, source_target_pairs={{0,8},{8,16},{16,24},{24,32},{32,40},{40,48},{48,56},{56,64},{64,7... | collective-permute-start | bytes 3145736 | tf_op jit(solution)/shard_map/while/body/eval_jaxpr/ppermute | solution.py:256
  227.4 2.3 collective-permute-start.1
  229.7 9.8 %collective-permute-done = f32[512,512]{1,0:T(8,128)} collective-permute-done((f32[512,512]{1,0:T(8,128)}, f32[512,512]{1,0:T(8,128)}, u32[]{:S(2)}, u32[]{:S(2)}) %collective-permute-start) | collective-permute-done | bytes 1048608 | tf_op jit(solution)/shard_map/while/body/eval_jaxpr/ppermute | solution.py:256
  239.5 7.8 %collective-permute-done.1 = f32[512,512]{1,0:T(8,128)} collective-permute-done((f32[512,512]{1,0:T(8,128)S(1)}, f32[512,512]{1,0:T(8,128)}, u32[]{:S(2)}, u32[]{:S(2)}) %collective-permute-start.1) | collective-permute-done | bytes 1048608 | tf_op jit(solution)/shard_map/while/body/eval_jaxpr/ppermute | solution.py:256
  247.3 1.9 slice_select_fusion.6
  249.2 0.1 pad_maximum_fusion.2
  249.3 1.3 copy.22
  (6 shorter events, 0.0 us)
Async XLA Ops:
  13.1 37.0 %all-to-all-start = ((f32[32,16,1024]{2,0,1:T(8,128)}), f32[32,16,1024]{2,0,1:T(8,128)S(1)}, u32[]{:S(2)}, u32[]{:S(2)}) async-start(f32[32,16,1024]{2,0,1:T(8,128)} %copy.9), calls=%async_computation | async-start | bytes 4194304 | tf_op jit(solution)/shard_map/all_to_all | solution.py:288
  109.5 5.9 %copy-start.1 = (f32[1024,1024]{1,0:T(8,128)S(1)}, f32[1024,1024]{1,0:T(8,128)}, u32[]{:S(2)}) copy-start(f32[1024,1024]{1,0:T(8,128)} %get-tuple-element.124) | copy-start | bytes 12582916 | tf_op jit(solution)/shard_map/while
  115.4 3.6 %copy-start = (f32[1024,1024]{1,0:T(8,128)S(1)}, f32[1024,1024]{1,0:T(8,128)}, u32[]{:S(2)}) copy-start(f32[1024,1024]{1,0:T(8,128)} %get-tuple-element.122) | copy-start | bytes 12582916 | tf_op jit(solution)/shard_map/while
  118.9 3.6 %copy-start.2 = (f32[1,1024]{1,0:T(1,128)S(1)}, f32[1,1024]{1,0:T(1,128)}, u32[]{:S(2)}) copy-start(f32[1,1024]{1,0:T(1,128)} %get-tuple-element.125) | copy-start | bytes 12292 | tf_op jit(solution)/shard_map/while
  127.3 14.4 %collective-permute-start = (f32[512,512]{1,0:T(8,128)}, f32[512,512]{1,0:T(8,128)}, u32[]{:S(2)}, u32[]{:S(2)}) collective-permute-start(f32[512,512]{1,0:T(8,128)} %get-tuple-element.126), channel_id=1, source_target_pairs={{0,8},{8,16},{16,24},{24,32},{32,40},{40,48},{48,56},{56,64},{64,7... | collective-permute-start | bytes 3145736 | tf_op jit(solution)/shard_map/while/body/eval_jaxpr/ppermute | solution.py:256
  129.7 19.8 %collective-permute-start.1 = (f32[512,512]{1,0:T(8,128)S(1)}, f32[512,512]{1,0:T(8,128)}, u32[]{:S(2)}, u32[]{:S(2)}) collective-permute-start(f32[512,512]{1,0:T(8,128)S(1)} %get-tuple-element.127), channel_id=1, source_target_pairs={{8,0},{16,8},{24,16},{32,24},{40,32},{48,40},{56,48},{64,56},{72,6... | collective-permute-start | bytes 3145736 | tf_op jit(solution)/shard_map/while/body/eval_jaxpr/ppermute | solution.py:256
  206.1 5.9 %copy-start.1 = (f32[1024,1024]{1,0:T(8,128)S(1)}, f32[1024,1024]{1,0:T(8,128)}, u32[]{:S(2)}) copy-start(f32[1024,1024]{1,0:T(8,128)} %get-tuple-element.124) | copy-start | bytes 12582916 | tf_op jit(solution)/shard_map/while
  212.0 3.6 %copy-start = (f32[1024,1024]{1,0:T(8,128)S(1)}, f32[1024,1024]{1,0:T(8,128)}, u32[]{:S(2)}) copy-start(f32[1024,1024]{1,0:T(8,128)} %get-tuple-element.122) | copy-start | bytes 12582916 | tf_op jit(solution)/shard_map/while
  215.6 3.6 %copy-start.2 = (f32[1,1024]{1,0:T(1,128)S(1)}, f32[1,1024]{1,0:T(1,128)}, u32[]{:S(2)}) copy-start(f32[1,1024]{1,0:T(1,128)} %get-tuple-element.125) | copy-start | bytes 12292 | tf_op jit(solution)/shard_map/while
  223.9 15.5 %collective-permute-start = (f32[512,512]{1,0:T(8,128)}, f32[512,512]{1,0:T(8,128)}, u32[]{:S(2)}, u32[]{:S(2)}) collective-permute-start(f32[512,512]{1,0:T(8,128)} %get-tuple-element.126), channel_id=1, source_target_pairs={{0,8},{8,16},{16,24},{24,32},{32,40},{40,48},{48,56},{56,64},{64,7... | collective-permute-start | bytes 3145736 | tf_op jit(solution)/shard_map/while/body/eval_jaxpr/ppermute | solution.py:256
  227.4 19.8 %collective-permute-start.1 = (f32[512,512]{1,0:T(8,128)S(1)}, f32[512,512]{1,0:T(8,128)}, u32[]{:S(2)}, u32[]{:S(2)}) collective-permute-start(f32[512,512]{1,0:T(8,128)S(1)} %get-tuple-element.127), channel_id=1, source_target_pairs={{8,0},{16,8},{24,16},{32,24},{40,32},{48,40},{56,48},{64,56},{72,6... | collective-permute-start | bytes 3145736 | tf_op jit(solution)/shard_map/while/body/eval_jaxpr/ppermute | solution.py:256

commit v3 on v2

--- a/solution.py
+++ b/solution.py
@@ -283,9 +283,13 @@
 
 def per_device(matrix, plan, outer, inner):
     local_rows = matrix.shape[0]
-    blocks = matrix.reshape(local_rows, -1, BLK)
-    slots = jnp.take(blocks, plan, axis=1, mode="clip").reshape(local_rows, -1)
-    current = lax.all_to_all(slots, "pair", split_axis=1, concat_axis=0, tiled=True)
+    blocks = jnp.transpose(matrix.reshape(local_rows, -1, BLK), (1, 0, 2))
+    pair_count = lax.axis_size("pair")
+    slots = jnp.take(blocks, plan, axis=0, mode="clip").reshape(pair_count, 2, local_rows, BLK)
+    arrived = lax.all_to_all(slots, "pair", split_axis=0, concat_axis=0, tiled=True)
+    current = jnp.concatenate(
+        [arrived[:, 0].reshape(-1, BLK), arrived[:, 1].reshape(-1, BLK)], axis=1
+    )
     pair_index = lax.axis_index("pair")
     pair_count = lax.axis_size("pair")
     def turn(turn_index, current):

time: 252 us -> 244 us (0.968)
  local copies, waits for them, and re-layouts: 13.8 us -> 5.34 us
    all_to_all x2 -> x0, local copies, waits for them, and re-layouts: 4.47 us -> none  [per_device(): lax.all_to_all(slots, 'pair', split_axis=1, concat_axis=0, tiled=True)]
    gather x2 -> x1, local copies, waits for them, and re-layouts: 4.81 us -> 2 us  [per_device(): jnp.take(blocks, plan, axis=0, mode='clip')]
where the time goes in v3:
time: 244 us; the launch traced here: 242 us
  Pallas kernels  104 us (43%)
  waiting for transfers between devices  63.9 us (26%)
  matrix products  39.3 us (16%)
  starting transfers between devices  18.7 us (8%)
  other arithmetic  10.5 us (4%)
  local copies, waits for them, and re-layouts  5.34 us (2%)
    pallas_call x2, Pallas kernels, rows_sum(): pl.pallas_call(functools.partial(rows_sum_kernel, outer, inner), out_shap...  104 us
    ppermute x4, waiting for transfers between devices, from_behind(): return lax.ppermute(x, axis, pairs)  34.4 us
    all_to_all x1, waiting for transfers between devices, per_device(): lax.all_to_all(slots, 'pair', split_axis=0, concat_axis=0, tiled=True)  29.5 us
    dot_general x4, matrix products, turn(): jnp.dot(chain, first_iter, precision=fast, preferred_element_type=jnp.flo...  14.3 us
    dot_general x2, matrix products, turn(): jnp.dot(weighted, first_iter, precision=fast, preferred_element_type=jnp....  11.7 us
    ppermute x4, starting transfers between devices, from_behind(): return lax.ppermute(x, axis, pairs)  11.2 us
    all_to_all x1, starting transfers between devices, per_device(): lax.all_to_all(slots, 'pair', split_axis=0, concat_axis=0, tiled=True)  7.47 us
    dot_general x2, matrix products, turn(): jnp.dot(applied, scaled_gram, precision=fast, preferred_element_type=jnp....  7.11 us
  transfers between devices with their start and end apart: 5, of which 5 were waited for; matrix products, arithmetic and copies ran while one was open for 0% of the time, Pallas kernels for 0%

profile of v3, /device:TPU:97, one launch (start us, length us, event | category | flops | bytes accessed | tf_op | source)
XLA Modules:
  0.0 242.5 jit_solution(6051401118022626778)
XLA Ops:
  0.0 0.7 pad_clamp_fusion
  0.7 1.8 copy.6
  2.5 2.0 gather_fusion
  4.5 7.5 %all-to-all-start = ((f32[16,2,32,512]{3,2,1,0:T(8,128)}), f32[16,2,32,512]{3,2,1,0:T(8,128)S(1)}, u32[]{:S(2)}, u32[]{:S(2)}) async-start(f32[16,2,32,512]{3,2,1,0:T(8,128)} %bitcast.40), calls=%async_computation | async-start | bytes 4194304 | tf_op jit(solution)/shard_map/all_to_all | solution.py:289
  12.0 29.5 %all-to-all-done = f32[16,2,32,512]{3,2,1,0:T(8,128)S(1)} async-done(((f32[16,2,32,512]{3,2,1,0:T(8,128)}), f32[16,2,32,512]{3,2,1,0:T(8,128)S(1)}, u32[]{:S(2)}, u32[]{:S(2)}) %all-to-all-start) | async-done | bytes 2097184 | tf_op jit(solution)/shard_map/all_to_all | solution.py:289
  41.5 0.2 fusion.9
  41.6 0.1 pad_maximum_fusion.1
  41.8 199.3 %while.13 = (s32[]{:T(128)}, f32[512,1024]{1,0:T(8,128)S(1)}, pred[]{:T(512)}, pred[]{:T(512)}, s32[]{:T(128)}) while((s32[]{:T(128)}, f32[512,1024]{1,0:T(8,128)S(1)}, pred[]{:T(512)}, pred[]{:T(512)}, s32[]{:T(128)}) %tuple.40), condition=%wide.region_2.3_spmd, body=%wide.region_0.2_spmd.sunk | while | flops 15307767808 | bytes 103968984 | solution.py:315
  41.8 1.0 fusion.45
  42.8 1.0 select_reduce_fusion.2
  43.9 1.0 convolution_select_fusion.2
  44.9 1.6 select_maximum_fusion.2.payload
  46.5 54.7 %eval_jaxpr.4 = (f32[1024,1024]{1,0:T(8,128)}, f32[1024,1024]{1,0:T(8,128)}, f32[1,1024]{1,0:T(1,128)}, f32[1,1024]{1,0:T(1,128)}) custom-call(f32[1088,512]{1,0:T(8,128)} %select_maximum_fusion.2.payload), custom_call_target="tpu_custom_call" | custom-call | tf_op jit(solution)/shard_map/while/body/eval_jaxpr/pallas_call | solution.py:211
  101.2 0.0 copy-start.2
  101.2 5.9 %fusion.46 = f32[512,1024]{1,0:T(8,128)S(1)} fusion(f32[1024,1024]{1,0:T(8,128)} %get-tuple-element.124, f32[512,1024]{1,0:T(8,128)S(1)} %get-tuple-element.138, f32[1024]{0:T(1024)} %bitcast.47), kind=kOutput, calls=%fused_computation.5.clone.1 | convolution fusion | flops 3221749760 | bytes 8392704 | tf_op jit(solution)/shard_map/while/body/eval_jaxpr/dot_general | solution.py:300
  107.1 0.0 copy-done.2
  107.1 0.0 copy-start
  107.1 3.6 %fusion.47 = f32[512,1024]{1,0:T(8,128)S(1)} fusion(f32[512,1024]{1,0:T(8,128)S(1)} %fusion.46, f32[1024,1024]{1,0:T(8,128)S(1)} %copy-done.2), kind=kOutput, calls=%fused_computation.25.clone.1 | convolution fusion | flops 3221225472 | bytes 8388608 | tf_op jit(solution)/shard_map/while/body/eval_jaxpr/dot_general | solution.py:301
  110.7 0.0 copy-done
  110.7 0.0 copy-start.3
  110.7 3.6 %fusion.48 = f32[512,1024]{1,0:T(8,128)S(1)} fusion(f32[512,1024]{1,0:T(8,128)S(1)} %fusion.47, f32[1024,1024]{1,0:T(8,128)S(1)} %copy-done), kind=kOutput, calls=%fused_computation.26.clone.1 | convolution fusion | flops 3221225472 | bytes 8388608 | tf_op jit(solution)/shard_map/while/body/eval_jaxpr/dot_general | solution.py:302
  114.3 0.0 copy-done.3
  114.3 3.6 %subtract_multiply_fusion.2 = f32[512,1024]{1,0:T(8,128)S(1)} fusion(f32[512,1024]{1,0:T(8,128)S(1)} %fusion.46, f32[512,1024]{1,0:T(8,128)S(1)} %fusion.48, f32[1024,1024]{1,0:T(8,128)S(1)} %copy-done, f32[1024]{0:T(1024)S(1)} %bitcast.46), kind=kOutput, calls=%fused_computation.4.clone.1 | convolution fusion | flops 3222798336 | bytes 10489856 | tf_op jit(solution)/shard_map/while/body/eval_jaxpr/dot_general | solution.py:303
  117.9 1.2 slice_select_fusion.5
  119.1 2.4 collective-permute-start
  121.5 3.1 %collective-permute-start.1 = (f32[512,512]{1,0:T(8,128)S(1)}, f32[512,512]{1,0:T(8,128)}, u32[]{:S(2)}, u32[]{:S(2)}) collective-permute-start(f32[512,512]{1,0:T(8,128)S(1)} %get-tuple-element.129), channel_id=1, source_target_pairs={{8,0},{16,8},{24,16},{32,24},{40,32},{48,40},{56,48},{64,56},{72,6... | collective-permute-start | bytes 3145736 | tf_op jit(solution)/shard_map/while/body/eval_jaxpr/ppermute | solution.py:256
  124.6 8.9 %collective-permute-done = f32[512,512]{1,0:T(8,128)} collective-permute-done((f32[512,512]{1,0:T(8,128)}, f32[512,512]{1,0:T(8,128)}, u32[]{:S(2)}, u32[]{:S(2)}) %collective-permute-start) | collective-permute-done | bytes 1048608 | tf_op jit(solution)/shard_map/while/body/eval_jaxpr/ppermute | solution.py:256
  133.5 7.8 %collective-permute-done.1 = f32[512,512]{1,0:T(8,128)} collective-permute-done((f32[512,512]{1,0:T(8,128)S(1)}, f32[512,512]{1,0:T(8,128)}, u32[]{:S(2)}, u32[]{:S(2)}) %collective-permute-start.1) | collective-permute-done | bytes 1048608 | tf_op jit(solution)/shard_map/while/body/eval_jaxpr/ppermute | solution.py:256
  141.3 1.9 slice_select_fusion.6
  143.2 0.1 pad_maximum_fusion.3
  143.3 1.0 fusion.45
  144.4 1.0 select_reduce_fusion.2
  145.4 1.0 convolution_select_fusion.2
  146.4 1.6 select_maximum_fusion.2.payload
  148.1 49.7 %eval_jaxpr.4 = (f32[1024,1024]{1,0:T(8,128)}, f32[1024,1024]{1,0:T(8,128)}, f32[1,1024]{1,0:T(1,128)}, f32[1,1024]{1,0:T(1,128)}) custom-call(f32[1088,512]{1,0:T(8,128)} %select_maximum_fusion.2.payload), custom_call_target="tpu_custom_call" | custom-call | tf_op jit(solution)/shard_map/while/body/eval_jaxpr/pallas_call | solution.py:211
  197.8 5.9 %fusion.46 = f32[512,1024]{1,0:T(8,128)S(1)} fusion(f32[1024,1024]{1,0:T(8,128)} %get-tuple-element.124, f32[512,1024]{1,0:T(8,128)S(1)} %get-tuple-element.138, f32[1024]{0:T(1024)} %bitcast.47), kind=kOutput, calls=%fused_computation.5.clone.1 | convolution fusion | flops 3221749760 | bytes 8392704 | tf_op jit(solution)/shard_map/while/body/eval_jaxpr/dot_general | solution.py:300
  203.7 3.6 %fusion.47 = f32[512,1024]{1,0:T(8,128)S(1)} fusion(f32[512,1024]{1,0:T(8,128)S(1)} %fusion.46, f32[1024,1024]{1,0:T(8,128)S(1)} %copy-done.2), kind=kOutput, calls=%fused_computation.25.clone.1 | convolution fusion | flops 3221225472 | bytes 8388608 | tf_op jit(solution)/shard_map/while/body/eval_jaxpr/dot_general | solution.py:301
  207.3 3.6 %fusion.48 = f32[512,1024]{1,0:T(8,128)S(1)} fusion(f32[512,1024]{1,0:T(8,128)S(1)} %fusion.47, f32[1024,1024]{1,0:T(8,128)S(1)} %copy-done), kind=kOutput, calls=%fused_computation.26.clone.1 | convolution fusion | flops 3221225472 | bytes 8388608 | tf_op jit(solution)/shard_map/while/body/eval_jaxpr/dot_general | solution.py:302
  210.8 3.6 %subtract_multiply_fusion.2 = f32[512,1024]{1,0:T(8,128)S(1)} fusion(f32[512,1024]{1,0:T(8,128)S(1)} %fusion.46, f32[512,1024]{1,0:T(8,128)S(1)} %fusion.48, f32[1024,1024]{1,0:T(8,128)S(1)} %copy-done, f32[1024]{0:T(1024)S(1)} %bitcast.46), kind=kOutput, calls=%fused_computation.4.clone.1 | convolution fusion | flops 3222798336 | bytes 10489856 | tf_op jit(solution)/shard_map/while/body/eval_jaxpr/dot_general | solution.py:303
  214.4 1.2 slice_select_fusion.5
  215.6 3.6 %collective-permute-start = (f32[512,512]{1,0:T(8,128)}, f32[512,512]{1,0:T(8,128)}, u32[]{:S(2)}, u32[]{:S(2)}) collective-permute-start(f32[512,512]{1,0:T(8,128)} %get-tuple-element.128), channel_id=1, source_target_pairs={{0,8},{8,16},{16,24},{24,32},{32,40},{40,48},{48,56},{56,64},{64,7... | collective-permute-start | bytes 3145736 | tf_op jit(solution)/shard_map/while/body/eval_jaxpr/ppermute | solution.py:256
  219.3 2.2 collective-permute-start.1
  221.4 9.8 %collective-permute-done = f32[512,512]{1,0:T(8,128)} collective-permute-done((f32[512,512]{1,0:T(8,128)}, f32[512,512]{1,0:T(8,128)}, u32[]{:S(2)}, u32[]{:S(2)}) %collective-permute-start) | collective-permute-done | bytes 1048608 | tf_op jit(solution)/shard_map/while/body/eval_jaxpr/ppermute | solution.py:256
  231.3 7.8 %collective-permute-done.1 = f32[512,512]{1,0:T(8,128)} collective-permute-done((f32[512,512]{1,0:T(8,128)S(1)}, f32[512,512]{1,0:T(8,128)}, u32[]{:S(2)}, u32[]{:S(2)}) %collective-permute-start.1) | collective-permute-done | bytes 1048608 | tf_op jit(solution)/shard_map/while/body/eval_jaxpr/ppermute | solution.py:256
  239.1 1.9 slice_select_fusion.6
  241.0 0.1 pad_maximum_fusion.3
  241.1 0.0 copy-start.1
  241.2 1.3 copy-done.1
  (6 shorter events, 0.0 us)
Async XLA Ops:
  4.5 37.0 %all-to-all-start = ((f32[16,2,32,512]{3,2,1,0:T(8,128)}), f32[16,2,32,512]{3,2,1,0:T(8,128)S(1)}, u32[]{:S(2)}, u32[]{:S(2)}) async-start(f32[16,2,32,512]{3,2,1,0:T(8,128)} %bitcast.40), calls=%async_computation | async-start | bytes 4194304 | tf_op jit(solution)/shard_map/all_to_all | solution.py:289
  101.2 5.9 %copy-start.2 = (f32[1024,1024]{1,0:T(8,128)S(1)}, f32[1024,1024]{1,0:T(8,128)}, u32[]{:S(2)}) copy-start(f32[1024,1024]{1,0:T(8,128)} %get-tuple-element.126) | copy-start | bytes 12582916 | tf_op jit(solution)/shard_map/while
  107.1 3.6 %copy-start = (f32[1024,1024]{1,0:T(8,128)S(1)}, f32[1024,1024]{1,0:T(8,128)}, u32[]{:S(2)}) copy-start(f32[1024,1024]{1,0:T(8,128)} %get-tuple-element.124) | copy-start | bytes 12582916 | tf_op jit(solution)/shard_map/while
  110.7 3.6 %copy-start.3 = (f32[1,1024]{1,0:T(1,128)S(1)}, f32[1,1024]{1,0:T(1,128)}, u32[]{:S(2)}) copy-start(f32[1,1024]{1,0:T(1,128)} %get-tuple-element.127) | copy-start | bytes 12292 | tf_op jit(solution)/shard_map/while
  119.1 14.4 %collective-permute-start = (f32[512,512]{1,0:T(8,128)}, f32[512,512]{1,0:T(8,128)}, u32[]{:S(2)}, u32[]{:S(2)}) collective-permute-start(f32[512,512]{1,0:T(8,128)} %get-tuple-element.128), channel_id=1, source_target_pairs={{0,8},{8,16},{16,24},{24,32},{32,40},{40,48},{48,56},{56,64},{64,7... | collective-permute-start | bytes 3145736 | tf_op jit(solution)/shard_map/while/body/eval_jaxpr/ppermute | solution.py:256
  121.5 19.8 %collective-permute-start.1 = (f32[512,512]{1,0:T(8,128)S(1)}, f32[512,512]{1,0:T(8,128)}, u32[]{:S(2)}, u32[]{:S(2)}) collective-permute-start(f32[512,512]{1,0:T(8,128)S(1)} %get-tuple-element.129), channel_id=1, source_target_pairs={{8,0},{16,8},{24,16},{32,24},{40,32},{48,40},{56,48},{64,56},{72,6... | collective-permute-start | bytes 3145736 | tf_op jit(solution)/shard_map/while/body/eval_jaxpr/ppermute | solution.py:256
  197.8 5.9 %copy-start.2 = (f32[1024,1024]{1,0:T(8,128)S(1)}, f32[1024,1024]{1,0:T(8,128)}, u32[]{:S(2)}) copy-start(f32[1024,1024]{1,0:T(8,128)} %get-tuple-element.126) | copy-start | bytes 12582916 | tf_op jit(solution)/shard_map/while
  203.7 3.6 %copy-start = (f32[1024,1024]{1,0:T(8,128)S(1)}, f32[1024,1024]{1,0:T(8,128)}, u32[]{:S(2)}) copy-start(f32[1024,1024]{1,0:T(8,128)} %get-tuple-element.124) | copy-start | bytes 12582916 | tf_op jit(solution)/shard_map/while
  207.3 3.6 %copy-start.3 = (f32[1,1024]{1,0:T(1,128)S(1)}, f32[1,1024]{1,0:T(1,128)}, u32[]{:S(2)}) copy-start(f32[1,1024]{1,0:T(1,128)} %get-tuple-element.127) | copy-start | bytes 12292 | tf_op jit(solution)/shard_map/while
  215.6 15.6 %collective-permute-start = (f32[512,512]{1,0:T(8,128)}, f32[512,512]{1,0:T(8,128)}, u32[]{:S(2)}, u32[]{:S(2)}) collective-permute-start(f32[512,512]{1,0:T(8,128)} %get-tuple-element.128), channel_id=1, source_target_pairs={{0,8},{8,16},{16,24},{24,32},{32,40},{40,48},{48,56},{56,64},{64,7... | collective-permute-start | bytes 3145736 | tf_op jit(solution)/shard_map/while/body/eval_jaxpr/ppermute | solution.py:256
  219.3 19.8 %collective-permute-start.1 = (f32[512,512]{1,0:T(8,128)S(1)}, f32[512,512]{1,0:T(8,128)}, u32[]{:S(2)}, u32[]{:S(2)}) collective-permute-start(f32[512,512]{1,0:T(8,128)S(1)} %get-tuple-element.129), channel_id=1, source_target_pairs={{8,0},{16,8},{24,16},{32,24},{40,32},{48,40},{56,48},{64,56},{72,6... | collective-permute-start | bytes 3145736 | tf_op jit(solution)/shard_map/while/body/eval_jaxpr/ppermute | solution.py:256
  241.1 1.3 copy-start.1

commit v4 on v3

--- a/solution.py
+++ b/solution.py
@@ -60,7 +60,7 @@
     payload,
     scaled_out,
     first_out,
-    inverse_out,
+    weighted_out,
     factor_out,
     a_in,
     a_acc,
@@ -152,10 +152,10 @@
     for j in range(outer):
         for k in range(inner):
             out[pl.ds(j * b_half + k * b_chunk, b_chunk), cols_b] = b_all[j, k]
-    normalize_packed(out, scaled_out, first_out, inverse_out, factor_out)
-
-
-def normalize_packed(packed, scaled_out, first_out, inverse_out, factor_out):
+    normalize_packed(out, scaled_out, first_out, weighted_out, factor_out)
+
+
+def normalize_packed(packed, scaled_out, first_out, weighted_out, factor_out):
     width = packed.shape[1]
     row = lax.broadcasted_iota(jnp.int32, (width, width), 0)
     col = lax.broadcasted_iota(jnp.int32, (width, width), 1)
@@ -195,8 +195,8 @@
     first_out[near, far] = 0.5 * (0.0 - cross)
     first_out[far, near] = 0.5 * (0.0 - cross.T)
     first_out[far, far] = 0.5 * (three - lower)
-    inverse_out[:, near] = inv_upper_row
-    inverse_out[:, far] = inv_lower_row
+    weighted_out[near, :] = first_out[near, :] * inv_upper_col
+    weighted_out[far, :] = first_out[far, :] * inv_lower_col
     factor_out[:, near] = 0.5 * jnp.sqrt(upper_row) / jnp.sqrt(spread)
     factor_out[:, far] = 0.5 * jnp.sqrt(lower_row) / jnp.sqrt(spread)
 
@@ -213,7 +213,7 @@
         out_shape=(
             jax.ShapeDtypeStruct((2 * width, 2 * width), jnp.float32),
             jax.ShapeDtypeStruct((2 * width, 2 * width), jnp.float32),
-            jax.ShapeDtypeStruct((1, 2 * width), jnp.float32),
+            jax.ShapeDtypeStruct((2 * width, 2 * width), jnp.float32),
             jax.ShapeDtypeStruct((1, 2 * width), jnp.float32),
         ),
         in_specs=[pl.BlockSpec(memory_space=pltpu.VMEM)],
@@ -295,9 +295,8 @@
     def turn(turn_index, current):
         upper = current[:, :BLK]
         lower = current[:, BLK:]
-        scaled_gram, first_iter, inverse, factor = summed_gram(upper, lower, outer, inner)
-        weighted = current * inverse
-        applied = jnp.dot(weighted, first_iter, precision=fast, preferred_element_type=jnp.float32)
+        scaled_gram, first_iter, weighted_first, factor = summed_gram(upper, lower, outer, inner)
+        applied = jnp.dot(current, weighted_first, precision=fast, preferred_element_type=jnp.float32)
         chain = jnp.dot(applied, scaled_gram, precision=fast, preferred_element_type=jnp.float32)
         chain = jnp.dot(chain, first_iter, precision=fast, preferred_element_type=jnp.float32)
         chain = jnp.dot(chain, first_iter, precision=fast, preferred_element_type=jnp.float32)

time: 244 us -> 251 us (1.029)
  Pallas kernels: 104 us -> 108 us
    while x12 -> x14, local copies, waits for them, and re-layouts: 0.03 us -> 3.76 us  [the longest x2 3.73 us: per_device(): current = lax.fori_loop(0, STEPS, turn, current)]
    pallas_call x2, Pallas kernels: 104 us -> 108 us  [rows_sum(): pl.pallas_call(functools.partial(rows_sum_kernel, outer, inner), out_shap...]
where the time goes in v4:
time: 251 us; the launch traced here: 249 us
  Pallas kernels  108 us (43%)
  waiting for transfers between devices  63.7 us (25%)
  matrix products  38.8 us (15%)
  starting transfers between devices  18.8 us (7%)
  other arithmetic  11.7 us (5%)
  local copies, waits for them, and re-layouts  7.76 us (3%)
    pallas_call x2, Pallas kernels, rows_sum(): pl.pallas_call(functools.partial(rows_sum_kernel, outer, inner), out_shap...  108 us
    ppermute x4, waiting for transfers between devices, from_behind(): return lax.ppermute(x, axis, pairs)  34.2 us
    all_to_all x1, waiting for transfers between devices, per_device(): lax.all_to_all(slots, 'pair', split_axis=0, concat_axis=0, tiled=True)  29.5 us
    dot_general x4, matrix products, turn(): jnp.dot(chain, first_iter, precision=fast, preferred_element_type=jnp.flo...  14.6 us
    ppermute x4, starting transfers between devices, from_behind(): return lax.ppermute(x, axis, pairs)  11.3 us
    dot_general x2, matrix products, turn(): jnp.dot(current, weighted_first, precision=fast, preferred_element_type=j...  10.9 us
    all_to_all x1, starting transfers between devices, per_device(): lax.all_to_all(slots, 'pair', split_axis=0, concat_axis=0, tiled=True)  7.47 us
    dot_general x2, matrix products, turn(): jnp.dot(applied, scaled_gram, precision=fast, preferred_element_type=jnp....  7.14 us
  transfers between devices with their start and end apart: 5, of which 5 were waited for; matrix products, arithmetic and copies ran while one was open for 0% of the time, Pallas kernels for 0%

profile of v4, /device:TPU:97, one launch (start us, length us, event | category | flops | bytes accessed | tf_op | source)
XLA Modules:
  0.0 249.0 jit_solution(8566847975955713071)
XLA Ops:
  0.0 0.7 pad_clamp_fusion
  0.7 1.8 copy.15
  2.5 2.0 gather_fusion
  4.5 7.5 %all-to-all-start = ((f32[16,2,32,512]{3,2,1,0:T(8,128)}), f32[16,2,32,512]{3,2,1,0:T(8,128)S(1)}, u32[]{:S(2)}, u32[]{:S(2)}) async-start(f32[16,2,32,512]{3,2,1,0:T(8,128)} %bitcast.46), calls=%async_computation | async-start | bytes 4194304 | tf_op jit(solution)/shard_map/all_to_all | solution.py:289
  12.0 29.5 %all-to-all-done = f32[16,2,32,512]{3,2,1,0:T(8,128)S(1)} async-done(((f32[16,2,32,512]{3,2,1,0:T(8,128)}), f32[16,2,32,512]{3,2,1,0:T(8,128)S(1)}, u32[]{:S(2)}, u32[]{:S(2)}) %all-to-all-start) | async-done | bytes 2097184 | tf_op jit(solution)/shard_map/all_to_all | solution.py:289
  41.5 0.2 fusion.7
  41.6 1.5 pad_maximum_fusion.1
  43.1 1.9 copy.10
  45.0 202.1 %while.13 = (s32[]{:T(128)}, f32[512,1024]{0,1:T(8,128)S(1)}, pred[]{:T(512)}, pred[]{:T(512)}, s32[]{:T(128)}) while((s32[]{:T(128)}, f32[512,1024]{0,1:T(8,128)S(1)}, pred[]{:T(512)}, pred[]{:T(512)}, s32[]{:T(128)}) %tuple.42), condition=%wide.region_2.3_spmd, body=%wide.region_0.2_spmd.sunk | while | flops 15307243520 | bytes 103964888 | solution.py:314
  45.0 1.0 fusion.46
  46.1 1.0 select_reduce_fusion.2
  47.1 1.0 convolution_select_fusion.2
  48.2 1.6 select_maximum_fusion.2.payload
  49.7 56.5 %eval_jaxpr.4 = (f32[1024,1024]{1,0:T(8,128)}, f32[1024,1024]{1,0:T(8,128)}, f32[1024,1024]{1,0:T(8,128)}, f32[1,1024]{1,0:T(1,128)}) custom-call(f32[1088,512]{1,0:T(8,128)} %select_maximum_fusion.2.payload), custom_call_target="tpu_custom_call" | custom-call | tf_op jit(solution)/shard_map/while/body/eval_jaxpr/pallas_call | solution.py:211
  106.2 0.0 copy-start.1
  106.2 5.5 %fusion.47 = f32[1024,512]{1,0:T(8,128)S(1)} fusion(f32[1024,1024]{1,0:T(8,128)} %get-tuple-element.132, f32[512,1024]{0,1:T(8,128)S(1)} %get-tuple-element.146), kind=kOutput, calls=%fused_computation.23.clone.1 | convolution fusion | flops 3221225472 | bytes 8388608 | tf_op jit(solution)/shard_map/while/body/eval_jaxpr/dot_general | solution.py:299
  111.6 0.0 copy-done.1
  111.7 0.0 copy-start
  111.7 3.6 %fusion.48 = f32[512,1024]{1,0:T(8,128)S(1)} fusion(f32[1024,512]{1,0:T(8,128)S(1)} %fusion.47, f32[1024,1024]{1,0:T(8,128)S(1)} %copy-done.1), kind=kOutput, calls=%fused_computation.24.clone.1 | convolution fusion | flops 3221225472 | bytes 8388608 | tf_op jit(solution)/shard_map/while/body/eval_jaxpr/dot_general | solution.py:300
  115.2 0.0 copy-done
  115.3 0.0 copy-start.2
  115.3 3.6 %fusion.49 = f32[512,1024]{1,0:T(8,128)S(1)} fusion(f32[512,1024]{1,0:T(8,128)S(1)} %fusion.48, f32[1024,1024]{1,0:T(8,128)S(1)} %copy-done), kind=kOutput, calls=%fused_computation.25.clone.1 | convolution fusion | flops 3221225472 | bytes 8388608 | tf_op jit(solution)/shard_map/while/body/eval_jaxpr/dot_general | solution.py:301
  118.8 0.0 copy-done.2
  118.8 3.7 %fusion.50 = f32[512,1024]{0,1:T(8,128)S(1)} fusion(f32[1024,512]{1,0:T(8,128)S(1)} %fusion.47, f32[512,1024]{1,0:T(8,128)S(1)} %fusion.49, f32[1024,1024]{1,0:T(8,128)S(1)} %copy-done, f32[1024]{0:T(1024)S(1)} %bitcast.52), kind=kOutput, calls=%fused_computation.5.clone.1 | convolution fusion | flops 3222798336 | bytes 10489856 | tf_op jit(solution)/shard_map/while/body/eval_jaxpr/dot_general | solution.py:302
  122.6 1.2 slice_select_fusion.5
  123.8 2.3 collective-permute-start
  126.1 3.2 %collective-permute-start.1 = (f32[512,512]{0,1:T(8,128)S(1)}, f32[512,512]{0,1:T(8,128)}, u32[]{:S(2)}, u32[]{:S(2)}) collective-permute-start(f32[512,512]{0,1:T(8,128)S(1)} %get-tuple-element.137), channel_id=1, source_target_pairs={{8,0},{16,8},{24,16},{32,24},{40,32},{48,40},{56,48},{64,56},{72,6... | collective-permute-start | bytes 3145736 | tf_op jit(solution)/shard_map/while/body/eval_jaxpr/ppermute | solution.py:256
  129.2 8.9 %collective-permute-done = f32[512,512]{0,1:T(8,128)} collective-permute-done((f32[512,512]{0,1:T(8,128)}, f32[512,512]{0,1:T(8,128)}, u32[]{:S(2)}, u32[]{:S(2)}) %collective-permute-start) | collective-permute-done | bytes 1048608 | tf_op jit(solution)/shard_map/while/body/eval_jaxpr/ppermute | solution.py:256
  138.1 7.8 %collective-permute-done.1 = f32[512,512]{0,1:T(8,128)} collective-permute-done((f32[512,512]{0,1:T(8,128)S(1)}, f32[512,512]{0,1:T(8,128)}, u32[]{:S(2)}, u32[]{:S(2)}) %collective-permute-start.1) | collective-permute-done | bytes 1048608 | tf_op jit(solution)/shard_map/while/body/eval_jaxpr/ppermute | solution.py:256
  145.9 1.9 slice_select_fusion.6
  147.8 0.2 pad_maximum_fusion.3
  148.0 1.0 fusion.46
  149.0 1.0 select_reduce_fusion.2
  150.1 1.0 convolution_select_fusion.2
  151.1 1.6 select_maximum_fusion.2.payload
  152.7 51.4 %eval_jaxpr.4 = (f32[1024,1024]{1,0:T(8,128)}, f32[1024,1024]{1,0:T(8,128)}, f32[1024,1024]{1,0:T(8,128)}, f32[1,1024]{1,0:T(1,128)}) custom-call(f32[1088,512]{1,0:T(8,128)} %select_maximum_fusion.2.payload), custom_call_target="tpu_custom_call" | custom-call | tf_op jit(solution)/shard_map/while/body/eval_jaxpr/pallas_call | solution.py:211
  204.1 5.4 %fusion.47 = f32[1024,512]{1,0:T(8,128)S(1)} fusion(f32[1024,1024]{1,0:T(8,128)} %get-tuple-element.132, f32[512,1024]{0,1:T(8,128)S(1)} %get-tuple-element.146), kind=kOutput, calls=%fused_computation.23.clone.1 | convolution fusion | flops 3221225472 | bytes 8388608 | tf_op jit(solution)/shard_map/while/body/eval_jaxpr/dot_general | solution.py:299
  209.6 3.6 %fusion.48 = f32[512,1024]{1,0:T(8,128)S(1)} fusion(f32[1024,512]{1,0:T(8,128)S(1)} %fusion.47, f32[1024,1024]{1,0:T(8,128)S(1)} %copy-done.1), kind=kOutput, calls=%fused_computation.24.clone.1 | convolution fusion | flops 3221225472 | bytes 8388608 | tf_op jit(solution)/shard_map/while/body/eval_jaxpr/dot_general | solution.py:300
  213.2 3.6 %fusion.49 = f32[512,1024]{1,0:T(8,128)S(1)} fusion(f32[512,1024]{1,0:T(8,128)S(1)} %fusion.48, f32[1024,1024]{1,0:T(8,128)S(1)} %copy-done), kind=kOutput, calls=%fused_computation.25.clone.1 | convolution fusion | flops 3221225472 | bytes 8388608 | tf_op jit(solution)/shard_map/while/body/eval_jaxpr/dot_general | solution.py:301
  216.8 3.7 %fusion.50 = f32[512,1024]{0,1:T(8,128)S(1)} fusion(f32[1024,512]{1,0:T(8,128)S(1)} %fusion.47, f32[512,1024]{1,0:T(8,128)S(1)} %fusion.49, f32[1024,1024]{1,0:T(8,128)S(1)} %copy-done, f32[1024]{0:T(1024)S(1)} %bitcast.52), kind=kOutput, calls=%fused_computation.5.clone.1 | convolution fusion | flops 3222798336 | bytes 10489856 | tf_op jit(solution)/shard_map/while/body/eval_jaxpr/dot_general | solution.py:302
  220.5 1.2 slice_select_fusion.5
  221.7 3.5 %collective-permute-start = (f32[512,512]{0,1:T(8,128)}, f32[512,512]{0,1:T(8,128)}, u32[]{:S(2)}, u32[]{:S(2)}) collective-permute-start(f32[512,512]{0,1:T(8,128)} %get-tuple-element.136), channel_id=1, source_target_pairs={{0,8},{8,16},{16,24},{24,32},{32,40},{40,48},{48,56},{56,64},{64,7... | collective-permute-start | bytes 3145736 | tf_op jit(solution)/shard_map/while/body/eval_jaxpr/ppermute | solution.py:256
  225.2 2.3 collective-permute-start.1
  227.6 9.7 %collective-permute-done = f32[512,512]{0,1:T(8,128)} collective-permute-done((f32[512,512]{0,1:T(8,128)}, f32[512,512]{0,1:T(8,128)}, u32[]{:S(2)}, u32[]{:S(2)}) %collective-permute-start) | collective-permute-done | bytes 1048608 | tf_op jit(solution)/shard_map/while/body/eval_jaxpr/ppermute | solution.py:256
  237.3 7.8 %collective-permute-done.1 = f32[512,512]{0,1:T(8,128)} collective-permute-done((f32[512,512]{0,1:T(8,128)S(1)}, f32[512,512]{0,1:T(8,128)}, u32[]{:S(2)}, u32[]{:S(2)}) %collective-permute-start.1) | collective-permute-done | bytes 1048608 | tf_op jit(solution)/shard_map/while/body/eval_jaxpr/ppermute | solution.py:256
  245.1 1.9 slice_select_fusion.6
  247.0 0.2 pad_maximum_fusion.3
  247.1 1.8 copy.11
  (6 shorter events, 0.0 us)
Async XLA Ops:
  4.5 37.0 %all-to-all-start = ((f32[16,2,32,512]{3,2,1,0:T(8,128)}), f32[16,2,32,512]{3,2,1,0:T(8,128)S(1)}, u32[]{:S(2)}, u32[]{:S(2)}) async-start(f32[16,2,32,512]{3,2,1,0:T(8,128)} %bitcast.46), calls=%async_computation | async-start | bytes 4194304 | tf_op jit(solution)/shard_map/all_to_all | solution.py:289
  106.2 5.5 %copy-start.1 = (f32[1024,1024]{1,0:T(8,128)S(1)}, f32[1024,1024]{1,0:T(8,128)}, u32[]{:S(2)}) copy-start(f32[1024,1024]{1,0:T(8,128)} %get-tuple-element.133) | copy-start | bytes 12582916 | tf_op jit(solution)/shard_map/while
  111.7 3.6 %copy-start = (f32[1024,1024]{1,0:T(8,128)S(1)}, f32[1024,1024]{1,0:T(8,128)}, u32[]{:S(2)}) copy-start(f32[1024,1024]{1,0:T(8,128)} %get-tuple-element.134) | copy-start | bytes 12582916 | tf_op jit(solution)/shard_map/while
  115.3 3.6 %copy-start.2 = (f32[1,1024]{1,0:T(1,128)S(1)}, f32[1,1024]{1,0:T(1,128)}, u32[]{:S(2)}) copy-start(f32[1,1024]{1,0:T(1,128)} %get-tuple-element.135) | copy-start | bytes 12292 | tf_op jit(solution)/shard_map/while
  123.8 14.3 %collective-permute-start = (f32[512,512]{0,1:T(8,128)}, f32[512,512]{0,1:T(8,128)}, u32[]{:S(2)}, u32[]{:S(2)}) collective-permute-start(f32[512,512]{0,1:T(8,128)} %get-tuple-element.136), channel_id=1, source_target_pairs={{0,8},{8,16},{16,24},{24,32},{32,40},{40,48},{48,56},{56,64},{64,7... | collective-permute-start | bytes 3145736 | tf_op jit(solution)/shard_map/while/body/eval_jaxpr/ppermute | solution.py:256
  126.1 19.8 %collective-permute-start.1 = (f32[512,512]{0,1:T(8,128)S(1)}, f32[512,512]{0,1:T(8,128)}, u32[]{:S(2)}, u32[]{:S(2)}) collective-permute-start(f32[512,512]{0,1:T(8,128)S(1)} %get-tuple-element.137), channel_id=1, source_target_pairs={{8,0},{16,8},{24,16},{32,24},{40,32},{48,40},{56,48},{64,56},{72,6... | collective-permute-start | bytes 3145736 | tf_op jit(solution)/shard_map/while/body/eval_jaxpr/ppermute | solution.py:256
  204.1 5.5 %copy-start.1 = (f32[1024,1024]{1,0:T(8,128)S(1)}, f32[1024,1024]{1,0:T(8,128)}, u32[]{:S(2)}) copy-start(f32[1024,1024]{1,0:T(8,128)} %get-tuple-element.133) | copy-start | bytes 12582916 | tf_op jit(solution)/shard_map/while
  209.6 3.6 %copy-start = (f32[1024,1024]{1,0:T(8,128)S(1)}, f32[1024,1024]{1,0:T(8,128)}, u32[]{:S(2)}) copy-start(f32[1024,1024]{1,0:T(8,128)} %get-tuple-element.134) | copy-start | bytes 12582916 | tf_op jit(solution)/shard_map/while
  213.2 3.6 %copy-start.2 = (f32[1,1024]{1,0:T(1,128)S(1)}, f32[1,1024]{1,0:T(1,128)}, u32[]{:S(2)}) copy-start(f32[1,1024]{1,0:T(1,128)} %get-tuple-element.135) | copy-start | bytes 12292 | tf_op jit(solution)/shard_map/while
  221.7 15.6 %collective-permute-start = (f32[512,512]{0,1:T(8,128)}, f32[512,512]{0,1:T(8,128)}, u32[]{:S(2)}, u32[]{:S(2)}) collective-permute-start(f32[512,512]{0,1:T(8,128)} %get-tuple-element.136), channel_id=1, source_target_pairs={{0,8},{8,16},{16,24},{24,32},{32,40},{40,48},{48,56},{56,64},{64,7... | collective-permute-start | bytes 3145736 | tf_op jit(solution)/shard_map/while/body/eval_jaxpr/ppermute | solution.py:256
  225.2 19.8 %collective-permute-start.1 = (f32[512,512]{0,1:T(8,128)S(1)}, f32[512,512]{0,1:T(8,128)}, u32[]{:S(2)}, u32[]{:S(2)}) collective-permute-start(f32[512,512]{0,1:T(8,128)S(1)} %get-tuple-element.137), channel_id=1, source_target_pairs={{8,0},{16,8},{24,16},{32,24},{40,32},{48,40},{56,48},{64,56},{72,6... | collective-permute-start | bytes 3145736 | tf_op jit(solution)/shard_map/while/body/eval_jaxpr/ppermute | solution.py:256

commit v5 on v3

--- a/solution.py
+++ b/solution.py
@@ -238,6 +238,94 @@
     )(v)
 
 
+def rotate_kernel(count, current, out, landed, sends, recvs):
+    me = lax.axis_index("pair")
+    me_y = lax.axis_index("ylo")
+    me_x = lax.axis_index("x")
+    half = current.shape[1] // 2
+    upper_cols, lower_cols = pl.ds(0, half), pl.ds(half, half)
+    following = ((me + 1) % count, me_y, me_x)
+    preceding = ((me + count - 1) % count, me_y, me_x)
+    barrier = pltpu.get_barrier_semaphore()
+
+    @pl.when(me < count - 1)
+    def _():
+        pl.semaphore_signal(barrier, inc=1, device_id=following, device_id_type=MESH)
+
+    @pl.when(me > 0)
+    def _():
+        pl.semaphore_signal(barrier, inc=1, device_id=preceding, device_id_type=MESH)
+
+    @pl.when(jnp.logical_and(me > 0, me < count - 1))
+    def _():
+        pl.semaphore_wait(barrier, 2)
+
+    @pl.when(jnp.logical_or(me == 0, me == count - 1))
+    def _():
+        pl.semaphore_wait(barrier, 1)
+
+    start = pl.multiple_of(jnp.where(me == 0, half, 0), 128)
+    upward = pltpu.make_async_remote_copy(
+        src_ref=current.at[:, pl.ds(start, half)],
+        dst_ref=landed.at[:, upper_cols],
+        send_sem=sends.at[0],
+        recv_sem=recvs.at[0],
+        device_id=following,
+        device_id_type=MESH,
+    )
+    downward = pltpu.make_async_remote_copy(
+        src_ref=current.at[:, lower_cols],
+        dst_ref=landed.at[:, lower_cols],
+        send_sem=sends.at[1],
+        recv_sem=recvs.at[1],
+        device_id=preceding,
+        device_id_type=MESH,
+    )
+
+    @pl.when(me < count - 1)
+    def _():
+        upward.start()
+
+    @pl.when(me > 0)
+    def _():
+        downward.start()
+
+    @pl.when(me == 0)
+    def _():
+        landed[:, upper_cols] = current[:, upper_cols]
+
+    @pl.when(me == count - 1)
+    def _():
+        landed[:, lower_cols] = current[:, upper_cols]
+
+    @pl.when(me < count - 1)
+    def _():
+        upward.wait_send()
+        downward.wait_recv()
+
+    @pl.when(me > 0)
+    def _():
+        downward.wait_send()
+        upward.wait_recv()
+
+    out[...] = landed[...]
+
+
+def rotate(current, count):
+    return pl.pallas_call(
+        functools.partial(rotate_kernel, count),
+        out_shape=jax.ShapeDtypeStruct(current.shape, current.dtype),
+        in_specs=[pl.BlockSpec(memory_space=pltpu.VMEM)],
+        out_specs=pl.BlockSpec(memory_space=pltpu.VMEM),
+        scratch_shapes=[
+            pltpu.VMEM(current.shape, jnp.float32),
+            pltpu.SemaphoreType.DMA((2,)),
+            pltpu.SemaphoreType.DMA((2,)),
+        ],
+        compiler_params=pltpu.CompilerParams(collective_id=2, has_side_effects=True),
+    )(current)
+
+
 def summed_gram(upper, lower, outer, inner):
     width = upper.shape[1]
     row = lax.broadcasted_iota(jnp.int32, (width, width), 0)
@@ -302,15 +390,7 @@
         chain = jnp.dot(chain, first_iter, precision=fast, preferred_element_type=jnp.float32)
         chain = jnp.dot(chain, first_iter, precision=fast, preferred_element_type=jnp.float32)
         current = (3.0 * applied - chain) * factor
-        upper = current[:, :BLK]
-        lower = current[:, BLK:]
-        outgoing = jnp.where(pair_index == 0, lower, upper)
-        arrived_up = from_behind(outgoing, "pair", 1)
-        arrived_down = from_behind(lower, "pair", -1)
-        new_upper = jnp.where(pair_index == 0, upper, arrived_up)
-        new_lower = jnp.where(pair_index == pair_count - 1, upper, arrived_down)
-        current = jnp.concatenate([new_upper, new_lower], axis=1)
-        return current
+        return rotate(current, pair_count)
 
     current = lax.fori_loop(0, STEPS, turn, current)
     return current

time: 244 us -> 235 us (0.963)
  Pallas kernels: 104 us -> 146 us
  waiting for transfers between devices: 63.9 us -> 29.5 us
  starting transfers between devices: 18.7 us -> 7.47 us
  other arithmetic: 10.5 us -> 3.99 us
  matrix products: 39.3 us -> 41.9 us
    pallas_call x0 -> x2, Pallas kernels: none -> 39.2 us  [rotate(): pl.pallas_call(functools.partial(rotate_kernel, count), out_shape=jax.Sha...]
    ppermute x4 -> x0, waiting for transfers between devices: 34.4 us -> none  [from_behind(): return lax.ppermute(x, axis, pairs)]
    ppermute x4 -> x0, starting transfers between devices: 11.2 us -> none  [from_behind(): return lax.ppermute(x, axis, pairs)]
    select_n x4 -> x0, other arithmetic: 6.24 us -> none  [the longest x2 3.79 us: turn(): new_upper = jnp.where(pair_index == 0, upper, arrived_up)]
    pallas_call x2, Pallas kernels: 104 us -> 107 us  [rows_sum(): pl.pallas_call(functools.partial(rows_sum_kernel, outer, inner), out_shap...]
    dot_general x4, matrix products: 14.3 us -> 16.9 us  [turn(): jnp.dot(chain, first_iter, precision=fast, preferred_element_type=jnp.flo...]
  transfers between devices with their start and end apart: 5 -> 1, of which waited for: 5 -> 1; matrix products, arithmetic and copies ran while one was open for 0% -> 0% of each run, Pallas kernels for 0% -> 0%
where the time goes in v5:
time: 235 us
  Pallas kernels  146 us (62%)
  matrix products  41.9 us (18%)
  waiting for transfers between devices  29.5 us (13%)
  starting transfers between devices  7.47 us (3%)
  local copies, waits for them, and re-layouts  5.34 us (2%)
  other arithmetic  3.99 us (2%)
    pallas_call x2, Pallas kernels, rows_sum(): pl.pallas_call(functools.partial(rows_sum_kernel, outer, inner), out_shap...  107 us
    pallas_call x2, Pallas kernels, rotate(): pl.pallas_call(functools.partial(rotate_kernel, count), out_shape=jax.Sha...  39.2 us
    all_to_all x1, waiting for transfers between devices, per_device(): lax.all_to_all(slots, 'pair', split_axis=0, concat_axis=0, tiled=True)  29.5 us
    dot_general x4, matrix products, turn(): jnp.dot(chain, first_iter, precision=fast, preferred_element_type=jnp.flo...  16.9 us
    dot_general x2, matrix products, turn(): jnp.dot(weighted, first_iter, precision=fast, preferred_element_type=jnp....  11.7 us
    all_to_all x1, starting transfers between devices, per_device(): lax.all_to_all(slots, 'pair', split_axis=0, concat_axis=0, tiled=True)  7.47 us
    dot_general x2, matrix products, turn(): jnp.dot(applied, scaled_gram, precision=fast, preferred_element_type=jnp....  7.11 us
    dot_general x6, matrix products, inner_gram(): lax.dot_general(left, right, (((0,), (0,)), ((), ())), precision=fast, pr...  6.18 us
  transfers between devices with their start and end apart: 1, of which 1 were waited for; matrix products, arithmetic and copies ran while one was open for 0% of the time, Pallas kernels for 0%

profile of v5, /device:TPU:97, one launch (start us, length us, event | category | flops | bytes accessed | tf_op | source)
XLA Modules:
  0.0 234.9 jit_solution(6931112789536007236)
XLA Ops:
  0.0 0.7 pad_clamp_fusion
  0.7 1.8 copy.6
  2.5 2.0 gather_fusion
  4.5 7.5 %all-to-all-start = ((f32[16,2,32,512]{3,2,1,0:T(8,128)}), f32[16,2,32,512]{3,2,1,0:T(8,128)S(1)}, u32[]{:S(2)}, u32[]{:S(2)}) async-start(f32[16,2,32,512]{3,2,1,0:T(8,128)} %bitcast.40), calls=%async_computation | async-start | bytes 4194304 | tf_op jit(solution)/shard_map/all_to_all | solution.py:377
  12.0 29.5 %all-to-all-done = f32[16,2,32,512]{3,2,1,0:T(8,128)S(1)} async-done(((f32[16,2,32,512]{3,2,1,0:T(8,128)}), f32[16,2,32,512]{3,2,1,0:T(8,128)S(1)}, u32[]{:S(2)}, u32[]{:S(2)}) %all-to-all-start) | async-done | bytes 2097184 | tf_op jit(solution)/shard_map/all_to_all | solution.py:377
  41.5 0.2 fusion.9
  41.6 0.1 pad_maximum_fusion
  41.8 191.8 %while.11 = (s32[]{:T(128)}, f32[512,1024]{1,0:T(8,128)S(1)}, s32[]{:T(128)}) while((s32[]{:T(128)}, f32[512,1024]{1,0:T(8,128)S(1)}, s32[]{:T(128)}) %tuple.26), condition=%wide.region_2.3_spmd, body=%wide.region_0.2_spmd.sunk | while | flops 15306457088 | bytes 81948792 | solution.py:395
  41.8 1.0 fusion.45
  42.8 1.0 select_reduce_fusion.2
  43.9 1.0 convolution_select_fusion.2
  44.9 1.6 select_maximum_fusion.2.payload
  46.5 54.7 %eval_jaxpr.2 = (f32[1024,1024]{1,0:T(8,128)}, f32[1024,1024]{1,0:T(8,128)}, f32[1,1024]{1,0:T(1,128)}, f32[1,1024]{1,0:T(1,128)}) custom-call(f32[1088,512]{1,0:T(8,128)} %select_maximum_fusion.2.payload), custom_call_target="tpu_custom_call" | custom-call | tf_op jit(solution)/shard_map/while/body/eval_jaxpr/pallas_call | solution.py:211
  101.2 0.0 copy-start.1
  101.2 5.9 %fusion.46 = f32[512,1024]{1,0:T(8,128)S(1)} fusion(f32[1024,1024]{1,0:T(8,128)} %get-tuple-element.63, f32[512,1024]{1,0:T(8,128)S(1)} %get-tuple-element.71, f32[1024]{0:T(1024)} %bitcast.47), kind=kOutput, calls=%fused_computation.4.clone.1 | convolution fusion | flops 3221749760 | bytes 8392704 | tf_op jit(solution)/shard_map/while/body/eval_jaxpr/dot_general | solution.py:388
  107.1 0.0 copy-done.1
  107.1 0.0 copy-start
  107.1 3.6 %fusion.47 = f32[512,1024]{1,0:T(8,128)S(1)} fusion(f32[512,1024]{1,0:T(8,128)S(1)} %fusion.46, f32[1024,1024]{1,0:T(8,128)S(1)} %copy-done.1), kind=kOutput, calls=%fused_computation.21.clone.1 | convolution fusion | flops 3221225472 | bytes 8388608 | tf_op jit(solution)/shard_map/while/body/eval_jaxpr/dot_general | solution.py:389
  110.7 0.0 copy-done
  110.7 0.0 copy-start.2
  110.7 3.6 %fusion.48 = f32[512,1024]{1,0:T(8,128)S(1)} fusion(f32[512,1024]{1,0:T(8,128)S(1)} %fusion.47, f32[1024,1024]{1,0:T(8,128)S(1)} %copy-done), kind=kOutput, calls=%fused_computation.22.clone.1 | convolution fusion | flops 3221225472 | bytes 8388608 | tf_op jit(solution)/shard_map/while/body/eval_jaxpr/dot_general | solution.py:390
  114.2 0.0 copy-done.2
  114.3 4.9 %subtract_multiply_fusion.2.current = f32[512,1024]{1,0:T(8,128)} fusion(f32[512,1024]{1,0:T(8,128)S(1)} %fusion.46, f32[512,1024]{1,0:T(8,128)S(1)} %fusion.48, f32[1024,1024]{1,0:T(8,128)S(1)} %copy-done, f32[1024]{0:T(1024)S(1)} %bitcast.46), kind=kOutput, calls=%fused_computation.3.clone.1 | convolution fusion | flops 3222798336 | bytes 10489856 | tf_op jit(solution)/shard_map/while/body/eval_jaxpr/dot_general | solution.py:391
  119.1 19.6 %eval_jaxpr.3 = f32[512,1024]{1,0:T(8,128)S(1)} custom-call(f32[512,1024]{1,0:T(8,128)} %subtract_multiply_fusion.2.current), custom_call_target="tpu_custom_call" | custom-call | tf_op jit(solution)/shard_map/while/body/eval_jaxpr/pallas_call | solution.py:315
  138.8 1.0 fusion.45
  139.8 1.0 select_reduce_fusion.2
  140.8 1.0 convolution_select_fusion.2
  141.9 1.6 select_maximum_fusion.2.payload
  143.5 52.6 %eval_jaxpr.2 = (f32[1024,1024]{1,0:T(8,128)}, f32[1024,1024]{1,0:T(8,128)}, f32[1,1024]{1,0:T(1,128)}, f32[1,1024]{1,0:T(1,128)}) custom-call(f32[1088,512]{1,0:T(8,128)} %select_maximum_fusion.2.payload), custom_call_target="tpu_custom_call" | custom-call | tf_op jit(solution)/shard_map/while/body/eval_jaxpr/pallas_call | solution.py:211
  196.0 0.0 copy-start.1
  196.0 5.9 %fusion.46 = f32[512,1024]{1,0:T(8,128)S(1)} fusion(f32[1024,1024]{1,0:T(8,128)} %get-tuple-element.63, f32[512,1024]{1,0:T(8,128)S(1)} %get-tuple-element.71, f32[1024]{0:T(1024)} %bitcast.47), kind=kOutput, calls=%fused_computation.4.clone.1 | convolution fusion | flops 3221749760 | bytes 8392704 | tf_op jit(solution)/shard_map/while/body/eval_jaxpr/dot_general | solution.py:388
  201.9 0.0 copy-done.1
  201.9 0.0 copy-start
  201.9 3.6 %fusion.47 = f32[512,1024]{1,0:T(8,128)S(1)} fusion(f32[512,1024]{1,0:T(8,128)S(1)} %fusion.46, f32[1024,1024]{1,0:T(8,128)S(1)} %copy-done.1), kind=kOutput, calls=%fused_computation.21.clone.1 | convolution fusion | flops 3221225472 | bytes 8388608 | tf_op jit(solution)/shard_map/while/body/eval_jaxpr/dot_general | solution.py:389
  205.5 0.0 copy-done
  205.5 0.0 copy-start.2
  205.5 3.6 %fusion.48 = f32[512,1024]{1,0:T(8,128)S(1)} fusion(f32[512,1024]{1,0:T(8,128)S(1)} %fusion.47, f32[1024,1024]{1,0:T(8,128)S(1)} %copy-done), kind=kOutput, calls=%fused_computation.22.clone.1 | convolution fusion | flops 3221225472 | bytes 8388608 | tf_op jit(solution)/shard_map/while/body/eval_jaxpr/dot_general | solution.py:390
  209.1 0.0 copy-done.2
  209.1 4.9 %subtract_multiply_fusion.2.current = f32[512,1024]{1,0:T(8,128)} fusion(f32[512,1024]{1,0:T(8,128)S(1)} %fusion.46, f32[512,1024]{1,0:T(8,128)S(1)} %fusion.48, f32[1024,1024]{1,0:T(8,128)S(1)} %copy-done, f32[1024]{0:T(1024)S(1)} %bitcast.46), kind=kOutput, calls=%fused_computation.3.clone.1 | convolution fusion | flops 3222798336 | bytes 10489856 | tf_op jit(solution)/shard_map/while/body/eval_jaxpr/dot_general | solution.py:391
  214.0 19.6 %eval_jaxpr.3 = f32[512,1024]{1,0:T(8,128)S(1)} custom-call(f32[512,1024]{1,0:T(8,128)} %subtract_multiply_fusion.2.current), custom_call_target="tpu_custom_call" | custom-call | tf_op jit(solution)/shard_map/while/body/eval_jaxpr/pallas_call | solution.py:315
  233.6 1.3 copy.16
Async XLA Ops:
  4.5 37.0 %all-to-all-start = ((f32[16,2,32,512]{3,2,1,0:T(8,128)}), f32[16,2,32,512]{3,2,1,0:T(8,128)S(1)}, u32[]{:S(2)}, u32[]{:S(2)}) async-start(f32[16,2,32,512]{3,2,1,0:T(8,128)} %bitcast.40), calls=%async_computation | async-start | bytes 4194304 | tf_op jit(solution)/shard_map/all_to_all | solution.py:377
  101.2 5.9 %copy-start.1 = (f32[1024,1024]{1,0:T(8,128)S(1)}, f32[1024,1024]{1,0:T(8,128)}, u32[]{:S(2)}) copy-start(f32[1024,1024]{1,0:T(8,128)} %get-tuple-element.65) | copy-start | bytes 12582916 | tf_op jit(solution)/shard_map/while
  107.1 3.6 %copy-start = (f32[1024,1024]{1,0:T(8,128)S(1)}, f32[1024,1024]{1,0:T(8,128)}, u32[]{:S(2)}) copy-start(f32[1024,1024]{1,0:T(8,128)} %get-tuple-element.63) | copy-start | bytes 12582916 | tf_op jit(solution)/shard_map/while
  110.7 3.6 %copy-start.2 = (f32[1,1024]{1,0:T(1,128)S(1)}, f32[1,1024]{1,0:T(1,128)}, u32[]{:S(2)}) copy-start(f32[1,1024]{1,0:T(1,128)} %get-tuple-element.66) | copy-start | bytes 12292 | tf_op jit(solution)/shard_map/while
  196.0 5.9 %copy-start.1 = (f32[1024,1024]{1,0:T(8,128)S(1)}, f32[1024,1024]{1,0:T(8,128)}, u32[]{:S(2)}) copy-start(f32[1024,1024]{1,0:T(8,128)} %get-tuple-element.65) | copy-start | bytes 12582916 | tf_op jit(solution)/shard_map/while
  201.9 3.6 %copy-start = (f32[1024,1024]{1,0:T(8,128)S(1)}, f32[1024,1024]{1,0:T(8,128)}, u32[]{:S(2)}) copy-start(f32[1024,1024]{1,0:T(8,128)} %get-tuple-element.63) | copy-start | bytes 12582916 | tf_op jit(solution)/shard_map/while
  205.5 3.6 %copy-start.2 = (f32[1,1024]{1,0:T(1,128)S(1)}, f32[1,1024]{1,0:T(1,128)}, u32[]{:S(2)}) copy-start(f32[1,1024]{1,0:T(1,128)} %get-tuple-element.66) | copy-start | bytes 12292 | tf_op jit(solution)/shard_map/while

commit v6 on v5

--- a/solution.py
+++ b/solution.py
@@ -265,30 +265,41 @@
         pl.semaphore_wait(barrier, 1)
 
     start = pl.multiple_of(jnp.where(me == 0, half, 0), 128)
-    upward = pltpu.make_async_remote_copy(
-        src_ref=current.at[:, pl.ds(start, half)],
-        dst_ref=landed.at[:, upper_cols],
-        send_sem=sends.at[0],
-        recv_sem=recvs.at[0],
-        device_id=following,
-        device_id_type=MESH,
-    )
-    downward = pltpu.make_async_remote_copy(
-        src_ref=current.at[:, lower_cols],
-        dst_ref=landed.at[:, lower_cols],
-        send_sem=sends.at[1],
-        recv_sem=recvs.at[1],
-        device_id=preceding,
-        device_id_type=MESH,
-    )
+    pieces = 4
+    rows = current.shape[0] // pieces
+    upward, downward = [], []
+    for k in range(pieces):
+        band = pl.ds(k * rows, rows)
+        upward.append(
+            pltpu.make_async_remote_copy(
+                src_ref=current.at[band, pl.ds(start, half)],
+                dst_ref=landed.at[band, upper_cols],
+                send_sem=sends.at[k],
+                recv_sem=recvs.at[k],
+                device_id=following,
+                device_id_type=MESH,
+            )
+        )
+        downward.append(
+            pltpu.make_async_remote_copy(
+                src_ref=current.at[band, lower_cols],
+                dst_ref=landed.at[band, lower_cols],
+                send_sem=sends.at[pieces + k],
+                recv_sem=recvs.at[pieces + k],
+                device_id=preceding,
+                device_id_type=MESH,
+            )
+        )
 
     @pl.when(me < count - 1)
     def _():
-        upward.start()
+        for copy in upward:
+            copy.start()
 
     @pl.when(me > 0)
     def _():
-        downward.start()
+        for copy in downward:
+            copy.start()
 
     @pl.when(me == 0)
     def _():
@@ -300,13 +311,17 @@
 
     @pl.when(me < count - 1)
     def _():
-        upward.wait_send()
-        downward.wait_recv()
+        for copy in upward:
+            copy.wait_send()
+        for copy in downward:
+            copy.wait_recv()
 
     @pl.when(me > 0)
     def _():
-        downward.wait_send()
-        upward.wait_recv()
+        for copy in downward:
+            copy.wait_send()
+        for copy in upward:
+            copy.wait_recv()
 
     out[...] = landed[...]
 
@@ -319,8 +334,8 @@
         out_specs=pl.BlockSpec(memory_space=pltpu.VMEM),
         scratch_shapes=[
             pltpu.VMEM(current.shape, jnp.float32),
-            pltpu.SemaphoreType.DMA((2,)),
-            pltpu.SemaphoreType.DMA((2,)),
+            pltpu.SemaphoreType.DMA((8,)),
+            pltpu.SemaphoreType.DMA((8,)),
         ],
         compiler_params=pltpu.CompilerParams(collective_id=2, has_side_effects=True),
     )(current)

time: 235 us -> 236 us (level)
  no operation moved by 1% of the time
where the time goes in v6:
time: 236 us; the launch traced here: 235 us
  Pallas kernels  147 us (62%)
  matrix products  41.9 us (18%)
  waiting for transfers between devices  29.5 us (12%)
  starting transfers between devices  7.47 us (3%)
  local copies, waits for them, and re-layouts  5.34 us (2%)
  other arithmetic  3.99 us (2%)
    pallas_call x2, Pallas kernels, rows_sum(): pl.pallas_call(functools.partial(rows_sum_kernel, outer, inner), out_shap...  107 us
    pallas_call x2, Pallas kernels, rotate(): pl.pallas_call(functools.partial(rotate_kernel, count), out_shape=jax.Sha...  39.4 us
    all_to_all x1, waiting for transfers between devices, per_device(): lax.all_to_all(slots, 'pair', split_axis=0, concat_axis=0, tiled=True)  29.5 us
    dot_general x4, matrix products, turn(): jnp.dot(chain, first_iter, precision=fast, preferred_element_type=jnp.flo...  16.9 us
    dot_general x2, matrix products, turn(): jnp.dot(weighted, first_iter, precision=fast, preferred_element_type=jnp....  11.7 us
    all_to_all x1, starting transfers between devices, per_device(): lax.all_to_all(slots, 'pair', split_axis=0, concat_axis=0, tiled=True)  7.47 us
    dot_general x2, matrix products, turn(): jnp.dot(applied, scaled_gram, precision=fast, preferred_element_type=jnp....  7.11 us
    dot_general x6, matrix products, inner_gram(): lax.dot_general(left, right, (((0,), (0,)), ((), ())), precision=fast, pr...  6.18 us
  transfers between devices with their start and end apart: 1, of which 1 were waited for; matrix products, arithmetic and copies ran while one was open for 0% of the time, Pallas kernels for 0%

profile of v6, /device:TPU:97, one launch (start us, length us, event | category | flops | bytes accessed | tf_op | source)
XLA Modules:
  0.0 235.2 jit_solution(2696554418075355129)
XLA Ops:
  0.0 0.7 pad_clamp_fusion
  0.7 1.8 copy.6
  2.5 2.0 gather_fusion
  4.5 7.5 %all-to-all-start = ((f32[16,2,32,512]{3,2,1,0:T(8,128)}), f32[16,2,32,512]{3,2,1,0:T(8,128)S(1)}, u32[]{:S(2)}, u32[]{:S(2)}) async-start(f32[16,2,32,512]{3,2,1,0:T(8,128)} %bitcast.40), calls=%async_computation | async-start | bytes 4194304 | tf_op jit(solution)/shard_map/all_to_all | solution.py:392
  12.0 29.5 %all-to-all-done = f32[16,2,32,512]{3,2,1,0:T(8,128)S(1)} async-done(((f32[16,2,32,512]{3,2,1,0:T(8,128)}), f32[16,2,32,512]{3,2,1,0:T(8,128)S(1)}, u32[]{:S(2)}, u32[]{:S(2)}) %all-to-all-start) | async-done | bytes 2097184 | tf_op jit(solution)/shard_map/all_to_all | solution.py:392
  41.5 0.2 fusion.9
  41.6 0.1 pad_maximum_fusion
  41.8 192.1 %while.11 = (s32[]{:T(128)}, f32[512,1024]{1,0:T(8,128)S(1)}, s32[]{:T(128)}) while((s32[]{:T(128)}, f32[512,1024]{1,0:T(8,128)S(1)}, s32[]{:T(128)}) %tuple.26), condition=%wide.region_2.3_spmd, body=%wide.region_0.2_spmd.sunk | while | flops 15306457088 | bytes 81948792 | solution.py:410
  41.8 1.0 fusion.45
  42.8 1.0 select_reduce_fusion.2
  43.9 1.0 convolution_select_fusion.2
  44.9 1.6 select_maximum_fusion.2.payload
  46.5 54.7 %eval_jaxpr.2 = (f32[1024,1024]{1,0:T(8,128)}, f32[1024,1024]{1,0:T(8,128)}, f32[1,1024]{1,0:T(1,128)}, f32[1,1024]{1,0:T(1,128)}) custom-call(f32[1088,512]{1,0:T(8,128)} %select_maximum_fusion.2.payload), custom_call_target="tpu_custom_call" | custom-call | tf_op jit(solution)/shard_map/while/body/eval_jaxpr/pallas_call | solution.py:211
  101.2 0.0 copy-start.1
  101.2 5.9 %fusion.46 = f32[512,1024]{1,0:T(8,128)S(1)} fusion(f32[1024,1024]{1,0:T(8,128)} %get-tuple-element.63, f32[512,1024]{1,0:T(8,128)S(1)} %get-tuple-element.71, f32[1024]{0:T(1024)} %bitcast.47), kind=kOutput, calls=%fused_computation.4.clone.1 | convolution fusion | flops 3221749760 | bytes 8392704 | tf_op jit(solution)/shard_map/while/body/eval_jaxpr/dot_general | solution.py:403
  107.1 0.0 copy-done.1
  107.1 0.0 copy-start
  107.1 3.6 %fusion.47 = f32[512,1024]{1,0:T(8,128)S(1)} fusion(f32[512,1024]{1,0:T(8,128)S(1)} %fusion.46, f32[1024,1024]{1,0:T(8,128)S(1)} %copy-done.1), kind=kOutput, calls=%fused_computation.21.clone.1 | convolution fusion | flops 3221225472 | bytes 8388608 | tf_op jit(solution)/shard_map/while/body/eval_jaxpr/dot_general | solution.py:404
  110.7 0.0 copy-done
  110.7 0.0 copy-start.2
  110.7 3.6 %fusion.48 = f32[512,1024]{1,0:T(8,128)S(1)} fusion(f32[512,1024]{1,0:T(8,128)S(1)} %fusion.47, f32[1024,1024]{1,0:T(8,128)S(1)} %copy-done), kind=kOutput, calls=%fused_computation.22.clone.1 | convolution fusion | flops 3221225472 | bytes 8388608 | tf_op jit(solution)/shard_map/while/body/eval_jaxpr/dot_general | solution.py:405
  114.2 0.0 copy-done.2
  114.3 4.9 %subtract_multiply_fusion.2.current = f32[512,1024]{1,0:T(8,128)} fusion(f32[512,1024]{1,0:T(8,128)S(1)} %fusion.46, f32[512,1024]{1,0:T(8,128)S(1)} %fusion.48, f32[1024,1024]{1,0:T(8,128)S(1)} %copy-done, f32[1024]{0:T(1024)S(1)} %bitcast.46), kind=kOutput, calls=%fused_computation.3.clone.1 | convolution fusion | flops 3222798336 | bytes 10489856 | tf_op jit(solution)/shard_map/while/body/eval_jaxpr/dot_general | solution.py:406
  119.1 19.7 %eval_jaxpr.3 = f32[512,1024]{1,0:T(8,128)S(1)} custom-call(f32[512,1024]{1,0:T(8,128)} %subtract_multiply_fusion.2.current), custom_call_target="tpu_custom_call" | custom-call | tf_op jit(solution)/shard_map/while/body/eval_jaxpr/pallas_call | solution.py:330
  138.9 1.0 fusion.45
  139.9 1.0 select_reduce_fusion.2
  141.0 1.0 convolution_select_fusion.2
  142.0 1.6 select_maximum_fusion.2.payload
  143.6 52.6 %eval_jaxpr.2 = (f32[1024,1024]{1,0:T(8,128)}, f32[1024,1024]{1,0:T(8,128)}, f32[1,1024]{1,0:T(1,128)}, f32[1,1024]{1,0:T(1,128)}) custom-call(f32[1088,512]{1,0:T(8,128)} %select_maximum_fusion.2.payload), custom_call_target="tpu_custom_call" | custom-call | tf_op jit(solution)/shard_map/while/body/eval_jaxpr/pallas_call | solution.py:211
  196.2 0.0 copy-start.1
  196.2 5.9 %fusion.46 = f32[512,1024]{1,0:T(8,128)S(1)} fusion(f32[1024,1024]{1,0:T(8,128)} %get-tuple-element.63, f32[512,1024]{1,0:T(8,128)S(1)} %get-tuple-element.71, f32[1024]{0:T(1024)} %bitcast.47), kind=kOutput, calls=%fused_computation.4.clone.1 | convolution fusion | flops 3221749760 | bytes 8392704 | tf_op jit(solution)/shard_map/while/body/eval_jaxpr/dot_general | solution.py:403
  202.1 0.0 copy-done.1
  202.1 0.0 copy-start
  202.1 3.6 %fusion.47 = f32[512,1024]{1,0:T(8,128)S(1)} fusion(f32[512,1024]{1,0:T(8,128)S(1)} %fusion.46, f32[1024,1024]{1,0:T(8,128)S(1)} %copy-done.1), kind=kOutput, calls=%fused_computation.21.clone.1 | convolution fusion | flops 3221225472 | bytes 8388608 | tf_op jit(solution)/shard_map/while/body/eval_jaxpr/dot_general | solution.py:404
  205.6 0.0 copy-done
  205.7 0.0 copy-start.2
  205.7 3.6 %fusion.48 = f32[512,1024]{1,0:T(8,128)S(1)} fusion(f32[512,1024]{1,0:T(8,128)S(1)} %fusion.47, f32[1024,1024]{1,0:T(8,128)S(1)} %copy-done), kind=kOutput, calls=%fused_computation.22.clone.1 | convolution fusion | flops 3221225472 | bytes 8388608 | tf_op jit(solution)/shard_map/while/body/eval_jaxpr/dot_general | solution.py:405
  209.2 0.0 copy-done.2
  209.2 4.9 %subtract_multiply_fusion.2.current = f32[512,1024]{1,0:T(8,128)} fusion(f32[512,1024]{1,0:T(8,128)S(1)} %fusion.46, f32[512,1024]{1,0:T(8,128)S(1)} %fusion.48, f32[1024,1024]{1,0:T(8,128)S(1)} %copy-done, f32[1024]{0:T(1024)S(1)} %bitcast.46), kind=kOutput, calls=%fused_computation.3.clone.1 | convolution fusion | flops 3222798336 | bytes 10489856 | tf_op jit(solution)/shard_map/while/body/eval_jaxpr/dot_general | solution.py:406
  214.1 19.7 %eval_jaxpr.3 = f32[512,1024]{1,0:T(8,128)S(1)} custom-call(f32[512,1024]{1,0:T(8,128)} %subtract_multiply_fusion.2.current), custom_call_target="tpu_custom_call" | custom-call | tf_op jit(solution)/shard_map/while/body/eval_jaxpr/pallas_call | solution.py:330
  233.9 1.3 copy.16
Async XLA Ops:
  4.5 37.0 %all-to-all-start = ((f32[16,2,32,512]{3,2,1,0:T(8,128)}), f32[16,2,32,512]{3,2,1,0:T(8,128)S(1)}, u32[]{:S(2)}, u32[]{:S(2)}) async-start(f32[16,2,32,512]{3,2,1,0:T(8,128)} %bitcast.40), calls=%async_computation | async-start | bytes 4194304 | tf_op jit(solution)/shard_map/all_to_all | solution.py:392
  101.2 5.9 %copy-start.1 = (f32[1024,1024]{1,0:T(8,128)S(1)}, f32[1024,1024]{1,0:T(8,128)}, u32[]{:S(2)}) copy-start(f32[1024,1024]{1,0:T(8,128)} %get-tuple-element.65) | copy-start | bytes 12582916 | tf_op jit(solution)/shard_map/while
  107.1 3.6 %copy-start = (f32[1024,1024]{1,0:T(8,128)S(1)}, f32[1024,1024]{1,0:T(8,128)}, u32[]{:S(2)}) copy-start(f32[1024,1024]{1,0:T(8,128)} %get-tuple-element.63) | copy-start | bytes 12582916 | tf_op jit(solution)/shard_map/while
  110.7 3.6 %copy-start.2 = (f32[1,1024]{1,0:T(1,128)S(1)}, f32[1,1024]{1,0:T(1,128)}, u32[]{:S(2)}) copy-start(f32[1,1024]{1,0:T(1,128)} %get-tuple-element.66) | copy-start | bytes 12292 | tf_op jit(solution)/shard_map/while
  196.2 5.9 %copy-start.1 = (f32[1024,1024]{1,0:T(8,128)S(1)}, f32[1024,1024]{1,0:T(8,128)}, u32[]{:S(2)}) copy-start(f32[1024,1024]{1,0:T(8,128)} %get-tuple-element.65) | copy-start | bytes 12582916 | tf_op jit(solution)/shard_map/while
  202.1 3.6 %copy-start = (f32[1024,1024]{1,0:T(8,128)S(1)}, f32[1024,1024]{1,0:T(8,128)}, u32[]{:S(2)}) copy-start(f32[1024,1024]{1,0:T(8,128)} %get-tuple-element.63) | copy-start | bytes 12582916 | tf_op jit(solution)/shard_map/while
  205.7 3.6 %copy-start.2 = (f32[1,1024]{1,0:T(1,128)S(1)}, f32[1,1024]{1,0:T(1,128)}, u32[]{:S(2)}) copy-start(f32[1,1024]{1,0:T(1,128)} %get-tuple-element.66) | copy-start | bytes 12292 | tf_op jit(solution)/shard_map/while

commit v7 on v5

--- a/solution.py
+++ b/solution.py
@@ -58,7 +58,6 @@
     outer,
     inner,
     payload,
-    scaled_out,
     first_out,
     inverse_out,
     factor_out,
@@ -152,10 +151,10 @@
     for j in range(outer):
         for k in range(inner):
             out[pl.ds(j * b_half + k * b_chunk, b_chunk), cols_b] = b_all[j, k]
-    normalize_packed(out, scaled_out, first_out, inverse_out, factor_out)
-
-
-def normalize_packed(packed, scaled_out, first_out, inverse_out, factor_out):
+    normalize_packed(out, first_out, inverse_out, factor_out)
+
+
+def normalize_packed(packed, first_out, inverse_out, factor_out):
     width = packed.shape[1]
     row = lax.broadcasted_iota(jnp.int32, (width, width), 0)
     col = lax.broadcasted_iota(jnp.int32, (width, width), 1)
@@ -187,10 +186,6 @@
     cross = cross / spread
     three = jnp.where(eye, 3.0, 0.0)
     near, far = pl.ds(0, width), pl.ds(width, width)
-    scaled_out[near, near] = upper
-    scaled_out[near, far] = cross
-    scaled_out[far, near] = cross.T
-    scaled_out[far, far] = lower
     first_out[near, near] = 0.5 * (three - upper)
     first_out[near, far] = 0.5 * (0.0 - cross)
     first_out[far, near] = 0.5 * (0.0 - cross.T)
@@ -212,12 +207,11 @@
         functools.partial(rows_sum_kernel, outer, inner),
         out_shape=(
             jax.ShapeDtypeStruct((2 * width, 2 * width), jnp.float32),
-            jax.ShapeDtypeStruct((2 * width, 2 * width), jnp.float32),
             jax.ShapeDtypeStruct((1, 2 * width), jnp.float32),
             jax.ShapeDtypeStruct((1, 2 * width), jnp.float32),
         ),
         in_specs=[pl.BlockSpec(memory_space=pltpu.VMEM)],
-        out_specs=[pl.BlockSpec(memory_space=pltpu.VMEM)] * 4,
+        out_specs=[pl.BlockSpec(memory_space=pltpu.VMEM)] * 3,
         scratch_shapes=[
             pltpu.VMEM((inner - 1, a_chunk, half_w), jnp.float32),
             pltpu.VMEM((a_chunk, half_w), jnp.float32),
@@ -383,10 +377,12 @@
     def turn(turn_index, current):
         upper = current[:, :BLK]
         lower = current[:, BLK:]
-        scaled_gram, first_iter, inverse, factor = summed_gram(upper, lower, outer, inner)
+        first_iter, inverse, factor = summed_gram(upper, lower, outer, inner)
         weighted = current * inverse
         applied = jnp.dot(weighted, first_iter, precision=fast, preferred_element_type=jnp.float32)
-        chain = jnp.dot(applied, scaled_gram, precision=fast, preferred_element_type=jnp.float32)
+        chain = 3.0 * applied - 2.0 * jnp.dot(
+            applied, first_iter, precision=fast, preferred_element_type=jnp.float32
+        )
         chain = jnp.dot(chain, first_iter, precision=fast, preferred_element_type=jnp.float32)
         chain = jnp.dot(chain, first_iter, precision=fast, preferred_element_type=jnp.float32)
         current = (3.0 * applied - chain) * factor

time: 235 us -> 232 us (0.987)
    pallas_call x2, Pallas kernels: 107 us -> 104 us  [rows_sum(): pl.pallas_call(functools.partial(rows_sum_kernel, outer, inner), out_shap...]
where the time goes in v7:
time: 232 us
  Pallas kernels  144 us (62%)
  matrix products  41.9 us (18%)
  waiting for transfers between devices  29.5 us (13%)
  starting transfers between devices  7.47 us (3%)
  local copies, waits for them, and re-layouts  5.33 us (2%)
  other arithmetic  3.91 us (2%)
    pallas_call x2, Pallas kernels, rows_sum(): pl.pallas_call(functools.partial(rows_sum_kernel, outer, inner), out_shap...  104 us
    pallas_call x2, Pallas kernels, rotate(): pl.pallas_call(functools.partial(rotate_kernel, count), out_shape=jax.Sha...  39.2 us
    all_to_all x1, waiting for transfers between devices, per_device(): lax.all_to_all(slots, 'pair', split_axis=0, concat_axis=0, tiled=True)  29.5 us
    dot_general x4, matrix products, turn(): jnp.dot(chain, first_iter, precision=fast, preferred_element_type=jnp.flo...  16.9 us
    dot_general x2, matrix products, turn(): jnp.dot(weighted, first_iter, precision=fast, preferred_element_type=jnp....  11.7 us
    all_to_all x1, starting transfers between devices, per_device(): lax.all_to_all(slots, 'pair', split_axis=0, concat_axis=0, tiled=True)  7.47 us
    dot_general x2, matrix products, turn(): jnp.dot(applied, first_iter, precision=fast, preferred_element_type=jnp.f...  7.11 us
    dot_general x6, matrix products, inner_gram(): lax.dot_general(left, right, (((0,), (0,)), ((), ())), precision=fast, pr...  6.18 us
  transfers between devices with their start and end apart: 1, of which 1 were waited for; matrix products, arithmetic and copies ran while one was open for 0% of the time, Pallas kernels for 0%

profile of v7, /device:TPU:97, one launch (start us, length us, event | category | flops | bytes accessed | tf_op | source)
XLA Modules:
  0.0 231.9 jit_solution(359093861113284453)
XLA Ops:
  0.0 0.7 pad_clamp_fusion
  0.7 1.8 copy.6
  2.5 2.0 gather_fusion
  4.5 7.5 %all-to-all-start = ((f32[16,2,32,512]{3,2,1,0:T(8,128)}), f32[16,2,32,512]{3,2,1,0:T(8,128)S(1)}, u32[]{:S(2)}, u32[]{:S(2)}) async-start(f32[16,2,32,512]{3,2,1,0:T(8,128)} %bitcast.37), calls=%async_computation | async-start | bytes 4194304 | tf_op jit(solution)/shard_map/all_to_all | solution.py:371
  12.0 29.5 %all-to-all-done = f32[16,2,32,512]{3,2,1,0:T(8,128)S(1)} async-done(((f32[16,2,32,512]{3,2,1,0:T(8,128)}), f32[16,2,32,512]{3,2,1,0:T(8,128)S(1)}, u32[]{:S(2)}, u32[]{:S(2)}) %all-to-all-start) | async-done | bytes 2097184 | tf_op jit(solution)/shard_map/all_to_all | solution.py:371
  41.5 0.2 fusion.17
  41.6 0.1 pad_maximum_fusion
  41.8 188.7 %while.11 = (s32[]{:T(128)}, f32[512,1024]{1,0:T(8,128)S(1)}, s32[]{:T(128)}) while((s32[]{:T(128)}, f32[512,1024]{1,0:T(8,128)S(1)}, s32[]{:T(128)}) %tuple.26), condition=%wide.region_2.3_spmd, body=%wide.region_0.2_spmd.sunk | while | flops 15308029952 | bytes 67268704 | solution.py:391
  41.8 1.0 fusion.51
  42.8 1.0 select_reduce_fusion.2
  43.9 1.0 convolution_select_fusion.2
  44.9 1.6 select_maximum_fusion.2.payload
  46.5 53.2 %eval_jaxpr.2 = (f32[1024,1024]{1,0:T(8,128)}, f32[1,1024]{1,0:T(1,128)}, f32[1,1024]{1,0:T(1,128)}) custom-call(f32[1088,512]{1,0:T(8,128)} %select_maximum_fusion.2.payload), custom_call_target="tpu_custom_call" | custom-call | tf_op jit(solution)/shard_map/while/body/eval_jaxpr/pallas_call | solution.py:206
  99.7 0.0 copy-start
  99.7 5.9 %fusion.52 = f32[512,1024]{1,0:T(8,128)S(1)} fusion(f32[1024,1024]{1,0:T(8,128)} %get-tuple-element.61, f32[512,1024]{1,0:T(8,128)S(1)} %get-tuple-element.68, f32[1024]{0:T(1024)} %bitcast.44), kind=kOutput, calls=%fused_computation.7.clone.1 | convolution fusion | flops 3221749760 | bytes 8392704 | tf_op jit(solution)/shard_map/while/body/eval_jaxpr/dot_general | solution.py:382
  105.6 0.0 copy-done
  105.6 3.6 %fusion.53 = f32[512,1024]{1,0:T(8,128)S(1)} fusion(f32[512,1024]{1,0:T(8,128)S(1)} %fusion.52, f32[1024,1024]{1,0:T(8,128)S(1)} %copy-done), kind=kOutput, calls=%fused_computation.29.clone.1 | convolution fusion | flops 3221225472 | bytes 8388608 | tf_op jit(solution)/shard_map/while/body/eval_jaxpr/dot_general | solution.py:383
  109.1 0.0 copy-start.1
  109.1 3.5 %fusion.54 = f32[512,1024]{1,0:T(8,128)S(1)} fusion(f32[1024,1024]{1,0:T(8,128)S(1)} %copy-done, f32[512,1024]{1,0:T(8,128)S(1)} %fusion.53, f32[512,1024]{1,0:T(8,128)S(1)} %fusion.52), kind=kOutput, calls=%fused_computation.4.clone.1 | convolution fusion | flops 3222798336 | bytes 10485760 | tf_op jit(solution)/shard_map/while/body/eval_jaxpr/dot_general | solution.py:386
  112.7 0.0 copy-done.1
  112.7 4.9 %subtract_multiply_fusion.2.current = f32[512,1024]{1,0:T(8,128)} fusion(f32[512,1024]{1,0:T(8,128)S(1)} %fusion.52, f32[512,1024]{1,0:T(8,128)S(1)} %fusion.54, f32[1024,1024]{1,0:T(8,128)S(1)} %copy-done, f32[1024]{0:T(1024)S(1)} %bitcast.43), kind=kOutput, calls=%fused_computation.3.clone.1 | convolution fusion | flops 3222798336 | bytes 10489856 | tf_op jit(solution)/shard_map/while/body/eval_jaxpr/dot_general | solution.py:387
  117.6 19.6 %eval_jaxpr.3 = f32[512,1024]{1,0:T(8,128)S(1)} custom-call(f32[512,1024]{1,0:T(8,128)} %subtract_multiply_fusion.2.current), custom_call_target="tpu_custom_call" | custom-call | tf_op jit(solution)/shard_map/while/body/eval_jaxpr/pallas_call | solution.py:309
  137.2 1.0 fusion.51
  138.3 1.0 select_reduce_fusion.2
  139.3 1.0 convolution_select_fusion.2
  140.3 1.6 select_maximum_fusion.2.payload
  141.9 51.1 %eval_jaxpr.2 = (f32[1024,1024]{1,0:T(8,128)}, f32[1,1024]{1,0:T(1,128)}, f32[1,1024]{1,0:T(1,128)}) custom-call(f32[1088,512]{1,0:T(8,128)} %select_maximum_fusion.2.payload), custom_call_target="tpu_custom_call" | custom-call | tf_op jit(solution)/shard_map/while/body/eval_jaxpr/pallas_call | solution.py:206
  193.0 0.0 copy-start
  193.0 5.9 %fusion.52 = f32[512,1024]{1,0:T(8,128)S(1)} fusion(f32[1024,1024]{1,0:T(8,128)} %get-tuple-element.61, f32[512,1024]{1,0:T(8,128)S(1)} %get-tuple-element.68, f32[1024]{0:T(1024)} %bitcast.44), kind=kOutput, calls=%fused_computation.7.clone.1 | convolution fusion | flops 3221749760 | bytes 8392704 | tf_op jit(solution)/shard_map/while/body/eval_jaxpr/dot_general | solution.py:382
  198.9 0.0 copy-done
  198.9 3.6 %fusion.53 = f32[512,1024]{1,0:T(8,128)S(1)} fusion(f32[512,1024]{1,0:T(8,128)S(1)} %fusion.52, f32[1024,1024]{1,0:T(8,128)S(1)} %copy-done), kind=kOutput, calls=%fused_computation.29.clone.1 | convolution fusion | flops 3221225472 | bytes 8388608 | tf_op jit(solution)/shard_map/while/body/eval_jaxpr/dot_general | solution.py:383
  202.4 0.0 copy-start.1
  202.5 3.5 %fusion.54 = f32[512,1024]{1,0:T(8,128)S(1)} fusion(f32[1024,1024]{1,0:T(8,128)S(1)} %copy-done, f32[512,1024]{1,0:T(8,128)S(1)} %fusion.53, f32[512,1024]{1,0:T(8,128)S(1)} %fusion.52), kind=kOutput, calls=%fused_computation.4.clone.1 | convolution fusion | flops 3222798336 | bytes 10485760 | tf_op jit(solution)/shard_map/while/body/eval_jaxpr/dot_general | solution.py:386
  206.0 0.0 copy-done.1
  206.0 4.9 %subtract_multiply_fusion.2.current = f32[512,1024]{1,0:T(8,128)} fusion(f32[512,1024]{1,0:T(8,128)S(1)} %fusion.52, f32[512,1024]{1,0:T(8,128)S(1)} %fusion.54, f32[1024,1024]{1,0:T(8,128)S(1)} %copy-done, f32[1024]{0:T(1024)S(1)} %bitcast.43), kind=kOutput, calls=%fused_computation.3.clone.1 | convolution fusion | flops 3222798336 | bytes 10489856 | tf_op jit(solution)/shard_map/while/body/eval_jaxpr/dot_general | solution.py:387
  210.9 19.6 %eval_jaxpr.3 = f32[512,1024]{1,0:T(8,128)S(1)} custom-call(f32[512,1024]{1,0:T(8,128)} %subtract_multiply_fusion.2.current), custom_call_target="tpu_custom_call" | custom-call | tf_op jit(solution)/shard_map/while/body/eval_jaxpr/pallas_call | solution.py:309
  230.5 1.3 copy.16
Async XLA Ops:
  4.5 37.0 %all-to-all-start = ((f32[16,2,32,512]{3,2,1,0:T(8,128)}), f32[16,2,32,512]{3,2,1,0:T(8,128)S(1)}, u32[]{:S(2)}, u32[]{:S(2)}) async-start(f32[16,2,32,512]{3,2,1,0:T(8,128)} %bitcast.37), calls=%async_computation | async-start | bytes 4194304 | tf_op jit(solution)/shard_map/all_to_all | solution.py:371
  99.7 5.9 %copy-start = (f32[1024,1024]{1,0:T(8,128)S(1)}, f32[1024,1024]{1,0:T(8,128)}, u32[]{:S(2)}) copy-start(f32[1024,1024]{1,0:T(8,128)} %get-tuple-element.61) | copy-start | bytes 12582916 | tf_op jit(solution)/shard_map/while
  109.1 3.6 %copy-start.1 = (f32[1,1024]{1,0:T(1,128)S(1)}, f32[1,1024]{1,0:T(1,128)}, u32[]{:S(2)}) copy-start(f32[1,1024]{1,0:T(1,128)} %get-tuple-element.63) | copy-start | bytes 12292 | tf_op jit(solution)/shard_map/while
  193.0 5.9 %copy-start = (f32[1024,1024]{1,0:T(8,128)S(1)}, f32[1024,1024]{1,0:T(8,128)}, u32[]{:S(2)}) copy-start(f32[1024,1024]{1,0:T(8,128)} %get-tuple-element.61) | copy-start | bytes 12582916 | tf_op jit(solution)/shard_map/while
  202.4 3.6 %copy-start.1 = (f32[1,1024]{1,0:T(1,128)S(1)}, f32[1,1024]{1,0:T(1,128)}, u32[]{:S(2)}) copy-start(f32[1,1024]{1,0:T(1,128)} %get-tuple-element.63) | copy-start | bytes 12292 | tf_op jit(solution)/shard_map/while

commit v8 on v7

--- a/solution.py
+++ b/solution.py
@@ -79,15 +79,15 @@
     pair = lax.axis_index("pair")
     me_y = lax.axis_index("ylo")
     me_x = lax.axis_index("x")
-    rows, width = payload.shape
-    half_w = width // 2
-    a_chunk = rows // inner
+    a_rows = a_in.shape[1] * inner
+    b_rows = b_in.shape[0] * outer
+    a_chunk = a_rows // inner
     a_half = a_chunk // outer
-    b_half = rows // outer
+    b_half = b_rows // outer
     b_chunk = b_half // inner
     partner = (me_y + 1) % outer
-    cols_a = pl.ds(0, half_w)
-    cols_b = pl.ds(half_w, half_w)
+    cols_a = slice(None)
+    cols_b = slice(None)
 
     def x_peer(by):
         return (pair, me_y, (me_x + by) % inner)
@@ -104,16 +104,16 @@
     for by in range(1, inner):
         target = (me_x + by) % inner
         rows_k = pl.ds(pl.multiple_of(target * a_chunk, 8), a_chunk)
-        copies.append(remote(payload.at[rows_k, cols_a], a_in.at[by - 1], sends, recvs, by - 1, x_peer(by)))
-    rows_k = pl.ds(pl.multiple_of(partner * b_half, 8), b_half)
-    copies.append(remote(payload.at[rows_k, cols_b], b_in, sends, recvs, 8, y_peer))
+        copies.append(remote(payload.at[rows_k], a_in.at[by - 1], sends, recvs, by - 1, x_peer(by)))
+    rows_k = pl.ds(pl.multiple_of(a_rows + partner * b_half, 8), b_half)
+    copies.append(remote(payload.at[rows_k], b_in, sends, recvs, 8, y_peer))
     for copy in copies:
         copy.wait()
-    total = payload[pl.ds(pl.multiple_of(me_x * a_chunk, 8), a_chunk), cols_a]
+    total = payload[pl.ds(pl.multiple_of(me_x * a_chunk, 8), a_chunk), :]
     for by in range(1, inner):
         total = total + a_in[by - 1]
     a_acc[...] = total
-    b_acc[...] = payload[pl.ds(pl.multiple_of(me_y * b_half, 8), b_half), cols_b] + b_in[...]
+    b_acc[...] = payload[pl.ds(pl.multiple_of(a_rows + me_y * b_half, 8), b_half), :] + b_in[...]
 
     copies = [
         remote(a_acc.at[pl.ds(pl.multiple_of(partner * a_half, 8), a_half)], a_halves.at[0], sends, recvs, 3, y_peer)
@@ -147,10 +147,10 @@
     for copy in copies:
         copy.wait()
     for k in range(inner):
-        out[pl.ds(k * a_chunk, a_chunk), cols_a] = a_all[k]
+        out[pl.ds(k * a_chunk, a_chunk), :] = a_all[k]
     for j in range(outer):
         for k in range(inner):
-            out[pl.ds(j * b_half + k * b_chunk, b_chunk), cols_b] = b_all[j, k]
+            out[pl.ds(a_rows + j * b_half + k * b_chunk, b_chunk), :] = b_all[j, k]
     normalize_packed(out, first_out, inverse_out, factor_out)
 
 
@@ -198,10 +198,11 @@
 
 def rows_sum(v, outer, inner):
     rows, width = v.shape
-    half_w = width // 2
-    a_chunk = rows // inner
+    half_w = width
+    a_rows = round(rows * 4 / 7 / 64) * 64
+    a_chunk = a_rows // inner
     a_half = a_chunk // outer
-    b_half = rows // outer
+    b_half = (rows - a_rows) // outer
     b_chunk = b_half // inner
     return pl.pallas_call(
         functools.partial(rows_sum_kernel, outer, inner),

time: 232 us -> 234 us (level)
  no operation moved by 1% of the time
where the time goes in v8:
time: 234 us; the launch traced here: 233 us
  Pallas kernels  145 us (62%)
  matrix products  41.9 us (18%)
  waiting for transfers between devices  29.5 us (13%)
  starting transfers between devices  7.47 us (3%)
  local copies, waits for them, and re-layouts  5.33 us (2%)
  other arithmetic  3.91 us (2%)
    pallas_call x2, Pallas kernels, rows_sum(): pl.pallas_call(functools.partial(rows_sum_kernel, outer, inner), out_shap...  106 us
    pallas_call x2, Pallas kernels, rotate(): pl.pallas_call(functools.partial(rotate_kernel, count), out_shape=jax.Sha...  39.2 us
    all_to_all x1, waiting for transfers between devices, per_device(): lax.all_to_all(slots, 'pair', split_axis=0, concat_axis=0, tiled=True)  29.5 us
    dot_general x4, matrix products, turn(): jnp.dot(chain, first_iter, precision=fast, preferred_element_type=jnp.flo...  16.9 us
    dot_general x2, matrix products, turn(): jnp.dot(weighted, first_iter, precision=fast, preferred_element_type=jnp....  11.7 us
    all_to_all x1, starting transfers between devices, per_device(): lax.all_to_all(slots, 'pair', split_axis=0, concat_axis=0, tiled=True)  7.47 us
    dot_general x2, matrix products, turn(): jnp.dot(applied, first_iter, precision=fast, preferred_element_type=jnp.f...  7.1 us
    dot_general x6, matrix products, inner_gram(): lax.dot_general(left, right, (((0,), (0,)), ((), ())), precision=fast, pr...  6.18 us
  transfers between devices with their start and end apart: 1, of which 1 were waited for; matrix products, arithmetic and copies ran while one was open for 0% of the time, Pallas kernels for 0%

profile of v8, /device:TPU:97, one launch (start us, length us, event | category | flops | bytes accessed | tf_op | source)
XLA Modules:
  0.0 233.4 jit_solution(3769069429369354870)
XLA Ops:
  0.0 0.7 pad_clamp_fusion
  0.7 1.8 copy.6
  2.5 2.0 gather_fusion
  4.5 7.5 %all-to-all-start = ((f32[16,2,32,512]{3,2,1,0:T(8,128)}), f32[16,2,32,512]{3,2,1,0:T(8,128)S(1)}, u32[]{:S(2)}, u32[]{:S(2)}) async-start(f32[16,2,32,512]{3,2,1,0:T(8,128)} %bitcast.37), calls=%async_computation | async-start | bytes 4194304 | tf_op jit(solution)/shard_map/all_to_all | solution.py:372
  12.0 29.5 %all-to-all-done = f32[16,2,32,512]{3,2,1,0:T(8,128)S(1)} async-done(((f32[16,2,32,512]{3,2,1,0:T(8,128)}), f32[16,2,32,512]{3,2,1,0:T(8,128)S(1)}, u32[]{:S(2)}, u32[]{:S(2)}) %all-to-all-start) | async-done | bytes 2097184 | tf_op jit(solution)/shard_map/all_to_all | solution.py:372
  41.5 0.2 fusion.17
  41.6 0.1 pad_maximum_fusion
  41.8 190.3 %while.11 = (s32[]{:T(128)}, f32[512,1024]{1,0:T(8,128)S(1)}, s32[]{:T(128)}) while((s32[]{:T(128)}, f32[512,1024]{1,0:T(8,128)S(1)}, s32[]{:T(128)}) %tuple.26), condition=%wide.region_2.3_spmd, body=%wide.region_0.2_spmd.sunk | while | flops 15308029952 | bytes 67268704 | solution.py:392
  41.8 1.0 fusion.51
  42.8 1.0 select_reduce_fusion.2
  43.9 1.0 convolution_select_fusion.2
  44.9 1.6 select_maximum_fusion.2.payload
  46.5 54.1 %eval_jaxpr.2 = (f32[1024,1024]{1,0:T(8,128)}, f32[1,1024]{1,0:T(1,128)}, f32[1,1024]{1,0:T(1,128)}) custom-call(f32[1088,512]{1,0:T(8,128)} %select_maximum_fusion.2.payload), custom_call_target="tpu_custom_call" | custom-call | tf_op jit(solution)/shard_map/while/body/eval_jaxpr/pallas_call | solution.py:207
  100.5 0.0 copy-start
  100.6 5.9 %fusion.52 = f32[512,1024]{1,0:T(8,128)S(1)} fusion(f32[1024,1024]{1,0:T(8,128)} %get-tuple-element.61, f32[512,1024]{1,0:T(8,128)S(1)} %get-tuple-element.68, f32[1024]{0:T(1024)} %bitcast.44), kind=kOutput, calls=%fused_computation.7.clone.1 | convolution fusion | flops 3221749760 | bytes 8392704 | tf_op jit(solution)/shard_map/while/body/eval_jaxpr/dot_general | solution.py:383
  106.4 0.0 copy-done
  106.4 3.6 %fusion.53 = f32[512,1024]{1,0:T(8,128)S(1)} fusion(f32[512,1024]{1,0:T(8,128)S(1)} %fusion.52, f32[1024,1024]{1,0:T(8,128)S(1)} %copy-done), kind=kOutput, calls=%fused_computation.29.clone.1 | convolution fusion | flops 3221225472 | bytes 8388608 | tf_op jit(solution)/shard_map/while/body/eval_jaxpr/dot_general | solution.py:384
  110.0 0.0 copy-start.1
  110.0 3.5 %fusion.54 = f32[512,1024]{1,0:T(8,128)S(1)} fusion(f32[1024,1024]{1,0:T(8,128)S(1)} %copy-done, f32[512,1024]{1,0:T(8,128)S(1)} %fusion.53, f32[512,1024]{1,0:T(8,128)S(1)} %fusion.52), kind=kOutput, calls=%fused_computation.4.clone.1 | convolution fusion | flops 3222798336 | bytes 10485760 | tf_op jit(solution)/shard_map/while/body/eval_jaxpr/dot_general | solution.py:387
  113.6 0.0 copy-done.1
  113.6 4.9 %subtract_multiply_fusion.2.current = f32[512,1024]{1,0:T(8,128)} fusion(f32[512,1024]{1,0:T(8,128)S(1)} %fusion.52, f32[512,1024]{1,0:T(8,128)S(1)} %fusion.54, f32[1024,1024]{1,0:T(8,128)S(1)} %copy-done, f32[1024]{0:T(1024)S(1)} %bitcast.43), kind=kOutput, calls=%fused_computation.3.clone.1 | convolution fusion | flops 3222798336 | bytes 10489856 | tf_op jit(solution)/shard_map/while/body/eval_jaxpr/dot_general | solution.py:388
  118.5 19.6 %eval_jaxpr.3 = f32[512,1024]{1,0:T(8,128)S(1)} custom-call(f32[512,1024]{1,0:T(8,128)} %subtract_multiply_fusion.2.current), custom_call_target="tpu_custom_call" | custom-call | tf_op jit(solution)/shard_map/while/body/eval_jaxpr/pallas_call | solution.py:310
  138.1 1.0 fusion.51
  139.1 1.0 select_reduce_fusion.2
  140.1 1.0 convolution_select_fusion.2
  141.2 1.6 select_maximum_fusion.2.payload
  142.7 51.8 %eval_jaxpr.2 = (f32[1024,1024]{1,0:T(8,128)}, f32[1,1024]{1,0:T(1,128)}, f32[1,1024]{1,0:T(1,128)}) custom-call(f32[1088,512]{1,0:T(8,128)} %select_maximum_fusion.2.payload), custom_call_target="tpu_custom_call" | custom-call | tf_op jit(solution)/shard_map/while/body/eval_jaxpr/pallas_call | solution.py:207
  194.5 0.0 copy-start
  194.6 5.9 %fusion.52 = f32[512,1024]{1,0:T(8,128)S(1)} fusion(f32[1024,1024]{1,0:T(8,128)} %get-tuple-element.61, f32[512,1024]{1,0:T(8,128)S(1)} %get-tuple-element.68, f32[1024]{0:T(1024)} %bitcast.44), kind=kOutput, calls=%fused_computation.7.clone.1 | convolution fusion | flops 3221749760 | bytes 8392704 | tf_op jit(solution)/shard_map/while/body/eval_jaxpr/dot_general | solution.py:383
  200.4 0.0 copy-done
  200.4 3.6 %fusion.53 = f32[512,1024]{1,0:T(8,128)S(1)} fusion(f32[512,1024]{1,0:T(8,128)S(1)} %fusion.52, f32[1024,1024]{1,0:T(8,128)S(1)} %copy-done), kind=kOutput, calls=%fused_computation.29.clone.1 | convolution fusion | flops 3221225472 | bytes 8388608 | tf_op jit(solution)/shard_map/while/body/eval_jaxpr/dot_general | solution.py:384
  204.0 0.0 copy-start.1
  204.0 3.5 %fusion.54 = f32[512,1024]{1,0:T(8,128)S(1)} fusion(f32[1024,1024]{1,0:T(8,128)S(1)} %copy-done, f32[512,1024]{1,0:T(8,128)S(1)} %fusion.53, f32[512,1024]{1,0:T(8,128)S(1)} %fusion.52), kind=kOutput, calls=%fused_computation.4.clone.1 | convolution fusion | flops 3222798336 | bytes 10485760 | tf_op jit(solution)/shard_map/while/body/eval_jaxpr/dot_general | solution.py:387
  207.6 0.0 copy-done.1
  207.6 4.9 %subtract_multiply_fusion.2.current = f32[512,1024]{1,0:T(8,128)} fusion(f32[512,1024]{1,0:T(8,128)S(1)} %fusion.52, f32[512,1024]{1,0:T(8,128)S(1)} %fusion.54, f32[1024,1024]{1,0:T(8,128)S(1)} %copy-done, f32[1024]{0:T(1024)S(1)} %bitcast.43), kind=kOutput, calls=%fused_computation.3.clone.1 | convolution fusion | flops 3222798336 | bytes 10489856 | tf_op jit(solution)/shard_map/while/body/eval_jaxpr/dot_general | solution.py:388
  212.5 19.6 %eval_jaxpr.3 = f32[512,1024]{1,0:T(8,128)S(1)} custom-call(f32[512,1024]{1,0:T(8,128)} %subtract_multiply_fusion.2.current), custom_call_target="tpu_custom_call" | custom-call | tf_op jit(solution)/shard_map/while/body/eval_jaxpr/pallas_call | solution.py:310
  232.1 1.3 copy.16
Async XLA Ops:
  4.5 37.0 %all-to-all-start = ((f32[16,2,32,512]{3,2,1,0:T(8,128)}), f32[16,2,32,512]{3,2,1,0:T(8,128)S(1)}, u32[]{:S(2)}, u32[]{:S(2)}) async-start(f32[16,2,32,512]{3,2,1,0:T(8,128)} %bitcast.37), calls=%async_computation | async-start | bytes 4194304 | tf_op jit(solution)/shard_map/all_to_all | solution.py:372
  100.5 5.9 %copy-start = (f32[1024,1024]{1,0:T(8,128)S(1)}, f32[1024,1024]{1,0:T(8,128)}, u32[]{:S(2)}) copy-start(f32[1024,1024]{1,0:T(8,128)} %get-tuple-element.61) | copy-start | bytes 12582916 | tf_op jit(solution)/shard_map/while
  110.0 3.6 %copy-start.1 = (f32[1,1024]{1,0:T(1,128)S(1)}, f32[1,1024]{1,0:T(1,128)}, u32[]{:S(2)}) copy-start(f32[1,1024]{1,0:T(1,128)} %get-tuple-element.63) | copy-start | bytes 12292 | tf_op jit(solution)/shard_map/while
  194.5 5.9 %copy-start = (f32[1024,1024]{1,0:T(8,128)S(1)}, f32[1024,1024]{1,0:T(8,128)}, u32[]{:S(2)}) copy-start(f32[1024,1024]{1,0:T(8,128)} %get-tuple-element.61) | copy-start | bytes 12582916 | tf_op jit(solution)/shard_map/while
  204.0 3.6 %copy-start.1 = (f32[1,1024]{1,0:T(1,128)S(1)}, f32[1,1024]{1,0:T(1,128)}, u32[]{:S(2)}) copy-start(f32[1,1024]{1,0:T(1,128)} %get-tuple-element.63) | copy-start | bytes 12292 | tf_op jit(solution)/shard_map/while

commit v9 on v8

--- a/solution.py
+++ b/solution.py
@@ -199,7 +199,7 @@
 def rows_sum(v, outer, inner):
     rows, width = v.shape
     half_w = width
-    a_rows = round(rows * 4 / 7 / 64) * 64
+    a_rows = round(rows * 3 / 7 / 64) * 64
     a_chunk = a_rows // inner
     a_half = a_chunk // outer
     b_half = (rows - a_rows) // outer

time: 234 us -> 242 us (1.034)
  Pallas kernels: 145 us -> 153 us
    pallas_call x2, Pallas kernels: 106 us -> 114 us  [rows_sum(): pl.pallas_call(functools.partial(rows_sum_kernel, outer, inner), out_shap...]
where the time goes in v9:
time: 242 us; the launch traced here: 241 us
  Pallas kernels  153 us (63%)
  matrix products  41.9 us (17%)
  waiting for transfers between devices  29.5 us (12%)
  starting transfers between devices  7.47 us (3%)
  local copies, waits for them, and re-layouts  5.33 us (2%)
  other arithmetic  3.91 us (2%)
    pallas_call x2, Pallas kernels, rows_sum(): pl.pallas_call(functools.partial(rows_sum_kernel, outer, inner), out_shap...  114 us
    pallas_call x2, Pallas kernels, rotate(): pl.pallas_call(functools.partial(rotate_kernel, count), out_shape=jax.Sha...  39.2 us
    all_to_all x1, waiting for transfers between devices, per_device(): lax.all_to_all(slots, 'pair', split_axis=0, concat_axis=0, tiled=True)  29.5 us
    dot_general x4, matrix products, turn(): jnp.dot(chain, first_iter, precision=fast, preferred_element_type=jnp.flo...  16.9 us
    dot_general x2, matrix products, turn(): jnp.dot(weighted, first_iter, precision=fast, preferred_element_type=jnp....  11.7 us
    all_to_all x1, starting transfers between devices, per_device(): lax.all_to_all(slots, 'pair', split_axis=0, concat_axis=0, tiled=True)  7.47 us
    dot_general x2, matrix products, turn(): jnp.dot(applied, first_iter, precision=fast, preferred_element_type=jnp.f...  7.1 us
    dot_general x6, matrix products, inner_gram(): lax.dot_general(left, right, (((0,), (0,)), ((), ())), precision=fast, pr...  6.18 us
  transfers between devices with their start and end apart: 1, of which 1 were waited for; matrix products, arithmetic and copies ran while one was open for 0% of the time, Pallas kernels for 0%

profile of v9, /device:TPU:97, one launch (start us, length us, event | category | flops | bytes accessed | tf_op | source)
XLA Modules:
  0.0 241.3 jit_solution(15717582105741011609)
XLA Ops:
  0.0 0.7 pad_clamp_fusion
  0.7 1.8 copy.6
  2.5 2.0 gather_fusion
  4.5 7.5 %all-to-all-start = ((f32[16,2,32,512]{3,2,1,0:T(8,128)}), f32[16,2,32,512]{3,2,1,0:T(8,128)S(1)}, u32[]{:S(2)}, u32[]{:S(2)}) async-start(f32[16,2,32,512]{3,2,1,0:T(8,128)} %bitcast.37), calls=%async_computation | async-start | bytes 4194304 | tf_op jit(solution)/shard_map/all_to_all | solution.py:372
  12.0 29.5 %all-to-all-done = f32[16,2,32,512]{3,2,1,0:T(8,128)S(1)} async-done(((f32[16,2,32,512]{3,2,1,0:T(8,128)}), f32[16,2,32,512]{3,2,1,0:T(8,128)S(1)}, u32[]{:S(2)}, u32[]{:S(2)}) %all-to-all-start) | async-done | bytes 2097184 | tf_op jit(solution)/shard_map/all_to_all | solution.py:372
  41.5 0.2 fusion.17
  41.6 0.1 pad_maximum_fusion
  41.8 198.2 %while.11 = (s32[]{:T(128)}, f32[512,1024]{1,0:T(8,128)S(1)}, s32[]{:T(128)}) while((s32[]{:T(128)}, f32[512,1024]{1,0:T(8,128)S(1)}, s32[]{:T(128)}) %tuple.26), condition=%wide.region_2.3_spmd, body=%wide.region_0.2_spmd.sunk | while | flops 15308029952 | bytes 67268704 | solution.py:392
  41.8 1.0 fusion.51
  42.8 1.0 select_reduce_fusion.2
  43.9 1.0 convolution_select_fusion.2
  44.9 1.6 select_maximum_fusion.2.payload
  46.5 57.5 %eval_jaxpr.2 = (f32[1024,1024]{1,0:T(8,128)}, f32[1,1024]{1,0:T(1,128)}, f32[1,1024]{1,0:T(1,128)}) custom-call(f32[1088,512]{1,0:T(8,128)} %select_maximum_fusion.2.payload), custom_call_target="tpu_custom_call" | custom-call | tf_op jit(solution)/shard_map/while/body/eval_jaxpr/pallas_call | solution.py:207
  104.0 0.0 copy-start
  104.0 5.9 %fusion.52 = f32[512,1024]{1,0:T(8,128)S(1)} fusion(f32[1024,1024]{1,0:T(8,128)} %get-tuple-element.61, f32[512,1024]{1,0:T(8,128)S(1)} %get-tuple-element.68, f32[1024]{0:T(1024)} %bitcast.44), kind=kOutput, calls=%fused_computation.7.clone.1 | convolution fusion | flops 3221749760 | bytes 8392704 | tf_op jit(solution)/shard_map/while/body/eval_jaxpr/dot_general | solution.py:383
  109.9 0.0 copy-done
  109.9 3.6 %fusion.53 = f32[512,1024]{1,0:T(8,128)S(1)} fusion(f32[512,1024]{1,0:T(8,128)S(1)} %fusion.52, f32[1024,1024]{1,0:T(8,128)S(1)} %copy-done), kind=kOutput, calls=%fused_computation.29.clone.1 | convolution fusion | flops 3221225472 | bytes 8388608 | tf_op jit(solution)/shard_map/while/body/eval_jaxpr/dot_general | solution.py:384
  113.4 0.0 copy-start.1
  113.5 3.5 %fusion.54 = f32[512,1024]{1,0:T(8,128)S(1)} fusion(f32[1024,1024]{1,0:T(8,128)S(1)} %copy-done, f32[512,1024]{1,0:T(8,128)S(1)} %fusion.53, f32[512,1024]{1,0:T(8,128)S(1)} %fusion.52), kind=kOutput, calls=%fused_computation.4.clone.1 | convolution fusion | flops 3222798336 | bytes 10485760 | tf_op jit(solution)/shard_map/while/body/eval_jaxpr/dot_general | solution.py:387
  117.0 0.0 copy-done.1
  117.0 4.9 %subtract_multiply_fusion.2.current = f32[512,1024]{1,0:T(8,128)} fusion(f32[512,1024]{1,0:T(8,128)S(1)} %fusion.52, f32[512,1024]{1,0:T(8,128)S(1)} %fusion.54, f32[1024,1024]{1,0:T(8,128)S(1)} %copy-done, f32[1024]{0:T(1024)S(1)} %bitcast.43), kind=kOutput, calls=%fused_computation.3.clone.1 | convolution fusion | flops 3222798336 | bytes 10489856 | tf_op jit(solution)/shard_map/while/body/eval_jaxpr/dot_general | solution.py:388
  121.9 19.6 %eval_jaxpr.3 = f32[512,1024]{1,0:T(8,128)S(1)} custom-call(f32[512,1024]{1,0:T(8,128)} %subtract_multiply_fusion.2.current), custom_call_target="tpu_custom_call" | custom-call | tf_op jit(solution)/shard_map/while/body/eval_jaxpr/pallas_call | solution.py:310
  141.5 1.0 fusion.51
  142.6 1.0 select_reduce_fusion.2
  143.6 1.0 convolution_select_fusion.2
  144.6 1.6 select_maximum_fusion.2.payload
  146.2 56.3 %eval_jaxpr.2 = (f32[1024,1024]{1,0:T(8,128)}, f32[1,1024]{1,0:T(1,128)}, f32[1,1024]{1,0:T(1,128)}) custom-call(f32[1088,512]{1,0:T(8,128)} %select_maximum_fusion.2.payload), custom_call_target="tpu_custom_call" | custom-call | tf_op jit(solution)/shard_map/while/body/eval_jaxpr/pallas_call | solution.py:207
  202.5 0.0 copy-start
  202.5 5.9 %fusion.52 = f32[512,1024]{1,0:T(8,128)S(1)} fusion(f32[1024,1024]{1,0:T(8,128)} %get-tuple-element.61, f32[512,1024]{1,0:T(8,128)S(1)} %get-tuple-element.68, f32[1024]{0:T(1024)} %bitcast.44), kind=kOutput, calls=%fused_computation.7.clone.1 | convolution fusion | flops 3221749760 | bytes 8392704 | tf_op jit(solution)/shard_map/while/body/eval_jaxpr/dot_general | solution.py:383
  208.3 0.0 copy-done
  208.4 3.6 %fusion.53 = f32[512,1024]{1,0:T(8,128)S(1)} fusion(f32[512,1024]{1,0:T(8,128)S(1)} %fusion.52, f32[1024,1024]{1,0:T(8,128)S(1)} %copy-done), kind=kOutput, calls=%fused_computation.29.clone.1 | convolution fusion | flops 3221225472 | bytes 8388608 | tf_op jit(solution)/shard_map/while/body/eval_jaxpr/dot_general | solution.py:384
  211.9 0.0 copy-start.1
  211.9 3.5 %fusion.54 = f32[512,1024]{1,0:T(8,128)S(1)} fusion(f32[1024,1024]{1,0:T(8,128)S(1)} %copy-done, f32[512,1024]{1,0:T(8,128)S(1)} %fusion.53, f32[512,1024]{1,0:T(8,128)S(1)} %fusion.52), kind=kOutput, calls=%fused_computation.4.clone.1 | convolution fusion | flops 3222798336 | bytes 10485760 | tf_op jit(solution)/shard_map/while/body/eval_jaxpr/dot_general | solution.py:387
  215.5 0.0 copy-done.1
  215.5 4.9 %subtract_multiply_fusion.2.current = f32[512,1024]{1,0:T(8,128)} fusion(f32[512,1024]{1,0:T(8,128)S(1)} %fusion.52, f32[512,1024]{1,0:T(8,128)S(1)} %fusion.54, f32[1024,1024]{1,0:T(8,128)S(1)} %copy-done, f32[1024]{0:T(1024)S(1)} %bitcast.43), kind=kOutput, calls=%fused_computation.3.clone.1 | convolution fusion | flops 3222798336 | bytes 10489856 | tf_op jit(solution)/shard_map/while/body/eval_jaxpr/dot_general | solution.py:388
  220.4 19.6 %eval_jaxpr.3 = f32[512,1024]{1,0:T(8,128)S(1)} custom-call(f32[512,1024]{1,0:T(8,128)} %subtract_multiply_fusion.2.current), custom_call_target="tpu_custom_call" | custom-call | tf_op jit(solution)/shard_map/while/body/eval_jaxpr/pallas_call | solution.py:310
  240.0 1.3 copy.16
Async XLA Ops:
  4.5 37.0 %all-to-all-start = ((f32[16,2,32,512]{3,2,1,0:T(8,128)}), f32[16,2,32,512]{3,2,1,0:T(8,128)S(1)}, u32[]{:S(2)}, u32[]{:S(2)}) async-start(f32[16,2,32,512]{3,2,1,0:T(8,128)} %bitcast.37), calls=%async_computation | async-start | bytes 4194304 | tf_op jit(solution)/shard_map/all_to_all | solution.py:372
  104.0 5.9 %copy-start = (f32[1024,1024]{1,0:T(8,128)S(1)}, f32[1024,1024]{1,0:T(8,128)}, u32[]{:S(2)}) copy-start(f32[1024,1024]{1,0:T(8,128)} %get-tuple-element.61) | copy-start | bytes 12582916 | tf_op jit(solution)/shard_map/while
  113.4 3.6 %copy-start.1 = (f32[1,1024]{1,0:T(1,128)S(1)}, f32[1,1024]{1,0:T(1,128)}, u32[]{:S(2)}) copy-start(f32[1,1024]{1,0:T(1,128)} %get-tuple-element.63) | copy-start | bytes 12292 | tf_op jit(solution)/shard_map/while
  202.5 5.9 %copy-start = (f32[1024,1024]{1,0:T(8,128)S(1)}, f32[1024,1024]{1,0:T(8,128)}, u32[]{:S(2)}) copy-start(f32[1024,1024]{1,0:T(8,128)} %get-tuple-element.61) | copy-start | bytes 12582916 | tf_op jit(solution)/shard_map/while
  211.9 3.6 %copy-start.1 = (f32[1,1024]{1,0:T(1,128)S(1)}, f32[1,1024]{1,0:T(1,128)}, u32[]{:S(2)}) copy-start(f32[1,1024]{1,0:T(1,128)} %get-tuple-element.63) | copy-start | bytes 12292 | tf_op jit(solution)/shard_map/while

commit v10 on v7

--- a/solution.py
+++ b/solution.py
@@ -100,51 +100,59 @@
     pl.semaphore_signal(barrier, inc=1, device_id=y_peer, device_id_type=MESH)
     pl.semaphore_wait(barrier, inner)
 
-    copies = []
+    a_copies = []
     for by in range(1, inner):
         target = (me_x + by) % inner
         rows_k = pl.ds(pl.multiple_of(target * a_chunk, 8), a_chunk)
-        copies.append(remote(payload.at[rows_k, cols_a], a_in.at[by - 1], sends, recvs, by - 1, x_peer(by)))
+        a_copies.append(remote(payload.at[rows_k, cols_a], a_in.at[by - 1], sends, recvs, by - 1, x_peer(by)))
     rows_k = pl.ds(pl.multiple_of(partner * b_half, 8), b_half)
-    copies.append(remote(payload.at[rows_k, cols_b], b_in, sends, recvs, 8, y_peer))
-    for copy in copies:
+    b_copies = [remote(payload.at[rows_k, cols_b], b_in, sends, recvs, 8, y_peer)]
+
+    for copy in a_copies:
         copy.wait()
     total = payload[pl.ds(pl.multiple_of(me_x * a_chunk, 8), a_chunk), cols_a]
     for by in range(1, inner):
         total = total + a_in[by - 1]
     a_acc[...] = total
-    b_acc[...] = payload[pl.ds(pl.multiple_of(me_y * b_half, 8), b_half), cols_b] + b_in[...]
-
-    copies = [
+    a_copies = [
         remote(a_acc.at[pl.ds(pl.multiple_of(partner * a_half, 8), a_half)], a_halves.at[0], sends, recvs, 3, y_peer)
     ]
+
+    for copy in b_copies:
+        copy.wait()
+    b_acc[...] = payload[pl.ds(pl.multiple_of(me_y * b_half, 8), b_half), cols_b] + b_in[...]
+    b_copies = []
     for by in range(1, inner):
         target = (me_x + by) % inner
         rows_k = pl.ds(pl.multiple_of(target * b_chunk, 8), b_chunk)
-        copies.append(remote(b_acc.at[rows_k], b_parts.at[by - 1], sends, recvs, 8 + by, x_peer(by)))
-    for copy in copies:
+        b_copies.append(remote(b_acc.at[rows_k], b_parts.at[by - 1], sends, recvs, 8 + by, x_peer(by)))
+
+    for copy in a_copies:
         copy.wait()
     a_own[...] = a_acc[pl.ds(pl.multiple_of(me_y * a_half, 8), a_half), :] + a_halves[0]
+    a_copies = [remote(a_own, a_halves.at[1], sends, recvs, 4, y_peer)]
+
+    for copy in b_copies:
+        copy.wait()
     total = b_acc[pl.ds(pl.multiple_of(me_x * b_chunk, 8), b_chunk), :]
     for by in range(1, inner):
         total = total + b_parts[by - 1]
     b_own[...] = total
-
-    copies = [remote(a_own, a_halves.at[1], sends, recvs, 4, y_peer)]
-    for by in range(1, inner):
-        copies.append(remote(b_own, b_row.at[me_x], sends, recvs, 11 + by, x_peer(by)))
-    for copy in copies:
+    b_copies = [remote(b_own, b_row.at[me_x], sends, recvs, 11 + by, x_peer(by)) for by in range(1, inner)]
+
+    for copy in a_copies:
         copy.wait()
     a_all[me_x, pl.ds(pl.multiple_of(me_y * a_half, 8), a_half), :] = a_own[...]
     a_all[me_x, pl.ds(pl.multiple_of(partner * a_half, 8), a_half), :] = a_halves[1]
+    a_copies = [remote(a_all.at[me_x], a_all.at[me_x], sends, recvs, 4 + by, x_peer(by)) for by in range(1, inner)]
+
     b_row[me_x] = b_own[...]
+    for copy in b_copies:
+        copy.wait()
     b_all[me_y] = b_row[...]
-
-    copies = []
-    for by in range(1, inner):
-        copies.append(remote(a_all.at[me_x], a_all.at[me_x], sends, recvs, 4 + by, x_peer(by)))
-    copies.append(remote(b_row, b_all.at[me_y], sends, recvs, 15, y_peer))
-    for copy in copies:
+    b_copies = [remote(b_row, b_all.at[me_y], sends, recvs, 15, y_peer)]
+
+    for copy in a_copies + b_copies:
         copy.wait()
     for k in range(inner):
         out[pl.ds(k * a_chunk, a_chunk), cols_a] = a_all[k]

time: 232 us -> 231 us (level)
  Pallas kernels: 144 us -> 140 us
    pallas_call x2, Pallas kernels: 104 us -> 101 us  [rows_sum(): pl.pallas_call(functools.partial(rows_sum_kernel, outer, inner), out_shap...]
where the time goes in v10:
time: 231 us; the launch traced here: 229 us
  Pallas kernels  140 us (61%)
  matrix products  41.9 us (18%)
  waiting for transfers between devices  29.5 us (13%)
  starting transfers between devices  7.47 us (3%)
  local copies, waits for them, and re-layouts  5.33 us (2%)
  other arithmetic  3.91 us (2%)
    pallas_call x2, Pallas kernels, rows_sum(): pl.pallas_call(functools.partial(rows_sum_kernel, outer, inner), out_shap...  101 us
    pallas_call x2, Pallas kernels, rotate(): pl.pallas_call(functools.partial(rotate_kernel, count), out_shape=jax.Sha...  39.2 us
    all_to_all x1, waiting for transfers between devices, per_device(): lax.all_to_all(slots, 'pair', split_axis=0, concat_axis=0, tiled=True)  29.5 us
    dot_general x4, matrix products, turn(): jnp.dot(chain, first_iter, precision=fast, preferred_element_type=jnp.flo...  16.9 us
    dot_general x2, matrix products, turn(): jnp.dot(weighted, first_iter, precision=fast, preferred_element_type=jnp....  11.7 us
    all_to_all x1, starting transfers between devices, per_device(): lax.all_to_all(slots, 'pair', split_axis=0, concat_axis=0, tiled=True)  7.47 us
    dot_general x2, matrix products, turn(): jnp.dot(applied, first_iter, precision=fast, preferred_element_type=jnp.f...  7.1 us
    dot_general x6, matrix products, inner_gram(): lax.dot_general(left, right, (((0,), (0,)), ((), ())), precision=fast, pr...  6.18 us
  transfers between devices with their start and end apart: 1, of which 1 were waited for; matrix products, arithmetic and copies ran while one was open for 0% of the time, Pallas kernels for 0%

profile of v10, /device:TPU:97, one launch (start us, length us, event | category | flops | bytes accessed | tf_op | source)
XLA Modules:
  0.0 228.8 jit_solution(1097862896737244799)
XLA Ops:
  0.0 0.7 pad_clamp_fusion
  0.7 1.8 copy.6
  2.5 2.0 gather_fusion
  4.5 7.5 %all-to-all-start = ((f32[16,2,32,512]{3,2,1,0:T(8,128)}), f32[16,2,32,512]{3,2,1,0:T(8,128)S(1)}, u32[]{:S(2)}, u32[]{:S(2)}) async-start(f32[16,2,32,512]{3,2,1,0:T(8,128)} %bitcast.37), calls=%async_computation | async-start | bytes 4194304 | tf_op jit(solution)/shard_map/all_to_all | solution.py:379
  12.0 29.5 %all-to-all-done = f32[16,2,32,512]{3,2,1,0:T(8,128)S(1)} async-done(((f32[16,2,32,512]{3,2,1,0:T(8,128)}), f32[16,2,32,512]{3,2,1,0:T(8,128)S(1)}, u32[]{:S(2)}, u32[]{:S(2)}) %all-to-all-start) | async-done | bytes 2097184 | tf_op jit(solution)/shard_map/all_to_all | solution.py:379
  41.5 0.2 fusion.17
  41.6 0.1 pad_maximum_fusion
  41.8 185.6 %while.11 = (s32[]{:T(128)}, f32[512,1024]{1,0:T(8,128)S(1)}, s32[]{:T(128)}) while((s32[]{:T(128)}, f32[512,1024]{1,0:T(8,128)S(1)}, s32[]{:T(128)}) %tuple.26), condition=%wide.region_2.3_spmd, body=%wide.region_0.2_spmd.sunk | while | flops 15308029952 | bytes 67268704 | solution.py:399
  41.8 1.0 fusion.51
  42.8 1.0 select_reduce_fusion.2
  43.9 1.0 convolution_select_fusion.2
  44.9 1.6 select_maximum_fusion.2.payload
  46.5 51.9 %eval_jaxpr.2 = (f32[1024,1024]{1,0:T(8,128)}, f32[1,1024]{1,0:T(1,128)}, f32[1,1024]{1,0:T(1,128)}) custom-call(f32[1088,512]{1,0:T(8,128)} %select_maximum_fusion.2.payload), custom_call_target="tpu_custom_call" | custom-call | tf_op jit(solution)/shard_map/while/body/eval_jaxpr/pallas_call | solution.py:214
  98.4 0.0 copy-start
  98.4 5.9 %fusion.52 = f32[512,1024]{1,0:T(8,128)S(1)} fusion(f32[1024,1024]{1,0:T(8,128)} %get-tuple-element.61, f32[512,1024]{1,0:T(8,128)S(1)} %get-tuple-element.68, f32[1024]{0:T(1024)} %bitcast.44), kind=kOutput, calls=%fused_computation.7.clone.1 | convolution fusion | flops 3221749760 | bytes 8392704 | tf_op jit(solution)/shard_map/while/body/eval_jaxpr/dot_general | solution.py:390
  104.3 0.0 copy-done
  104.3 3.6 %fusion.53 = f32[512,1024]{1,0:T(8,128)S(1)} fusion(f32[512,1024]{1,0:T(8,128)S(1)} %fusion.52, f32[1024,1024]{1,0:T(8,128)S(1)} %copy-done), kind=kOutput, calls=%fused_computation.29.clone.1 | convolution fusion | flops 3221225472 | bytes 8388608 | tf_op jit(solution)/shard_map/while/body/eval_jaxpr/dot_general | solution.py:391
  107.8 0.0 copy-start.1
  107.8 3.5 %fusion.54 = f32[512,1024]{1,0:T(8,128)S(1)} fusion(f32[1024,1024]{1,0:T(8,128)S(1)} %copy-done, f32[512,1024]{1,0:T(8,128)S(1)} %fusion.53, f32[512,1024]{1,0:T(8,128)S(1)} %fusion.52), kind=kOutput, calls=%fused_computation.4.clone.1 | convolution fusion | flops 3222798336 | bytes 10485760 | tf_op jit(solution)/shard_map/while/body/eval_jaxpr/dot_general | solution.py:394
  111.4 0.0 copy-done.1
  111.4 4.9 %subtract_multiply_fusion.2.current = f32[512,1024]{1,0:T(8,128)} fusion(f32[512,1024]{1,0:T(8,128)S(1)} %fusion.52, f32[512,1024]{1,0:T(8,128)S(1)} %fusion.54, f32[1024,1024]{1,0:T(8,128)S(1)} %copy-done, f32[1024]{0:T(1024)S(1)} %bitcast.43), kind=kOutput, calls=%fused_computation.3.clone.1 | convolution fusion | flops 3222798336 | bytes 10489856 | tf_op jit(solution)/shard_map/while/body/eval_jaxpr/dot_general | solution.py:395
  116.3 19.6 %eval_jaxpr.3 = f32[512,1024]{1,0:T(8,128)S(1)} custom-call(f32[512,1024]{1,0:T(8,128)} %subtract_multiply_fusion.2.current), custom_call_target="tpu_custom_call" | custom-call | tf_op jit(solution)/shard_map/while/body/eval_jaxpr/pallas_call | solution.py:317
  135.9 1.0 fusion.51
  137.0 1.0 select_reduce_fusion.2
  138.0 1.0 convolution_select_fusion.2
  139.0 1.6 select_maximum_fusion.2.payload
  140.6 49.3 %eval_jaxpr.2 = (f32[1024,1024]{1,0:T(8,128)}, f32[1,1024]{1,0:T(1,128)}, f32[1,1024]{1,0:T(1,128)}) custom-call(f32[1088,512]{1,0:T(8,128)} %select_maximum_fusion.2.payload), custom_call_target="tpu_custom_call" | custom-call | tf_op jit(solution)/shard_map/while/body/eval_jaxpr/pallas_call | solution.py:214
  189.9 0.0 copy-start
  189.9 5.9 %fusion.52 = f32[512,1024]{1,0:T(8,128)S(1)} fusion(f32[1024,1024]{1,0:T(8,128)} %get-tuple-element.61, f32[512,1024]{1,0:T(8,128)S(1)} %get-tuple-element.68, f32[1024]{0:T(1024)} %bitcast.44), kind=kOutput, calls=%fused_computation.7.clone.1 | convolution fusion | flops 3221749760 | bytes 8392704 | tf_op jit(solution)/shard_map/while/body/eval_jaxpr/dot_general | solution.py:390
  195.8 0.0 copy-done
  195.8 3.6 %fusion.53 = f32[512,1024]{1,0:T(8,128)S(1)} fusion(f32[512,1024]{1,0:T(8,128)S(1)} %fusion.52, f32[1024,1024]{1,0:T(8,128)S(1)} %copy-done), kind=kOutput, calls=%fused_computation.29.clone.1 | convolution fusion | flops 3221225472 | bytes 8388608 | tf_op jit(solution)/shard_map/while/body/eval_jaxpr/dot_general | solution.py:391
  199.3 0.0 copy-start.1
  199.4 3.5 %fusion.54 = f32[512,1024]{1,0:T(8,128)S(1)} fusion(f32[1024,1024]{1,0:T(8,128)S(1)} %copy-done, f32[512,1024]{1,0:T(8,128)S(1)} %fusion.53, f32[512,1024]{1,0:T(8,128)S(1)} %fusion.52), kind=kOutput, calls=%fused_computation.4.clone.1 | convolution fusion | flops 3222798336 | bytes 10485760 | tf_op jit(solution)/shard_map/while/body/eval_jaxpr/dot_general | solution.py:394
  202.9 0.0 copy-done.1
  202.9 4.9 %subtract_multiply_fusion.2.current = f32[512,1024]{1,0:T(8,128)} fusion(f32[512,1024]{1,0:T(8,128)S(1)} %fusion.52, f32[512,1024]{1,0:T(8,128)S(1)} %fusion.54, f32[1024,1024]{1,0:T(8,128)S(1)} %copy-done, f32[1024]{0:T(1024)S(1)} %bitcast.43), kind=kOutput, calls=%fused_computation.3.clone.1 | convolution fusion | flops 3222798336 | bytes 10489856 | tf_op jit(solution)/shard_map/while/body/eval_jaxpr/dot_general | solution.py:395
  207.8 19.6 %eval_jaxpr.3 = f32[512,1024]{1,0:T(8,128)S(1)} custom-call(f32[512,1024]{1,0:T(8,128)} %subtract_multiply_fusion.2.current), custom_call_target="tpu_custom_call" | custom-call | tf_op jit(solution)/shard_map/while/body/eval_jaxpr/pallas_call | solution.py:317
  227.4 1.3 copy.16
Async XLA Ops:
  4.5 37.0 %all-to-all-start = ((f32[16,2,32,512]{3,2,1,0:T(8,128)}), f32[16,2,32,512]{3,2,1,0:T(8,128)S(1)}, u32[]{:S(2)}, u32[]{:S(2)}) async-start(f32[16,2,32,512]{3,2,1,0:T(8,128)} %bitcast.37), calls=%async_computation | async-start | bytes 4194304 | tf_op jit(solution)/shard_map/all_to_all | solution.py:379
  98.4 5.9 %copy-start = (f32[1024,1024]{1,0:T(8,128)S(1)}, f32[1024,1024]{1,0:T(8,128)}, u32[]{:S(2)}) copy-start(f32[1024,1024]{1,0:T(8,128)} %get-tuple-element.61) | copy-start | bytes 12582916 | tf_op jit(solution)/shard_map/while
  107.8 3.6 %copy-start.1 = (f32[1,1024]{1,0:T(1,128)S(1)}, f32[1,1024]{1,0:T(1,128)}, u32[]{:S(2)}) copy-start(f32[1,1024]{1,0:T(1,128)} %get-tuple-element.63) | copy-start | bytes 12292 | tf_op jit(solution)/shard_map/while
  189.9 5.9 %copy-start = (f32[1024,1024]{1,0:T(8,128)S(1)}, f32[1024,1024]{1,0:T(8,128)}, u32[]{:S(2)}) copy-start(f32[1024,1024]{1,0:T(8,128)} %get-tuple-element.61) | copy-start | bytes 12582916 | tf_op jit(solution)/shard_map/while
  199.3 3.6 %copy-start.1 = (f32[1,1024]{1,0:T(1,128)S(1)}, f32[1,1024]{1,0:T(1,128)}, u32[]{:S(2)}) copy-start(f32[1,1024]{1,0:T(1,128)} %get-tuple-element.63) | copy-start | bytes 12292 | tf_op jit(solution)/shard_map/while

commit v11 on v10

--- a/solution.py
+++ b/solution.py
@@ -100,13 +100,13 @@
     pl.semaphore_signal(barrier, inc=1, device_id=y_peer, device_id_type=MESH)
     pl.semaphore_wait(barrier, inner)
 
+    rows_k = pl.ds(pl.multiple_of(partner * b_half, 8), b_half)
+    b_copies = [remote(payload.at[rows_k, cols_b], b_in, sends, recvs, 8, y_peer)]
     a_copies = []
     for by in range(1, inner):
         target = (me_x + by) % inner
         rows_k = pl.ds(pl.multiple_of(target * a_chunk, 8), a_chunk)
         a_copies.append(remote(payload.at[rows_k, cols_a], a_in.at[by - 1], sends, recvs, by - 1, x_peer(by)))
-    rows_k = pl.ds(pl.multiple_of(partner * b_half, 8), b_half)
-    b_copies = [remote(payload.at[rows_k, cols_b], b_in, sends, recvs, 8, y_peer)]
 
     for copy in a_copies:
         copy.wait()
@@ -152,10 +152,12 @@
     b_all[me_y] = b_row[...]
     b_copies = [remote(b_row, b_all.at[me_y], sends, recvs, 15, y_peer)]
 
-    for copy in a_copies + b_copies:
+    for copy in a_copies:
         copy.wait()
     for k in range(inner):
         out[pl.ds(k * a_chunk, a_chunk), cols_a] = a_all[k]
+    for copy in b_copies:
+        copy.wait()
     for j in range(outer):
         for k in range(inner):
             out[pl.ds(j * b_half + k * b_chunk, b_chunk), cols_b] = b_all[j, k]

time: 231 us -> 231 us (level)
  no operation moved by 1% of the time
where the time goes in v11:
time: 231 us; the launch traced here: 229 us
  Pallas kernels  140 us (61%)
  matrix products  41.9 us (18%)
  waiting for transfers between devices  29.5 us (13%)
  starting transfers between devices  7.47 us (3%)
  local copies, waits for them, and re-layouts  5.33 us (2%)
  other arithmetic  3.91 us (2%)
    pallas_call x2, Pallas kernels, rows_sum(): pl.pallas_call(functools.partial(rows_sum_kernel, outer, inner), out_shap...  101 us
    pallas_call x2, Pallas kernels, rotate(): pl.pallas_call(functools.partial(rotate_kernel, count), out_shape=jax.Sha...  39.2 us
    all_to_all x1, waiting for transfers between devices, per_device(): lax.all_to_all(slots, 'pair', split_axis=0, concat_axis=0, tiled=True)  29.5 us
    dot_general x4, matrix products, turn(): jnp.dot(chain, first_iter, precision=fast, preferred_element_type=jnp.flo...  16.9 us
    dot_general x2, matrix products, turn(): jnp.dot(weighted, first_iter, precision=fast, preferred_element_type=jnp....  11.7 us
    all_to_all x1, starting transfers between devices, per_device(): lax.all_to_all(slots, 'pair', split_axis=0, concat_axis=0, tiled=True)  7.47 us
    dot_general x2, matrix products, turn(): jnp.dot(applied, first_iter, precision=fast, preferred_element_type=jnp.f...  7.11 us
    dot_general x6, matrix products, inner_gram(): lax.dot_general(left, right, (((0,), (0,)), ((), ())), precision=fast, pr...  6.18 us
  transfers between devices with their start and end apart: 1, of which 1 were waited for; matrix products, arithmetic and copies ran while one was open for 0% of the time, Pallas kernels for 0%

profile of v11, /device:TPU:97, one launch (start us, length us, event | category | flops | bytes accessed | tf_op | source)
XLA Modules:
  0.0 228.6 jit_solution(15941395867357337954)
XLA Ops:
  0.0 0.7 pad_clamp_fusion
  0.7 1.8 copy.6
  2.5 2.0 gather_fusion
  4.5 7.5 %all-to-all-start = ((f32[16,2,32,512]{3,2,1,0:T(8,128)}), f32[16,2,32,512]{3,2,1,0:T(8,128)S(1)}, u32[]{:S(2)}, u32[]{:S(2)}) async-start(f32[16,2,32,512]{3,2,1,0:T(8,128)} %bitcast.37), calls=%async_computation | async-start | bytes 4194304 | tf_op jit(solution)/shard_map/all_to_all | solution.py:381
  12.0 29.5 %all-to-all-done = f32[16,2,32,512]{3,2,1,0:T(8,128)S(1)} async-done(((f32[16,2,32,512]{3,2,1,0:T(8,128)}), f32[16,2,32,512]{3,2,1,0:T(8,128)S(1)}, u32[]{:S(2)}, u32[]{:S(2)}) %all-to-all-start) | async-done | bytes 2097184 | tf_op jit(solution)/shard_map/all_to_all | solution.py:381
  41.5 0.2 fusion.17
  41.6 0.1 pad_maximum_fusion
  41.8 185.5 %while.11 = (s32[]{:T(128)}, f32[512,1024]{1,0:T(8,128)S(1)}, s32[]{:T(128)}) while((s32[]{:T(128)}, f32[512,1024]{1,0:T(8,128)S(1)}, s32[]{:T(128)}) %tuple.26), condition=%wide.region_2.3_spmd, body=%wide.region_0.2_spmd.sunk | while | flops 15308029952 | bytes 67268704 | solution.py:401
  41.8 1.0 fusion.51
  42.8 1.0 select_reduce_fusion.2
  43.9 1.0 convolution_select_fusion.2
  44.9 1.6 select_maximum_fusion.2.payload
  46.5 52.0 %eval_jaxpr.2 = (f32[1024,1024]{1,0:T(8,128)}, f32[1,1024]{1,0:T(1,128)}, f32[1,1024]{1,0:T(1,128)}) custom-call(f32[1088,512]{1,0:T(8,128)} %select_maximum_fusion.2.payload), custom_call_target="tpu_custom_call" | custom-call | tf_op jit(solution)/shard_map/while/body/eval_jaxpr/pallas_call | solution.py:216
  98.4 0.0 copy-start
  98.5 5.9 %fusion.52 = f32[512,1024]{1,0:T(8,128)S(1)} fusion(f32[1024,1024]{1,0:T(8,128)} %get-tuple-element.61, f32[512,1024]{1,0:T(8,128)S(1)} %get-tuple-element.68, f32[1024]{0:T(1024)} %bitcast.44), kind=kOutput, calls=%fused_computation.7.clone.1 | convolution fusion | flops 3221749760 | bytes 8392704 | tf_op jit(solution)/shard_map/while/body/eval_jaxpr/dot_general | solution.py:392
  104.3 0.0 copy-done
  104.3 3.6 %fusion.53 = f32[512,1024]{1,0:T(8,128)S(1)} fusion(f32[512,1024]{1,0:T(8,128)S(1)} %fusion.52, f32[1024,1024]{1,0:T(8,128)S(1)} %copy-done), kind=kOutput, calls=%fused_computation.29.clone.1 | convolution fusion | flops 3221225472 | bytes 8388608 | tf_op jit(solution)/shard_map/while/body/eval_jaxpr/dot_general | solution.py:393
  107.9 0.0 copy-start.1
  107.9 3.5 %fusion.54 = f32[512,1024]{1,0:T(8,128)S(1)} fusion(f32[1024,1024]{1,0:T(8,128)S(1)} %copy-done, f32[512,1024]{1,0:T(8,128)S(1)} %fusion.53, f32[512,1024]{1,0:T(8,128)S(1)} %fusion.52), kind=kOutput, calls=%fused_computation.4.clone.1 | convolution fusion | flops 3222798336 | bytes 10485760 | tf_op jit(solution)/shard_map/while/body/eval_jaxpr/dot_general | solution.py:396
  111.5 0.0 copy-done.1
  111.5 4.9 %subtract_multiply_fusion.2.current = f32[512,1024]{1,0:T(8,128)} fusion(f32[512,1024]{1,0:T(8,128)S(1)} %fusion.52, f32[512,1024]{1,0:T(8,128)S(1)} %fusion.54, f32[1024,1024]{1,0:T(8,128)S(1)} %copy-done, f32[1024]{0:T(1024)S(1)} %bitcast.43), kind=kOutput, calls=%fused_computation.3.clone.1 | convolution fusion | flops 3222798336 | bytes 10489856 | tf_op jit(solution)/shard_map/while/body/eval_jaxpr/dot_general | solution.py:397
  116.4 19.6 %eval_jaxpr.3 = f32[512,1024]{1,0:T(8,128)S(1)} custom-call(f32[512,1024]{1,0:T(8,128)} %subtract_multiply_fusion.2.current), custom_call_target="tpu_custom_call" | custom-call | tf_op jit(solution)/shard_map/while/body/eval_jaxpr/pallas_call | solution.py:319
  136.0 1.0 fusion.51
  137.0 1.0 select_reduce_fusion.2
  138.1 1.0 convolution_select_fusion.2
  139.1 1.6 select_maximum_fusion.2.payload
  140.7 49.1 %eval_jaxpr.2 = (f32[1024,1024]{1,0:T(8,128)}, f32[1,1024]{1,0:T(1,128)}, f32[1,1024]{1,0:T(1,128)}) custom-call(f32[1088,512]{1,0:T(8,128)} %select_maximum_fusion.2.payload), custom_call_target="tpu_custom_call" | custom-call | tf_op jit(solution)/shard_map/while/body/eval_jaxpr/pallas_call | solution.py:216
  189.8 0.0 copy-start
  189.8 5.9 %fusion.52 = f32[512,1024]{1,0:T(8,128)S(1)} fusion(f32[1024,1024]{1,0:T(8,128)} %get-tuple-element.61, f32[512,1024]{1,0:T(8,128)S(1)} %get-tuple-element.68, f32[1024]{0:T(1024)} %bitcast.44), kind=kOutput, calls=%fused_computation.7.clone.1 | convolution fusion | flops 3221749760 | bytes 8392704 | tf_op jit(solution)/shard_map/while/body/eval_jaxpr/dot_general | solution.py:392
  195.6 0.0 copy-done
  195.7 3.6 %fusion.53 = f32[512,1024]{1,0:T(8,128)S(1)} fusion(f32[512,1024]{1,0:T(8,128)S(1)} %fusion.52, f32[1024,1024]{1,0:T(8,128)S(1)} %copy-done), kind=kOutput, calls=%fused_computation.29.clone.1 | convolution fusion | flops 3221225472 | bytes 8388608 | tf_op jit(solution)/shard_map/while/body/eval_jaxpr/dot_general | solution.py:393
  199.2 0.0 copy-start.1
  199.2 3.5 %fusion.54 = f32[512,1024]{1,0:T(8,128)S(1)} fusion(f32[1024,1024]{1,0:T(8,128)S(1)} %copy-done, f32[512,1024]{1,0:T(8,128)S(1)} %fusion.53, f32[512,1024]{1,0:T(8,128)S(1)} %fusion.52), kind=kOutput, calls=%fused_computation.4.clone.1 | convolution fusion | flops 3222798336 | bytes 10485760 | tf_op jit(solution)/shard_map/while/body/eval_jaxpr/dot_general | solution.py:396
  202.8 0.0 copy-done.1
  202.8 4.9 %subtract_multiply_fusion.2.current = f32[512,1024]{1,0:T(8,128)} fusion(f32[512,1024]{1,0:T(8,128)S(1)} %fusion.52, f32[512,1024]{1,0:T(8,128)S(1)} %fusion.54, f32[1024,1024]{1,0:T(8,128)S(1)} %copy-done, f32[1024]{0:T(1024)S(1)} %bitcast.43), kind=kOutput, calls=%fused_computation.3.clone.1 | convolution fusion | flops 3222798336 | bytes 10489856 | tf_op jit(solution)/shard_map/while/body/eval_jaxpr/dot_general | solution.py:397
  207.7 19.6 %eval_jaxpr.3 = f32[512,1024]{1,0:T(8,128)S(1)} custom-call(f32[512,1024]{1,0:T(8,128)} %subtract_multiply_fusion.2.current), custom_call_target="tpu_custom_call" | custom-call | tf_op jit(solution)/shard_map/while/body/eval_jaxpr/pallas_call | solution.py:319
  227.3 1.3 copy.16
Async XLA Ops:
  4.5 37.0 %all-to-all-start = ((f32[16,2,32,512]{3,2,1,0:T(8,128)}), f32[16,2,32,512]{3,2,1,0:T(8,128)S(1)}, u32[]{:S(2)}, u32[]{:S(2)}) async-start(f32[16,2,32,512]{3,2,1,0:T(8,128)} %bitcast.37), calls=%async_computation | async-start | bytes 4194304 | tf_op jit(solution)/shard_map/all_to_all | solution.py:381
  98.4 5.9 %copy-start = (f32[1024,1024]{1,0:T(8,128)S(1)}, f32[1024,1024]{1,0:T(8,128)}, u32[]{:S(2)}) copy-start(f32[1024,1024]{1,0:T(8,128)} %get-tuple-element.61) | copy-start | bytes 12582916 | tf_op jit(solution)/shard_map/while
  107.9 3.6 %copy-start.1 = (f32[1,1024]{1,0:T(1,128)S(1)}, f32[1,1024]{1,0:T(1,128)}, u32[]{:S(2)}) copy-start(f32[1,1024]{1,0:T(1,128)} %get-tuple-element.63) | copy-start | bytes 12292 | tf_op jit(solution)/shard_map/while
  189.8 5.9 %copy-start = (f32[1024,1024]{1,0:T(8,128)S(1)}, f32[1024,1024]{1,0:T(8,128)}, u32[]{:S(2)}) copy-start(f32[1024,1024]{1,0:T(8,128)} %get-tuple-element.61) | copy-start | bytes 12582916 | tf_op jit(solution)/shard_map/while
  199.2 3.6 %copy-start.1 = (f32[1,1024]{1,0:T(1,128)S(1)}, f32[1,1024]{1,0:T(1,128)}, u32[]{:S(2)}) copy-start(f32[1,1024]{1,0:T(1,128)} %get-tuple-element.63) | copy-start | bytes 12292 | tf_op jit(solution)/shard_map/while

commit v12 on v10

--- a/solution.py
+++ b/solution.py
@@ -332,9 +332,9 @@
     width = upper.shape[1]
     row = lax.broadcasted_iota(jnp.int32, (width, width), 0)
     col = lax.broadcasted_iota(jnp.int32, (width, width), 1)
-    upper_gram = inner_gram(upper, upper)
+    top = inner_gram(upper, jnp.concatenate([upper, lower], axis=1))
+    upper_gram, cross_gram = top[:, :width], top[:, width:]
     lower_gram = inner_gram(lower, lower)
-    cross_gram = inner_gram(upper, lower)
     packed = jnp.where(col >= row, upper_gram, lower_gram)
     tail = jnp.zeros((64, width), jnp.float32).at[0].set(masked_diagonal(lower_gram))
     return rows_sum(jnp.concatenate([packed, cross_gram, tail]), outer, inner)

time: 231 us -> 230 us (level)
    dot_general x6 -> x4, matrix products: 6.18 us -> 5.89 us  [inner_gram(): lax.dot_general(left, right, (((0,), (0,)), ((), ())), precision=fast, pr...]
where the time goes in v12:
time: 230 us; the launch traced here: 228 us
  Pallas kernels  140 us (61%)
  matrix products  41.6 us (18%)
  waiting for transfers between devices  29.5 us (13%)
  starting transfers between devices  7.47 us (3%)
  local copies, waits for them, and re-layouts  5.33 us (2%)
  other arithmetic  3.92 us (2%)
    pallas_call x2, Pallas kernels, rows_sum(): pl.pallas_call(functools.partial(rows_sum_kernel, outer, inner), out_shap...  101 us
    pallas_call x2, Pallas kernels, rotate(): pl.pallas_call(functools.partial(rotate_kernel, count), out_shape=jax.Sha...  39.2 us
    all_to_all x1, waiting for transfers between devices, per_device(): lax.all_to_all(slots, 'pair', split_axis=0, concat_axis=0, tiled=True)  29.5 us
    dot_general x4, matrix products, turn(): jnp.dot(chain, first_iter, precision=fast, preferred_element_type=jnp.flo...  16.9 us
    dot_general x2, matrix products, turn(): jnp.dot(weighted, first_iter, precision=fast, preferred_element_type=jnp....  11.7 us
    all_to_all x1, starting transfers between devices, per_device(): lax.all_to_all(slots, 'pair', split_axis=0, concat_axis=0, tiled=True)  7.47 us
    dot_general x2, matrix products, turn(): jnp.dot(applied, first_iter, precision=fast, preferred_element_type=jnp.f...  7.1 us
    dot_general x4, matrix products, inner_gram(): lax.dot_general(left, right, (((0,), (0,)), ((), ())), precision=fast, pr...  5.89 us
  transfers between devices with their start and end apart: 1, of which 1 were waited for; matrix products, arithmetic and copies ran while one was open for 0% of the time, Pallas kernels for 0%

profile of v12, /device:TPU:97, one launch (start us, length us, event | category | flops | bytes accessed | tf_op | source)
XLA Modules:
  0.0 228.5 jit_solution(12527804190355989027)
XLA Ops:
  0.0 0.7 pad_clamp_fusion
  0.7 1.8 copy.6
  2.5 2.0 gather_fusion
  4.5 7.5 %all-to-all-start = ((f32[16,2,32,512]{3,2,1,0:T(8,128)}), f32[16,2,32,512]{3,2,1,0:T(8,128)S(1)}, u32[]{:S(2)}, u32[]{:S(2)}) async-start(f32[16,2,32,512]{3,2,1,0:T(8,128)} %bitcast.40), calls=%async_computation | async-start | bytes 4194304 | tf_op jit(solution)/shard_map/all_to_all | solution.py:379
  12.0 29.5 %all-to-all-done = f32[16,2,32,512]{3,2,1,0:T(8,128)S(1)} async-done(((f32[16,2,32,512]{3,2,1,0:T(8,128)}), f32[16,2,32,512]{3,2,1,0:T(8,128)S(1)}, u32[]{:S(2)}, u32[]{:S(2)}) %all-to-all-start) | async-done | bytes 2097184 | tf_op jit(solution)/shard_map/all_to_all | solution.py:379
  41.5 0.2 fusion.15
  41.6 0.1 pad_maximum_fusion
  41.8 185.3 %while.11 = (s32[]{:T(128)}, f32[512,1024]{1,0:T(8,128)S(1)}, s32[]{:T(128)}) while((s32[]{:T(128)}, f32[512,1024]{1,0:T(8,128)S(1)}, s32[]{:T(128)}) %tuple.27), condition=%wide.region_2.3_spmd, body=%wide.region_0.2_spmd.sunk | while | flops 15308029952 | bytes 69365856 | solution.py:399
  41.8 1.9 fusion.52
  43.7 1.1 slice_select_fusion.2
  44.8 1.6 select_maximum_fusion.2.payload
  46.3 51.9 %eval_jaxpr.2 = (f32[1024,1024]{1,0:T(8,128)}, f32[1,1024]{1,0:T(1,128)}, f32[1,1024]{1,0:T(1,128)}) custom-call(f32[1088,512]{1,0:T(8,128)} %select_maximum_fusion.2.payload), custom_call_target="tpu_custom_call" | custom-call | tf_op jit(solution)/shard_map/while/body/eval_jaxpr/pallas_call | solution.py:214
  98.3 0.0 copy-start
  98.3 5.9 %fusion.53 = f32[512,1024]{1,0:T(8,128)S(1)} fusion(f32[1024,1024]{1,0:T(8,128)} %get-tuple-element.64, f32[512,1024]{1,0:T(8,128)S(1)} %get-tuple-element.71, f32[1024]{0:T(1024)} %bitcast.47), kind=kOutput, calls=%fused_computation.7.clone.1 | convolution fusion | flops 3221749760 | bytes 8392704 | tf_op jit(solution)/shard_map/while/body/eval_jaxpr/dot_general | solution.py:390
  104.1 0.0 copy-done
  104.1 3.6 %fusion.54 = f32[512,1024]{1,0:T(8,128)S(1)} fusion(f32[512,1024]{1,0:T(8,128)S(1)} %fusion.53, f32[1024,1024]{1,0:T(8,128)S(1)} %copy-done), kind=kOutput, calls=%fused_computation.27.clone.1 | convolution fusion | flops 3221225472 | bytes 8388608 | tf_op jit(solution)/shard_map/while/body/eval_jaxpr/dot_general | solution.py:391
  107.7 0.0 copy-start.1
  107.7 3.5 %fusion.55 = f32[512,1024]{1,0:T(8,128)S(1)} fusion(f32[1024,1024]{1,0:T(8,128)S(1)} %copy-done, f32[512,1024]{1,0:T(8,128)S(1)} %fusion.54, f32[512,1024]{1,0:T(8,128)S(1)} %fusion.53), kind=kOutput, calls=%fused_computation.4.clone.1 | convolution fusion | flops 3222798336 | bytes 10485760 | tf_op jit(solution)/shard_map/while/body/eval_jaxpr/dot_general | solution.py:394
  111.3 0.0 copy-done.1
  111.3 4.9 %subtract_multiply_fusion.2.current = f32[512,1024]{1,0:T(8,128)} fusion(f32[512,1024]{1,0:T(8,128)S(1)} %fusion.53, f32[512,1024]{1,0:T(8,128)S(1)} %fusion.55, f32[1024,1024]{1,0:T(8,128)S(1)} %copy-done, f32[1024]{0:T(1024)S(1)} %bitcast.46), kind=kOutput, calls=%fused_computation.3.clone.1 | convolution fusion | flops 3222798336 | bytes 10489856 | tf_op jit(solution)/shard_map/while/body/eval_jaxpr/dot_general | solution.py:395
  116.2 19.6 %eval_jaxpr.3 = f32[512,1024]{1,0:T(8,128)S(1)} custom-call(f32[512,1024]{1,0:T(8,128)} %subtract_multiply_fusion.2.current), custom_call_target="tpu_custom_call" | custom-call | tf_op jit(solution)/shard_map/while/body/eval_jaxpr/pallas_call | solution.py:317
  135.8 1.9 fusion.52
  137.7 1.1 slice_select_fusion.2
  138.7 1.6 select_maximum_fusion.2.payload
  140.3 49.3 %eval_jaxpr.2 = (f32[1024,1024]{1,0:T(8,128)}, f32[1,1024]{1,0:T(1,128)}, f32[1,1024]{1,0:T(1,128)}) custom-call(f32[1088,512]{1,0:T(8,128)} %select_maximum_fusion.2.payload), custom_call_target="tpu_custom_call" | custom-call | tf_op jit(solution)/shard_map/while/body/eval_jaxpr/pallas_call | solution.py:214
  189.6 0.0 copy-start
  189.6 5.9 %fusion.53 = f32[512,1024]{1,0:T(8,128)S(1)} fusion(f32[1024,1024]{1,0:T(8,128)} %get-tuple-element.64, f32[512,1024]{1,0:T(8,128)S(1)} %get-tuple-element.71, f32[1024]{0:T(1024)} %bitcast.47), kind=kOutput, calls=%fused_computation.7.clone.1 | convolution fusion | flops 3221749760 | bytes 8392704 | tf_op jit(solution)/shard_map/while/body/eval_jaxpr/dot_general | solution.py:390
  195.5 0.0 copy-done
  195.5 3.6 %fusion.54 = f32[512,1024]{1,0:T(8,128)S(1)} fusion(f32[512,1024]{1,0:T(8,128)S(1)} %fusion.53, f32[1024,1024]{1,0:T(8,128)S(1)} %copy-done), kind=kOutput, calls=%fused_computation.27.clone.1 | convolution fusion | flops 3221225472 | bytes 8388608 | tf_op jit(solution)/shard_map/while/body/eval_jaxpr/dot_general | solution.py:391
  199.1 0.0 copy-start.1
  199.1 3.5 %fusion.55 = f32[512,1024]{1,0:T(8,128)S(1)} fusion(f32[1024,1024]{1,0:T(8,128)S(1)} %copy-done, f32[512,1024]{1,0:T(8,128)S(1)} %fusion.54, f32[512,1024]{1,0:T(8,128)S(1)} %fusion.53), kind=kOutput, calls=%fused_computation.4.clone.1 | convolution fusion | flops 3222798336 | bytes 10485760 | tf_op jit(solution)/shard_map/while/body/eval_jaxpr/dot_general | solution.py:394
  202.6 0.0 copy-done.1
  202.6 4.9 %subtract_multiply_fusion.2.current = f32[512,1024]{1,0:T(8,128)} fusion(f32[512,1024]{1,0:T(8,128)S(1)} %fusion.53, f32[512,1024]{1,0:T(8,128)S(1)} %fusion.55, f32[1024,1024]{1,0:T(8,128)S(1)} %copy-done, f32[1024]{0:T(1024)S(1)} %bitcast.46), kind=kOutput, calls=%fused_computation.3.clone.1 | convolution fusion | flops 3222798336 | bytes 10489856 | tf_op jit(solution)/shard_map/while/body/eval_jaxpr/dot_general | solution.py:395
  207.5 19.6 %eval_jaxpr.3 = f32[512,1024]{1,0:T(8,128)S(1)} custom-call(f32[512,1024]{1,0:T(8,128)} %subtract_multiply_fusion.2.current), custom_call_target="tpu_custom_call" | custom-call | tf_op jit(solution)/shard_map/while/body/eval_jaxpr/pallas_call | solution.py:317
  227.1 1.3 copy.16
Async XLA Ops:
  4.5 37.0 %all-to-all-start = ((f32[16,2,32,512]{3,2,1,0:T(8,128)}), f32[16,2,32,512]{3,2,1,0:T(8,128)S(1)}, u32[]{:S(2)}, u32[]{:S(2)}) async-start(f32[16,2,32,512]{3,2,1,0:T(8,128)} %bitcast.40), calls=%async_computation | async-start | bytes 4194304 | tf_op jit(solution)/shard_map/all_to_all | solution.py:379
  98.3 5.9 %copy-start = (f32[1024,1024]{1,0:T(8,128)S(1)}, f32[1024,1024]{1,0:T(8,128)}, u32[]{:S(2)}) copy-start(f32[1024,1024]{1,0:T(8,128)} %get-tuple-element.64) | copy-start | bytes 12582916 | tf_op jit(solution)/shard_map/while
  107.7 3.6 %copy-start.1 = (f32[1,1024]{1,0:T(1,128)S(1)}, f32[1,1024]{1,0:T(1,128)}, u32[]{:S(2)}) copy-start(f32[1,1024]{1,0:T(1,128)} %get-tuple-element.66) | copy-start | bytes 12292 | tf_op jit(solution)/shard_map/while
  189.6 5.9 %copy-start = (f32[1024,1024]{1,0:T(8,128)S(1)}, f32[1024,1024]{1,0:T(8,128)}, u32[]{:S(2)}) copy-start(f32[1024,1024]{1,0:T(8,128)} %get-tuple-element.64) | copy-start | bytes 12582916 | tf_op jit(solution)/shard_map/while
  199.1 3.6 %copy-start.1 = (f32[1,1024]{1,0:T(1,128)S(1)}, f32[1,1024]{1,0:T(1,128)}, u32[]{:S(2)}) copy-start(f32[1,1024]{1,0:T(1,128)} %get-tuple-element.66) | copy-start | bytes 12292 | tf_op jit(solution)/shard_map/while

commit v13 on v12

--- a/solution.py
+++ b/solution.py
@@ -240,7 +240,7 @@
     )(v)
 
 
-def rotate_kernel(count, current, out, landed, sends, recvs):
+def rotate_kernel(count, current, landed, sends, recvs):
     me = lax.axis_index("pair")
     me_y = lax.axis_index("ylo")
     me_x = lax.axis_index("x")
@@ -310,8 +310,6 @@
         downward.wait_send()
         upward.wait_recv()
 
-    out[...] = landed[...]
-
 
 def rotate(current, count):
     return pl.pallas_call(
@@ -320,7 +318,6 @@
         in_specs=[pl.BlockSpec(memory_space=pltpu.VMEM)],
         out_specs=pl.BlockSpec(memory_space=pltpu.VMEM),
         scratch_shapes=[
-            pltpu.VMEM(current.shape, jnp.float32),
             pltpu.SemaphoreType.DMA((2,)),
             pltpu.SemaphoreType.DMA((2,)),
         ],

time: 230 us -> 230 us (level)
  no operation moved by 1% of the time
where the time goes in v13:
time: 230 us; the launch traced here: 228 us
  Pallas kernels  140 us (61%)
  matrix products  41.6 us (18%)
  waiting for transfers between devices  29.5 us (13%)
  starting transfers between devices  7.47 us (3%)
  local copies, waits for them, and re-layouts  5.33 us (2%)
  other arithmetic  3.92 us (2%)
    pallas_call x2, Pallas kernels, rows_sum(): pl.pallas_call(functools.partial(rows_sum_kernel, outer, inner), out_shap...  101 us
    pallas_call x2, Pallas kernels, rotate(): pl.pallas_call(functools.partial(rotate_kernel, count), out_shape=jax.Sha...  38.9 us
    all_to_all x1, waiting for transfers between devices, per_device(): lax.all_to_all(slots, 'pair', split_axis=0, concat_axis=0, tiled=True)  29.5 us
    dot_general x4, matrix products, turn(): jnp.dot(chain, first_iter, precision=fast, preferred_element_type=jnp.flo...  16.9 us
    dot_general x2, matrix products, turn(): jnp.dot(weighted, first_iter, precision=fast, preferred_element_type=jnp....  11.7 us
    all_to_all x1, starting transfers between devices, per_device(): lax.all_to_all(slots, 'pair', split_axis=0, concat_axis=0, tiled=True)  7.47 us
    dot_general x2, matrix products, turn(): jnp.dot(applied, first_iter, precision=fast, preferred_element_type=jnp.f...  7.1 us
    dot_general x4, matrix products, inner_gram(): lax.dot_general(left, right, (((0,), (0,)), ((), ())), precision=fast, pr...  5.89 us
  transfers between devices with their start and end apart: 1, of which 1 were waited for; matrix products, arithmetic and copies ran while one was open for 0% of the time, Pallas kernels for 0%

profile of v13, /device:TPU:97, one launch (start us, length us, event | category | flops | bytes accessed | tf_op | source)
XLA Modules:
  0.0 228.2 jit_solution(12113981818084570211)
XLA Ops:
  0.0 0.7 pad_clamp_fusion
  0.7 1.8 copy.6
  2.5 2.0 gather_fusion
  4.5 7.5 %all-to-all-start = ((f32[16,2,32,512]{3,2,1,0:T(8,128)}), f32[16,2,32,512]{3,2,1,0:T(8,128)S(1)}, u32[]{:S(2)}, u32[]{:S(2)}) async-start(f32[16,2,32,512]{3,2,1,0:T(8,128)} %bitcast.40), calls=%async_computation | async-start | bytes 4194304 | tf_op jit(solution)/shard_map/all_to_all | solution.py:376
  12.0 29.5 %all-to-all-done = f32[16,2,32,512]{3,2,1,0:T(8,128)S(1)} async-done(((f32[16,2,32,512]{3,2,1,0:T(8,128)}), f32[16,2,32,512]{3,2,1,0:T(8,128)S(1)}, u32[]{:S(2)}, u32[]{:S(2)}) %all-to-all-start) | async-done | bytes 2097184 | tf_op jit(solution)/shard_map/all_to_all | solution.py:376
  41.5 0.2 fusion.15
  41.6 0.1 pad_maximum_fusion
  41.8 185.1 %while.11 = (s32[]{:T(128)}, f32[512,1024]{1,0:T(8,128)S(1)}, s32[]{:T(128)}) while((s32[]{:T(128)}, f32[512,1024]{1,0:T(8,128)S(1)}, s32[]{:T(128)}) %tuple.27), condition=%wide.region_2.3_spmd, body=%wide.region_0.2_spmd.sunk | while | flops 15308029952 | bytes 69365856 | solution.py:396
  41.8 1.9 fusion.52
  43.7 1.1 slice_select_fusion.2
  44.8 1.6 select_maximum_fusion.2.payload
  46.3 51.9 %eval_jaxpr.2 = (f32[1024,1024]{1,0:T(8,128)}, f32[1,1024]{1,0:T(1,128)}, f32[1,1024]{1,0:T(1,128)}) custom-call(f32[1088,512]{1,0:T(8,128)} %select_maximum_fusion.2.payload), custom_call_target="tpu_custom_call" | custom-call | tf_op jit(solution)/shard_map/while/body/eval_jaxpr/pallas_call | solution.py:214
  98.3 0.0 copy-start
  98.3 5.9 %fusion.53 = f32[512,1024]{1,0:T(8,128)S(1)} fusion(f32[1024,1024]{1,0:T(8,128)} %get-tuple-element.64, f32[512,1024]{1,0:T(8,128)S(1)} %get-tuple-element.71, f32[1024]{0:T(1024)} %bitcast.47), kind=kOutput, calls=%fused_computation.7.clone.1 | convolution fusion | flops 3221749760 | bytes 8392704 | tf_op jit(solution)/shard_map/while/body/eval_jaxpr/dot_general | solution.py:387
  104.1 0.0 copy-done
  104.1 3.6 %fusion.54 = f32[512,1024]{1,0:T(8,128)S(1)} fusion(f32[512,1024]{1,0:T(8,128)S(1)} %fusion.53, f32[1024,1024]{1,0:T(8,128)S(1)} %copy-done), kind=kOutput, calls=%fused_computation.27.clone.1 | convolution fusion | flops 3221225472 | bytes 8388608 | tf_op jit(solution)/shard_map/while/body/eval_jaxpr/dot_general | solution.py:388
  107.7 0.0 copy-start.1
  107.7 3.5 %fusion.55 = f32[512,1024]{1,0:T(8,128)S(1)} fusion(f32[1024,1024]{1,0:T(8,128)S(1)} %copy-done, f32[512,1024]{1,0:T(8,128)S(1)} %fusion.54, f32[512,1024]{1,0:T(8,128)S(1)} %fusion.53), kind=kOutput, calls=%fused_computation.4.clone.1 | convolution fusion | flops 3222798336 | bytes 10485760 | tf_op jit(solution)/shard_map/while/body/eval_jaxpr/dot_general | solution.py:391
  111.3 0.0 copy-done.1
  111.3 4.9 %subtract_multiply_fusion.2.current = f32[512,1024]{1,0:T(8,128)} fusion(f32[512,1024]{1,0:T(8,128)S(1)} %fusion.53, f32[512,1024]{1,0:T(8,128)S(1)} %fusion.55, f32[1024,1024]{1,0:T(8,128)S(1)} %copy-done, f32[1024]{0:T(1024)S(1)} %bitcast.46), kind=kOutput, calls=%fused_computation.3.clone.1 | convolution fusion | flops 3222798336 | bytes 10489856 | tf_op jit(solution)/shard_map/while/body/eval_jaxpr/dot_general | solution.py:392
  116.2 19.5 %eval_jaxpr.3 = f32[512,1024]{1,0:T(8,128)S(1)} custom-call(f32[512,1024]{1,0:T(8,128)} %subtract_multiply_fusion.2.current), custom_call_target="tpu_custom_call" | custom-call | tf_op jit(solution)/shard_map/while/body/eval_jaxpr/pallas_call | solution.py:315
  135.7 1.9 fusion.52
  137.6 1.1 slice_select_fusion.2
  138.6 1.6 select_maximum_fusion.2.payload
  140.2 49.3 %eval_jaxpr.2 = (f32[1024,1024]{1,0:T(8,128)}, f32[1,1024]{1,0:T(1,128)}, f32[1,1024]{1,0:T(1,128)}) custom-call(f32[1088,512]{1,0:T(8,128)} %select_maximum_fusion.2.payload), custom_call_target="tpu_custom_call" | custom-call | tf_op jit(solution)/shard_map/while/body/eval_jaxpr/pallas_call | solution.py:214
  189.5 0.0 copy-start
  189.5 5.9 %fusion.53 = f32[512,1024]{1,0:T(8,128)S(1)} fusion(f32[1024,1024]{1,0:T(8,128)} %get-tuple-element.64, f32[512,1024]{1,0:T(8,128)S(1)} %get-tuple-element.71, f32[1024]{0:T(1024)} %bitcast.47), kind=kOutput, calls=%fused_computation.7.clone.1 | convolution fusion | flops 3221749760 | bytes 8392704 | tf_op jit(solution)/shard_map/while/body/eval_jaxpr/dot_general | solution.py:387
  195.4 0.0 copy-done
  195.4 3.6 %fusion.54 = f32[512,1024]{1,0:T(8,128)S(1)} fusion(f32[512,1024]{1,0:T(8,128)S(1)} %fusion.53, f32[1024,1024]{1,0:T(8,128)S(1)} %copy-done), kind=kOutput, calls=%fused_computation.27.clone.1 | convolution fusion | flops 3221225472 | bytes 8388608 | tf_op jit(solution)/shard_map/while/body/eval_jaxpr/dot_general | solution.py:388
  198.9 0.0 copy-start.1
  198.9 3.5 %fusion.55 = f32[512,1024]{1,0:T(8,128)S(1)} fusion(f32[1024,1024]{1,0:T(8,128)S(1)} %copy-done, f32[512,1024]{1,0:T(8,128)S(1)} %fusion.54, f32[512,1024]{1,0:T(8,128)S(1)} %fusion.53), kind=kOutput, calls=%fused_computation.4.clone.1 | convolution fusion | flops 3222798336 | bytes 10485760 | tf_op jit(solution)/shard_map/while/body/eval_jaxpr/dot_general | solution.py:391
  202.5 0.0 copy-done.1
  202.5 4.9 %subtract_multiply_fusion.2.current = f32[512,1024]{1,0:T(8,128)} fusion(f32[512,1024]{1,0:T(8,128)S(1)} %fusion.53, f32[512,1024]{1,0:T(8,128)S(1)} %fusion.55, f32[1024,1024]{1,0:T(8,128)S(1)} %copy-done, f32[1024]{0:T(1024)S(1)} %bitcast.46), kind=kOutput, calls=%fused_computation.3.clone.1 | convolution fusion | flops 3222798336 | bytes 10489856 | tf_op jit(solution)/shard_map/while/body/eval_jaxpr/dot_general | solution.py:392
  207.4 19.5 %eval_jaxpr.3 = f32[512,1024]{1,0:T(8,128)S(1)} custom-call(f32[512,1024]{1,0:T(8,128)} %subtract_multiply_fusion.2.current), custom_call_target="tpu_custom_call" | custom-call | tf_op jit(solution)/shard_map/while/body/eval_jaxpr/pallas_call | solution.py:315
  226.9 1.3 copy.16
Async XLA Ops:
  4.5 37.0 %all-to-all-start = ((f32[16,2,32,512]{3,2,1,0:T(8,128)}), f32[16,2,32,512]{3,2,1,0:T(8,128)S(1)}, u32[]{:S(2)}, u32[]{:S(2)}) async-start(f32[16,2,32,512]{3,2,1,0:T(8,128)} %bitcast.40), calls=%async_computation | async-start | bytes 4194304 | tf_op jit(solution)/shard_map/all_to_all | solution.py:376
  98.3 5.9 %copy-start = (f32[1024,1024]{1,0:T(8,128)S(1)}, f32[1024,1024]{1,0:T(8,128)}, u32[]{:S(2)}) copy-start(f32[1024,1024]{1,0:T(8,128)} %get-tuple-element.64) | copy-start | bytes 12582916 | tf_op jit(solution)/shard_map/while
  107.7 3.6 %copy-start.1 = (f32[1,1024]{1,0:T(1,128)S(1)}, f32[1,1024]{1,0:T(1,128)}, u32[]{:S(2)}) copy-start(f32[1,1024]{1,0:T(1,128)} %get-tuple-element.66) | copy-start | bytes 12292 | tf_op jit(solution)/shard_map/while
  189.5 5.9 %copy-start = (f32[1024,1024]{1,0:T(8,128)S(1)}, f32[1024,1024]{1,0:T(8,128)}, u32[]{:S(2)}) copy-start(f32[1024,1024]{1,0:T(8,128)} %get-tuple-element.64) | copy-start | bytes 12582916 | tf_op jit(solution)/shard_map/while
  198.9 3.6 %copy-start.1 = (f32[1,1024]{1,0:T(1,128)S(1)}, f32[1,1024]{1,0:T(1,128)}, u32[]{:S(2)}) copy-start(f32[1,1024]{1,0:T(1,128)} %get-tuple-element.66) | copy-start | bytes 12292 | tf_op jit(solution)/shard_map/while
